TPU v7x, 32 devices: a whole 2x2x4 slice. The times are simulated.
32 devices in a mesh: dp: 4 (over y, x), seq: 8 (over z, core).
Axes of the slice: x: 2, y: 2, z: 4, core: 2. Of those that a mesh axis runs over, the one named last changes fastest.
Arguments:
- tokens: bfloat16 [4, 1024, 2048], P('dp', 'seq'), may hold values from -6 to 6
- lengths: int32 [4], P('dp'), may hold values from 1024 to 1024, as said below
- w_qkv: bfloat16 [2048, 3072], P('seq', 'dp'), may hold values from -0.5 to 0.5
- w_out: bfloat16 [2048, 2048], P('seq', 'dp'), may hold values from -1 to 1
- w_gate_up: bfloat16 [2048, 16384], P('seq', 'dp'), may hold values from -0.125 to 0.125
- w_down: bfloat16 [8192, 2048], P('seq', 'dp'), may hold values from -0.5 to 0.5
- gains: bfloat16 [2048, 2], P('seq'), may hold values from 0.5 to 1.5
- cotangent: bfloat16 [4, 1024, 2048], P('dp', 'seq'), may hold values from -6 to 6
Outputs:
- output: bfloat16 [4, 1024, 2048], P('dp', 'seq')
- grad_tokens: float32 [4, 1024, 2048], P('dp', 'seq')
- grad_qkv: float32 [2048, 3072], P('seq', 'dp')
- grad_out: float32 [2048, 2048], P('seq', 'dp')
- grad_gate_up: float32 [2048, 16384], P('seq', 'dp')
- grad_down: float32 [8192, 2048], P('seq', 'dp')
- grad_gains: float32 [2048, 2], P('seq')
Inputs may be any that keep to these rules, and one draw needn't show every extreme that they name: `lengths`: some sequence uses all 1024 slots.
All inputs are finite; a program needn't handle non-finite values.
Results may differ from a plain program's by a relative error of at most 0.015.
The roundings to bfloat16 on the way count: a program that leaves them out, or rounds other values in their place, can miss the bound.
Values may be sent and summed in bfloat16 or wider, within the bound.
No kernel may reach another device: no remote copies, remote signals or barrier semaphores. Data moves between devices by JAX's collectives and lax.ppermute only.
A program may use at most 512 MiB of HBM per device.

v0:
```python
import jax
import jax.numpy as jnp
from jax import lax
from jax.sharding import PartitionSpec as P

HEADS = 32
KV_HEADS = 8
HEAD_DIM = 64
FF = 8192


EPSILON = 1e-05
RESIDUAL_SCALE = 0.22
SCORE_SCALE = 1.0 / 64.0
ROPE_THETA = 10000000.0


def rotary(positions):
    half_dim = HEAD_DIM // 2
    frequency = ROPE_THETA ** (-(jnp.arange(half_dim, dtype=jnp.float32) * 2.0) / HEAD_DIM)
    angles = positions.astype(jnp.float32)[:, None] * frequency[None, :]
    angles = jnp.concatenate([angles, angles], axis=1)
    return (jnp.cos(angles), jnp.sin(angles))


def rotate(values, cosine, sine_table, direction):
    half_dim = values.shape[-1] // 2
    turned = jnp.concatenate([-values[..., half_dim:], values[..., :half_dim]], axis=-1)
    return values * cosine[:, None, :] + turned * (direction * sine_table)[:, None, :]


def times_transposed(left, right):
    return lax.dot_general(
        left, right, (((1,), (1,)), ((), ())), preferred_element_type=jnp.float32
    )


def local(tokens, lengths, w_qkv, w_out, w_gate_up, w_down, gains, cotangent):
    tok_rows = tokens.shape[1]
    group_size = HEADS // KV_HEADS
    attn_width = HEADS * HEAD_DIM
    kv_width = KV_HEADS * HEAD_DIM
    seq_count = lax.axis_size("seq")
    slot_count = tok_rows * seq_count
    first_slot = lax.axis_index("seq") * tok_rows
    positions = first_slot + jnp.arange(tok_rows, dtype=jnp.int32)
    length = lengths[0]
    valid_rows = (positions < length).astype(jnp.float32)[:, None]
    key_positions = jnp.arange(slot_count, dtype=jnp.int32)
    allowed = (key_positions[None, :] <= positions[:, None]) & (key_positions[None, :] < length)
    cosine, sine_table = rotary(positions)
    columns = (
        lax.all_gather(w_qkv, "dp", axis=1, tiled=True),
        lax.all_gather(w_out, "dp", axis=1, tiled=True),
        lax.all_gather(w_gate_up, "dp", axis=1, tiled=True),
        lax.all_gather(w_down, "dp", axis=1, tiled=True),
    )
    full_qkv, full_out, full_gate_up, full_down, full_gains = (
        lax.all_gather(columns[0], "seq", axis=0, tiled=True),
        lax.all_gather(columns[1], "seq", axis=0, tiled=True),
        lax.all_gather(columns[2], "seq", axis=0, tiled=True),
        lax.all_gather(columns[3], "seq", axis=0, tiled=True),
        lax.all_gather(gains, "seq", axis=0, tiled=True),
    )
    token_vals = tokens[0].astype(jnp.float32)
    gain_first = full_gains[:, 0].astype(jnp.float32)
    gain_second = full_gains[:, 1].astype(jnp.float32)
    inv_first = lax.rsqrt(jnp.mean(token_vals * token_vals, axis=1, keepdims=True) + EPSILON)
    unit_first = token_vals * inv_first
    normed = (unit_first * gain_first).astype(jnp.bfloat16)
    qkv = jnp.dot(normed, full_qkv, preferred_element_type=jnp.float32)
    queries = rotate(
        qkv[:, :attn_width].reshape(tok_rows, HEADS, HEAD_DIM), cosine, sine_table, 1.0
    ).astype(jnp.bfloat16)
    key_vals = rotate(
        qkv[:, attn_width : attn_width + kv_width].reshape(tok_rows, KV_HEADS, HEAD_DIM),
        cosine,
        sine_table,
        1.0,
    ).astype(jnp.bfloat16)
    value_vals = qkv[:, attn_width + kv_width :].astype(jnp.bfloat16)
    keys_all, values_all = (
        lax.all_gather(key_vals.reshape(tok_rows, kv_width), "seq", axis=0, tiled=True),
        lax.all_gather(value_vals, "seq", axis=0, tiled=True),
    )
    query_heads = queries.reshape(tok_rows, KV_HEADS, group_size, HEAD_DIM).transpose(1, 0, 2, 3)
    key_heads = keys_all.reshape(slot_count, KV_HEADS, HEAD_DIM).transpose(1, 0, 2)
    value_heads = values_all.reshape(slot_count, KV_HEADS, HEAD_DIM).transpose(1, 0, 2)

    def masked_scores(query_piece, key_piece):
        raw_scores = jnp.einsum(
            "tgd,sd->tgs", query_piece, key_piece, preferred_element_type=jnp.float32
        )
        return jnp.where(allowed[:, None, :], raw_scores * SCORE_SCALE, -1e30)

    def forward_head(head_item):
        query_piece, key_piece, value_piece = head_item
        scores = masked_scores(query_piece, key_piece)
        largest = jnp.max(scores, axis=2, keepdims=True)
        totals = jnp.sum(jnp.exp(scores - largest), axis=2, keepdims=True)
        log_totals = largest + jnp.log(totals)
        probabilities = jnp.exp(scores - log_totals).astype(jnp.bfloat16)
        head_out = jnp.einsum(
            "tgs,sd->tgd", probabilities, value_piece, preferred_element_type=jnp.float32
        )
        return (head_out.astype(jnp.bfloat16), log_totals[:, :, 0])

    head_outs, log_sums = lax.map(forward_head, (query_heads, key_heads, value_heads))
    attended = head_outs.transpose(1, 0, 2, 3).reshape(tok_rows, attn_width)
    branch = jnp.dot(attended, full_out, preferred_element_type=jnp.float32)
    hidden = token_vals + RESIDUAL_SCALE * branch
    inv_second = lax.rsqrt(jnp.mean(hidden * hidden, axis=1, keepdims=True) + EPSILON)
    unit_second = hidden * inv_second
    normed2 = (unit_second * gain_second).astype(jnp.bfloat16)
    gate_up = jnp.dot(normed2, full_gate_up, preferred_element_type=jnp.float32)
    gate_vals = gate_up[:, :FF]
    up_vals = gate_up[:, FF:]
    sigmoid_gate = jax.nn.sigmoid(gate_vals)
    mixed_vals = (gate_vals * sigmoid_gate * up_vals).astype(jnp.bfloat16)
    down_out = jnp.dot(mixed_vals, full_down, preferred_element_type=jnp.float32)
    output = (valid_rows * (hidden + RESIDUAL_SCALE * down_out)).astype(jnp.bfloat16)
    back_columns = (
        lax.all_gather(w_qkv, "dp", axis=1, tiled=True),
        lax.all_gather(w_out, "dp", axis=1, tiled=True),
        lax.all_gather(w_gate_up, "dp", axis=1, tiled=True),
        lax.all_gather(w_down, "dp", axis=1, tiled=True),
    )
    back_qkv, back_out, back_gate_up, back_down, back_gains = (
        lax.all_gather(back_columns[0], "seq", axis=0, tiled=True),
        lax.all_gather(back_columns[1], "seq", axis=0, tiled=True),
        lax.all_gather(back_columns[2], "seq", axis=0, tiled=True),
        lax.all_gather(back_columns[3], "seq", axis=0, tiled=True),
        lax.all_gather(gains, "seq", axis=0, tiled=True),
    )
    back_first = back_gains[:, 0].astype(jnp.float32)
    back_second = back_gains[:, 1].astype(jnp.float32)
    upstream = cotangent[0].astype(jnp.float32) * valid_rows
    down_grad = (RESIDUAL_SCALE * upstream).astype(jnp.bfloat16)
    mixed_grad = times_transposed(down_grad, back_down)
    gate_grad = mixed_grad * up_vals * sigmoid_gate * (1.0 + gate_vals * (1.0 - sigmoid_gate))
    up_grad = mixed_grad * gate_vals * sigmoid_gate
    gate_up_grad = jnp.concatenate([gate_grad, up_grad], axis=1).astype(jnp.bfloat16)
    grad_down_rows = lax.psum_scatter(
        jnp.einsum("tf,td->fd", mixed_vals, down_grad, preferred_element_type=jnp.float32),
        "seq",
        scatter_dimension=0,
        tiled=True,
    )
    grad_gate_up_rows = lax.psum_scatter(
        jnp.einsum("tc,tf->cf", normed2, gate_up_grad, preferred_element_type=jnp.float32),
        "seq",
        scatter_dimension=0,
        tiled=True,
    )
    normed2_grad = times_transposed(gate_up_grad, back_gate_up)
    unit_grad2 = normed2_grad * back_second
    hidden_grad = upstream + inv_second * (
        unit_grad2 - unit_second * jnp.mean(unit_grad2 * unit_second, axis=1, keepdims=True)
    )
    gain_second_term = jnp.sum(normed2_grad * unit_second, axis=0)
    branch_grad = (RESIDUAL_SCALE * hidden_grad).astype(jnp.bfloat16)
    grad_out_term = jnp.einsum(
        "ta,td->ad", attended, branch_grad, preferred_element_type=jnp.float32
    )
    attended_grad = times_transposed(branch_grad, back_out).astype(jnp.bfloat16)
    grad_heads = attended_grad.reshape(tok_rows, KV_HEADS, group_size, HEAD_DIM).transpose(
        1, 0, 2, 3
    )

    def backward_head(head_item):
        query_piece, key_piece, value_piece, grad_piece, log_piece = head_item
        scores = masked_scores(query_piece, key_piece)
        probabilities = jnp.exp(scores - log_piece[:, :, None])
        value_term = jnp.einsum(
            "tgs,tgd->sd",
            probabilities.astype(jnp.bfloat16),
            grad_piece,
            preferred_element_type=jnp.float32,
        )
        prob_grad = jnp.einsum(
            "tgd,sd->tgs", grad_piece, value_piece, preferred_element_type=jnp.float32
        )
        row_dot = jnp.sum(probabilities * prob_grad, axis=2, keepdims=True)
        score_grad = (probabilities * (prob_grad - row_dot) * SCORE_SCALE).astype(jnp.bfloat16)
        query_grad = jnp.einsum(
            "tgs,sd->tgd", score_grad, key_piece, preferred_element_type=jnp.float32
        )
        key_term = jnp.einsum(
            "tgs,tgd->sd", score_grad, query_piece, preferred_element_type=jnp.float32
        )
        return (query_grad, key_term, value_term)

    query_grads, key_terms, value_terms = lax.map(
        backward_head, (query_heads, key_heads, value_heads, grad_heads, log_sums)
    )
    key_grad, value_grad = (
        lax.psum_scatter(
            key_terms.transpose(1, 0, 2).reshape(slot_count, kv_width),
            "seq",
            scatter_dimension=0,
            tiled=True,
        ),
        lax.psum_scatter(
            value_terms.transpose(1, 0, 2).reshape(slot_count, kv_width),
            "seq",
            scatter_dimension=0,
            tiled=True,
        ),
    )
    query_back = rotate(
        query_grads.transpose(1, 0, 2, 3).reshape(tok_rows, HEADS, HEAD_DIM),
        cosine,
        sine_table,
        -1.0,
    )
    key_back = rotate(key_grad.reshape(tok_rows, KV_HEADS, HEAD_DIM), cosine, sine_table, -1.0)
    qkv_grad = jnp.concatenate(
        [
            query_back.reshape(tok_rows, attn_width),
            key_back.reshape(tok_rows, kv_width),
            value_grad,
        ],
        axis=1,
    ).astype(jnp.bfloat16)
    grad_qkv_term = jnp.einsum("tc,tq->cq", normed, qkv_grad, preferred_element_type=jnp.float32)
    normed_grad = times_transposed(qkv_grad, back_qkv)
    unit_grad1 = normed_grad * back_first
    token_grad = hidden_grad + inv_first * (
        unit_grad1 - unit_first * jnp.mean(unit_grad1 * unit_first, axis=1, keepdims=True)
    )
    gain_first_term = jnp.sum(normed_grad * unit_first, axis=0)
    gains_term = jnp.stack([gain_first_term, gain_second_term], axis=1)
    grad_qkv_rows, grad_out_rows, grad_gain_rows = (
        lax.psum_scatter(grad_qkv_term, "seq", scatter_dimension=0, tiled=True),
        lax.psum_scatter(grad_out_term, "seq", scatter_dimension=0, tiled=True),
        lax.psum_scatter(gains_term, "seq", scatter_dimension=0, tiled=True),
    )
    summed = (
        lax.psum_scatter(grad_qkv_rows, "dp", scatter_dimension=1, tiled=True),
        lax.psum_scatter(grad_out_rows, "dp", scatter_dimension=1, tiled=True),
        lax.psum_scatter(grad_gate_up_rows, "dp", scatter_dimension=1, tiled=True),
        lax.psum_scatter(grad_down_rows, "dp", scatter_dimension=1, tiled=True),
    )
    grad_gains = lax.psum(grad_gain_rows, "dp")
    return (output[None], token_grad[None], summed[0], summed[1], summed[2], summed[3], grad_gains)


def solution(mesh):
    in_specs = (
        P("dp", "seq", None),
        P("dp"),
        P("seq", "dp"),
        P("seq", "dp"),
        P("seq", "dp"),
        P("seq", "dp"),
        P("seq", None),
        P("dp", "seq", None),
    )
    out_specs = (
        P("dp", "seq", None),
        P("dp", "seq", None),
        P("seq", "dp"),
        P("seq", "dp"),
        P("seq", "dp"),
        P("seq", "dp"),
        P("seq", None),
    )
    return jax.shard_map(local, mesh=mesh, in_specs=in_specs, out_specs=out_specs, check_vma=False)
```

profile of v0, /device:TPU:0, one launch (start us, length us, event | category | flops | bytes accessed | tf_op | source)
XLA Modules:
  0.0 4255.1 jit_solution(1165664101666246665)
XLA Ops:
  7.9 35.5 all-gather.11.cloned.1.call-done
  45.4 11.7 all_gather.42
  57.4 104.4 %all-gather.13.cloned.1.call-done = bf16[2048,3072]{1,0:T(8,128)(2,1)} async-done(((bf16[256,3072]{1,0:T(8,128)(2,1)}), bf16[2048,3072]{1,0:T(8,128)(2,1)}) %all-gather.13.cloned.1.call-update) | async-done | bytes 12582928 | tf_op jit(solution)/shard_map/all_gather | solution.py:59
  161.8 6.5 fusion.104
  170.5 17.7 all-gather.19.cloned.1.call-done
  188.3 89.1 %all-gather.23.cloned.1.call-done = bf16[256,16384]{1,0:T(8,128)(2,1)} async-done(((bf16[256,4096]{1,0:T(8,128)(2,1)}), bf16[256,16384]{1,0:T(8,128)(2,1)}) %all-gather.23.cloned.1.call-update) | async-done | bytes 8388624 | tf_op jit(solution)/shard_map/all_gather | solution.py:55
  277.5 54.1 %all-gather.27.cloned.1.call-done = bf16[1024,2048]{1,0:T(8,128)(2,1)} async-done(((bf16[1024,512]{1,0:T(8,128)(2,1)}), bf16[1024,2048]{1,0:T(8,128)(2,1)}) %all-gather.27.cloned.1.call-update) | async-done | bytes 4194320 | tf_op jit(solution)/shard_map/all_gather | solution.py:56
  336.1 19.8 all-gather.17.cloned.1.call-done
  355.9 2.0 copy.40
  357.9 22.0 all-gather.15.cloned.1.call-done
  381.4 22.0 while.28
  403.4 59.8 %all-gather.21.cloned.1.call-done = bf16[2048,2048]{1,0:T(8,128)(2,1)} async-done(((bf16[256,2048]{1,0:T(8,128)(2,1)}), bf16[2048,2048]{1,0:T(8,128)(2,1)}) %all-gather.21.cloned.1.call-update) | async-done | bytes 8388624 | tf_op jit(solution)/shard_map/all_gather | solution.py:60
  463.2 4.8 multiply_reduce_fusion.3
  468.0 559.3 %all-gather.25.cloned.1.call-done = bf16[2048,16384]{1,0:T(8,128)(2,1)} async-done(((bf16[256,16384]{1,0:T(8,128)(2,1)}), bf16[2048,16384]{1,0:T(8,128)(2,1)}) %all-gather.25.cloned.1.call-update) | async-done | bytes 67108880 | tf_op jit(solution)/shard_map/all_gather | solution.py:61
  1027.3 31.5 fusion.117
  1058.8 256.7 %all-gather.29.cloned.1.call-done = bf16[8192,2048]{1,0:T(8,128)(2,1)} async-done(((bf16[1024,2048]{1,0:T(8,128)(2,1)}), bf16[8192,2048]{1,0:T(8,128)(2,1)}) %all-gather.29.cloned.1.call-update) | async-done | bytes 33554448 | tf_op jit(solution)/shard_map/all_gather | solution.py:62
  1315.5 20.0 multiply_convert_fusion.2
  1335.5 31.0 multiply_reduce_fusion.1
  1369.3 6.3 convolution_convert_fusion.1
  1376.5 107.2 %while.29 = (s32[]{:T(128)}, f32[8,128,4,64]{1,3,2,0:T(8,128)}, f32[8,1024,64]{1,2,0:T(8,128)}, f32[8,1024,64]{1,2,0:T(8,128)}, bf16[8,128,4,64]{1,3,2,0:T(8,128...) while((s32[]{:T(128)}, f32[8,128,4,64]{1,3,2,0:T(8,128)}, ...), condition=%wide.region_9.10_spmd.clone, body=%wide.region_7.9_spmd.clone.sunk | while | flops 343149568 | bytes 24654464 | solution.py:193
  1378.3 2.7 fusion.167
  1381.0 3.5 fusion.168
  1384.6 3.5 fusion.169
  1391.7 2.7 fusion.167
  1394.4 3.5 fusion.168
  1398.0 3.5 fusion.169
  1405.1 2.7 fusion.167
  1407.9 3.5 fusion.168
  1411.4 3.5 fusion.169
  1418.5 2.7 fusion.167
  1421.2 3.5 fusion.168
  1424.8 3.5 fusion.169
  1431.9 2.7 fusion.167
  1434.6 3.5 fusion.168
  1438.1 3.5 fusion.169
  1441.7 1.8 fusion.170
  1445.3 2.7 fusion.167
  1448.0 3.5 fusion.168
  1451.5 3.5 fusion.169
  1458.7 2.7 fusion.167
  1461.4 3.5 fusion.168
  1464.9 3.5 fusion.169
  1472.1 2.7 fusion.167
  1474.8 3.5 fusion.168
  1478.3 3.5 fusion.169
  1481.9 1.9 fusion.170
  1485.1 8.1 fusion.98
  1494.8 23.4 reduce-scatter.16.cloned.1.call-done
  1519.1 36.4 reduce-scatter.14.cloned.1.call-done
  1557.6 11.3 fusion.95
  1569.9 25.6 fusion.99
  1595.6 47.3 %fusion.68 = f32[2048,16384]{1,0:T(8,128)} fusion(bf16[128,8192]{1,0:T(8,128)(2,1)} %get-tuple-element.197, bf16[128,8192]{1,0:T(8,128)(2,1)} %copy-done.5, f32[128,2048]{1,0:T(8,128)S(1)} %get-tuple-element.213, f32[2048]{0:T(1024)S(1)} %bitcast.189, f32[128]{0:T(128)S(1)} %add_rsqrt_fusion), kind=kOutput, calls=%fused_computation.70 | convolution fusion | flops 8599109632 | bytes 139469312 | tf_op jit(solution)/shard_map/tc,tf->cf/dot_general | solution.py:150
  1643.0 9.4 fusion.85
  1654.0 70.7 %reduce-scatter.22.cloned.1.call-done = f32[256,2048]{1,0:T(8,128)} async-done(((f32[2048,2048]{1,0:T(8,128)}), f32[256,2048]{1,0:T(8,128)}) %reduce-scatter.22.cloned.1.call-update) | async-done | bytes 2097168 | tf_op jit(solution)/shard_map/reduce_scatter | solution.py:235
  1724.8 247.7 %reduce-scatter.18.cloned.1.call-done = f32[256,3072]{1,0:T(8,128)} async-done(((f32[2048,3072]{1,0:T(8,128)}), f32[256,3072]{1,0:T(8,128)}) %reduce-scatter.18.cloned.1.call-update) | async-done | bytes 3145744 | tf_op jit(solution)/shard_map/reduce_scatter | solution.py:234
  1972.6 640.7 %reduce-scatter.30.cloned.1.call-done = f32[1024,2048]{1,0:T(8,128)} async-done(((f32[8192,2048]{1,0:T(8,128)}), f32[1024,2048]{1,0:T(8,128)}) %reduce-scatter.30.cloned.1.call-update) | async-done | bytes 8388624 | tf_op jit(solution)/shard_map/reduce_scatter | solution.py:143
  2613.6 1269.6 %reduce-scatter.26.cloned.1.call-done = f32[256,16384]{1,0:T(8,128)} async-done(((f32[2048,16384]{1,0:T(8,128)}), f32[256,16384]{1,0:T(8,128)}) %reduce-scatter.26.cloned.1.call-update) | async-done | bytes 16777232 | tf_op jit(solution)/shard_map/reduce_scatter | solution.py:149
  3883.3 16.7 fusion.74
  3901.3 15.1 reduce-scatter.34.cloned.1.call-done
  3917.4 10.6 psum.7
  3928.0 25.3 reduce-scatter.24.cloned.1.call-done
  3953.2 47.5 %reduce-scatter.20.cloned.1.call-done = f32[256,768]{1,0:T(8,128)} async-done(((f32[256,3072]{1,0:T(8,128)}), f32[256,768]{1,0:T(8,128)}) %reduce-scatter.20.cloned.1.call-update) | async-done | bytes 786448 | tf_op jit(solution)/shard_map/reduce_scatter | solution.py:239
  4000.8 89.8 %reduce-scatter.32.cloned.1.call-done = f32[1024,512]{1,0:T(8,128)} async-done(((f32[1024,2048]{1,0:T(8,128)}), f32[1024,512]{1,0:T(8,128)}) %reduce-scatter.32.cloned.1.call-update) | async-done | bytes 2097168 | tf_op jit(solution)/shard_map/reduce_scatter | solution.py:242
  4090.6 157.4 %reduce-scatter.28.cloned.1.call-done = f32[256,4096]{1,0:T(8,128)} async-done(((f32[256,16384]{1,0:T(8,128)}), f32[256,4096]{1,0:T(8,128)}) %reduce-scatter.28.cloned.1.call-update) | async-done | bytes 4194320 | tf_op jit(solution)/shard_map/reduce_scatter | solution.py:241
  (187 shorter events, 72.2 us)
Async XLA Ops:
  7.2 36.3 all-gather.11.cloned.1.call-start
  7.9 153.9 %all-gather.13.cloned.1.call-start = ((), (), s32[]{:S(2)}) async-start(), calls=%async_computation.12 | async-start | bytes 14155776 | tf_op jit(solution)/shard_map/all_gather | solution.py:59
  43.4 2.0 copy-start.14
  43.5 13.7 copy-start
  43.5 144.8 %all-gather.19.cloned.1.call-start = ((), (), s32[]{:S(2)}) async-start(), calls=%async_computation.15 | async-start | bytes 1310720 | tf_op jit(solution)/shard_map/all_gather | solution.py:54
  44.2 233.2 %all-gather.23.cloned.1.call-start = ((), (), s32[]{:S(2)}) async-start(), calls=%async_computation.17 | async-start | bytes 10485760 | tf_op jit(solution)/shard_map/all_gather | solution.py:55
  44.8 286.8 %all-gather.27.cloned.1.call-start = ((), (), s32[]{:S(2)}) async-start(), calls=%async_computation.19 | async-start | bytes 5242880 | tf_op jit(solution)/shard_map/all_gather | solution.py:56
  45.4 310.5 %all-gather.17.cloned.1.call-start = ((), (), s32[]{:S(2)}) async-start(), calls=%async_computation.14 | async-start | bytes 1179648 | tf_op jit(solution)/shard_map/all_gather | solution.py:84
  169.0 210.9 %all-gather.15.cloned.1.call-start = ((), (), s32[]{:S(2)}) async-start(), calls=%async_computation.13 | async-start | bytes 1179648 | tf_op jit(solution)/shard_map/all_gather | solution.py:83
  170.5 292.7 %all-gather.21.cloned.1.call-start = ((), (), s32[]{:S(2)}) async-start(), calls=%async_computation.16 | async-start | bytes 9437184 | tf_op jit(solution)/shard_map/all_gather | solution.py:60
  188.2 839.0 %all-gather.25.cloned.1.call-start = ((), (), s32[]{:S(2)}) async-start(), calls=%async_computation.18 | async-start | bytes 75497472 | tf_op jit(solution)/shard_map/all_gather | solution.py:61
  277.5 1038.1 %all-gather.29.cloned.1.call-start = ((), (), s32[]{:S(2)}) async-start(), calls=%async_computation.20 | async-start | bytes 37748736 | tf_op jit(solution)/shard_map/all_gather | solution.py:62
  331.6 1186.5 %reduce-scatter.16.cloned.1.call-start = ((), (), s32[]{:S(2)}) async-start(), calls=%async_computation.22 | async-start | bytes 2359296 | tf_op jit(solution)/shard_map/reduce_scatter | solution.py:203
  336.1 45.3 %copy-start.8 = (bf16[8,128,4,64]{1,3,2,0:T(8,128)(2,1)S(1)}, bf16[8,128,4,64]{1,3,2,0:T(8,128)(2,1)}, u32[]{:S(2)}) copy-start(bf16[8,128,4,64]{1,3,2,0:T(8,128)(2,1)} %custom-call) | copy-start | bytes 1572868
  403.4 59.8 %copy-start.6 = (bf16[8,1024,64]{1,2,0:T(8,128)(2,1)}, bf16[8,1024,64]{1,2,0:T(8,128)(2,1)S(1)}, u32[]{:S(2)}) copy-start(bf16[8,1024,64]{1,2,0:T(8,128)(2,1)S(1)} %get-tuple-element.440) | copy-start | bytes 3145732
  403.4 64.6 %copy-start.7 = (bf16[8,1024,64]{1,2,0:T(8,128)(2,1)}, bf16[8,1024,64]{1,2,0:T(8,128)(2,1)S(1)}, u32[]{:S(2)}) copy-start(bf16[8,1024,64]{1,2,0:T(8,128)(2,1)S(1)} %get-tuple-element.441) | copy-start | bytes 3145732
  403.4 64.6 %copy-start.9 = (bf16[8,128,4,64]{1,3,2,0:T(8,128)(2,1)}, bf16[8,128,4,64]{1,3,2,0:T(8,128)(2,1)S(1)}, u32[]{:S(2)}) copy-start(bf16[8,128,4,64]{1,3,2,0:T(8,128)(2,1)S(1)} %get-tuple-element.99) | copy-start | bytes 1572868
  1335.5 31.1 copy-start.5
  1368.3 1.0 copy-start.2
  1483.7 1.2 copy-start.3
  1483.7 1.4 copy-start.10
  1483.7 71.8 %reduce-scatter.14.cloned.1.call-start = ((), (), s32[]{:S(2)}) async-start(), calls=%async_computation.21 | async-start | bytes 2359296 | tf_op jit(solution)/shard_map/reduce_scatter | solution.py:197
  1484.3 240.4 %reduce-scatter.22.cloned.1.call-start = ((), (), s32[]{:S(2)}) async-start(), calls=%async_computation.25 | async-start | bytes 18874368 | tf_op jit(solution)/shard_map/reduce_scatter | solution.py:235
  1493.2 1.2 copy-start.11
  1493.2 479.3 %reduce-scatter.18.cloned.1.call-start = ((), (), s32[]{:S(2)}) async-start(), calls=%async_computation.23 | async-start | bytes 28311552 | tf_op jit(solution)/shard_map/reduce_scatter | solution.py:234
  1494.6 63.0 %copy-start.1 = (bf16[1,128,2048]{2,1,0:T(8,128)(2,1)S(1)}, bf16[1,128,2048]{2,1,0:T(8,128)(2,1)}, u32[]{:S(2)}) copy-start(bf16[1,128,2048]{2,1,0:T(8,128)(2,1)} %param.12) | copy-start | bytes 1572868
  1568.8 1.0 copy-start.12
  1568.9 1044.4 %reduce-scatter.30.cloned.1.call-start = ((), (), s32[]{:S(2)}) async-start(), calls=%async_computation.29 | async-start | bytes 75497472 | tf_op jit(solution)/shard_map/reduce_scatter | solution.py:143
  1595.5 2287.7 %reduce-scatter.26.cloned.1.call-start = ((), (), s32[]{:S(2)}) async-start(), calls=%async_computation.27 | async-start | bytes 150994944 | tf_op jit(solution)/shard_map/reduce_scatter | solution.py:149
  1642.9 9.5 copy-start.13
  1642.9 2273.5 %reduce-scatter.34.cloned.1.call-start = ((), (), s32[]{:S(2)}) async-start(), calls=%async_computation.31 | async-start | bytes 1179648
  1653.9 2299.3 %reduce-scatter.24.cloned.1.call-start = ((), (), s32[]{:S(2)}) async-start(), calls=%async_computation.26 | async-start | bytes 2621440 | tf_op jit(solution)/shard_map/reduce_scatter | solution.py:240
  1724.7 2276.0 %reduce-scatter.20.cloned.1.call-start = ((), (), s32[]{:S(2)}) async-start(), calls=%async_computation.24 | async-start | bytes 3932160 | tf_op jit(solution)/shard_map/reduce_scatter | solution.py:239
  1972.5 2118.1 %reduce-scatter.32.cloned.1.call-start = ((), (), s32[]{:S(2)}) async-start(), calls=%async_computation.30 | async-start | bytes 10485760 | tf_op jit(solution)/shard_map/reduce_scatter | solution.py:242
  2613.3 1634.7 %reduce-scatter.28.cloned.1.call-start = ((), (), s32[]{:S(2)}) async-start(), calls=%async_computation.28 | async-start | bytes 20971520 | tf_op jit(solution)/shard_map/reduce_scatter | solution.py:241
  3883.2 16.7 copy-start.4
Sparse Core Ops, SparseCore 0:
  9.8 33.5 all-gather.10
  45.1 116.6 all-gather.12
  163.6 24.5 all-gather.18
  189.9 87.4 all-gather.22
  279.1 52.4 all-gather.26
  333.6 22.2 all-gather.16
  358.0 21.8 all-gather.14
  381.5 81.6 all-gather.20
  464.8 562.4 all-gather.24
  1028.7 286.7 all-gather.28
  1483.9 34.2 reduce-scatter.15
  1520.9 34.6 reduce-scatter.13
  1557.9 166.7 reduce-scatter.21
  1726.9 245.5 reduce-scatter.17
  1974.7 638.4 reduce-scatter.29
  2615.5 1267.6 reduce-scatter.25
  3885.3 31.0 reduce-scatter.33
  3919.8 33.3 reduce-scatter.23
  3956.8 43.9 reduce-scatter.19
  4004.3 86.3 reduce-scatter.31
  4094.3 153.7 reduce-scatter.27
where the time goes:
time: 4260 us
  waiting for transfers between devices  3850 us (90%)
  matrix products  340 us (8%)
    reduce_scatter x1, waiting for transfers between devices, local(): lax.psum_scatter(jnp.einsum('tc,tf->cf', normed2, gate_up_grad, preferred...  1270 us
    reduce_scatter x1, waiting for transfers between devices, local(): lax.psum_scatter(jnp.einsum('tf,td->fd', mixed_vals, down_grad, preferred...  641 us
    all_gather x1, waiting for transfers between devices, local(): lax.all_gather(columns[2], 'seq', axis=0, tiled=True)  559 us
    all_gather x1, waiting for transfers between devices, local(): lax.all_gather(columns[3], 'seq', axis=0, tiled=True)  257 us
    reduce_scatter x1, waiting for transfers between devices, local(): lax.psum_scatter(grad_qkv_term, 'seq', scatter_dimension=0, tiled=True)  248 us
    reduce_scatter x1, waiting for transfers between devices, local(): lax.psum_scatter(grad_gate_up_rows, 'dp', scatter_dimension=1, tiled=True)  157 us
    all_gather x1, waiting for transfers between devices, local(): lax.all_gather(columns[0], 'seq', axis=0, tiled=True)  104 us
    reduce_scatter x1, waiting for transfers between devices, local(): lax.psum_scatter(grad_down_rows, 'dp', scatter_dimension=1, tiled=True)  89.8 us
  transfers between devices with their start and end apart: 21, of which 21 were waited for; matrix products, arithmetic and copies ran while one was open for 5% of the time, Pallas kernels for 0%

commit v1 on v0

v1 whole, which is shorter than its diff:
```python
import functools

import jax
import jax.numpy as jnp
from jax import lax
from jax.experimental import pallas as pl
from jax.experimental.pallas import tpu as pltpu
from jax.sharding import PartitionSpec as P

HEADS = 32
KV_HEADS = 8
HEAD_DIM = 64
FF = 8192
ATTN = HEADS * HEAD_DIM
KV = KV_HEADS * HEAD_DIM
PAIR = 2 * HEAD_DIM

EPSILON = 1e-05
RESIDUAL_SCALE = 0.22
SCORE_SCALE = 1.0 / 64.0
ROPE_THETA = 10000000.0
BLOCK = 256

BF16 = jnp.bfloat16
F32 = jnp.float32


def dot(left, right):
    return jnp.dot(left, right, preferred_element_type=F32)


def dot_nt(left, right):
    return lax.dot_general(left, right, (((1,), (1,)), ((), ())), preferred_element_type=F32)


def dot_tn(left, right):
    return lax.dot_general(left, right, (((0,), (0,)), ((), ())), preferred_element_type=F32)


tie = lax.optimization_barrier


def rotary_pair(slots):
    half_dim = HEAD_DIM // 2
    frequency = ROPE_THETA ** (-(jnp.arange(half_dim, dtype=F32) * 2.0) / HEAD_DIM)
    angles = jnp.arange(slots, dtype=jnp.int32).astype(F32)[:, None] * frequency[None, :]
    angles = jnp.concatenate([angles] * 4, axis=1)
    return (jnp.cos(angles), jnp.sin(angles))


def turn(values):
    half = HEAD_DIM // 2
    lane = lax.broadcasted_iota(jnp.int32, values.shape, 1) % HEAD_DIM
    ahead = pltpu.roll(values, PAIR - half, 1)
    behind = pltpu.roll(values, half, 1)
    return jnp.where(lane < half, -ahead, behind)


def left_lanes(shape):
    return lax.broadcasted_iota(jnp.int32, shape, 1) < HEAD_DIM


def mask_bias(start, block, stop, length):
    key = lax.broadcasted_iota(jnp.int32, (stop, block), 0)
    query = lax.broadcasted_iota(jnp.int32, (stop, block), 1) + start
    return jnp.where((key <= query) & (key < length), 0.0, -1e30)


def attend_kernel(block, length_ref, qkv_ref, cos_ref, sin_ref, out_ref, q_ref, k_ref, v_ref, lse_ref):
    slots = qkv_ref.shape[0]
    pairs = q_ref.shape[1] // PAIR
    length = length_ref[0]
    cosine, sine = cos_ref[...], sin_ref[...]
    for pair in range(pairs):
        lanes = slice(pair * PAIR, (pair + 1) * PAIR)
        values = qkv_ref[:, lanes]
        rotated = (values * cosine + turn(values) * sine).astype(BF16)
        q_ref[:, lanes] = rotated * jnp.asarray(SCORE_SCALE, BF16)
    values = qkv_ref[:, pairs * PAIR :]
    left = left_lanes(values.shape)
    swapped = pltpu.roll(values, HEAD_DIM, 1)
    keys = jnp.where(left, values, swapped)
    k_ref[...] = (keys * cosine + turn(keys) * sine).astype(BF16)
    v_both = jnp.where(left, swapped, values)
    v_ref[...] = v_both.astype(BF16)
    v_t = v_both.T.astype(BF16)
    lse_ref[...] = jnp.zeros_like(lse_ref)
    for start in range(0, slots, block):
        stop = start + block
        rows = slice(start, stop)
        bias = mask_bias(start, block, stop, length)
        keys = k_ref[:stop]
        for pair in range(pairs):
            lanes = slice(pair * PAIR, (pair + 1) * PAIR)
            queries = q_ref[rows, lanes]
            left = left_lanes(queries.shape)
            outs = []
            for side in range(2):
                query = jnp.where(left == (side == 0), queries, jnp.zeros_like(queries))
                scores = dot_nt(keys, query) + bias
                largest = jnp.max(scores, axis=0, keepdims=True)
                weights = jnp.exp(scores - largest)
                total = jnp.sum(weights, axis=0, keepdims=True)
                head = 2 * pair + side
                lse_ref[head : head + 1, rows] = largest + jnp.log(total)
                probabilities = (weights * (1.0 / total)).astype(BF16)
                outs.append(dot(v_t[:, :stop], probabilities))
            first = lax.broadcasted_iota(jnp.int32, outs[0].shape, 0) < HEAD_DIM
            out_ref[rows, lanes] = jnp.where(first, outs[0], outs[1]).T.astype(BF16)


def attend(qkv, cosine, sine, lengths, q_width):
    slots = qkv.shape[0]
    block = min(BLOCK, slots)
    full = pl.BlockSpec(memory_space=pltpu.VMEM)
    shape = jax.ShapeDtypeStruct
    return pl.pallas_call(
        functools.partial(attend_kernel, block),
        out_shape=(
            shape((slots, q_width), BF16),
            shape((slots, q_width), BF16),
            shape((slots, PAIR), BF16),
            shape((slots, PAIR), BF16),
            shape((8, slots), F32),
        ),
        in_specs=[pl.BlockSpec(memory_space=pltpu.SMEM), full, full, full],
        out_specs=(full,) * 5,
        compiler_params=pltpu.CompilerParams(vmem_limit_bytes=48 << 20),
        cost_estimate=pl.CostEstimate(
            flops=4 * slots * slots * q_width, bytes_accessed=12 * slots * q_width,
            transcendentals=slots * slots * q_width // HEAD_DIM,
        ),
    )(lengths, qkv, cosine, sine)


def attend_back_kernel(
    block, length_ref, q_ref, k_ref, v_ref, lse_ref, grad_ref, cos_ref, sin_ref, out_ref, dk_ref, dv_ref
):
    slots = q_ref.shape[0]
    pairs = q_ref.shape[1] // PAIR
    length = length_ref[0]
    dk_ref[...] = jnp.zeros_like(dk_ref)
    dv_ref[...] = jnp.zeros_like(dv_ref)
    k_t = k_ref[...].astype(F32).T.astype(BF16)
    for start in range(0, slots, block):
        stop = start + block
        rows = slice(start, stop)
        bias = mask_bias(start, block, stop, length)
        keys, values = k_ref[:stop], v_ref[:stop]
        for pair in range(pairs):
            lanes = slice(pair * PAIR, (pair + 1) * PAIR)
            queries, grads = q_ref[rows, lanes], grad_ref[rows, lanes]
            left = left_lanes(queries.shape)
            parts = []
            for side in range(2):
                head = 2 * pair + side
                query = jnp.where(left == (side == 0), queries, jnp.zeros_like(queries))
                grad = jnp.where(left == (side == 0), grads, jnp.zeros_like(grads))
                scores = dot_nt(keys, query) + bias
                weights = jnp.exp(scores - lse_ref[head : head + 1, rows])
                dv_ref[:stop] += dot(weights.astype(BF16), grad)
                d_weights = dot_nt(values, grad)
                row_dot = jnp.sum(weights * d_weights, axis=0, keepdims=True)
                d_scores = (weights * (d_weights - row_dot)).astype(BF16)
                dk_ref[:stop] += dot(d_scores, query)
                parts.append(dot(k_t[:, :stop], d_scores))
            first = lax.broadcasted_iota(jnp.int32, parts[0].shape, 0) < HEAD_DIM
            d_query = jnp.where(first, parts[0], parts[1]).T * SCORE_SCALE
            d_query = d_query * cos_ref[rows] - turn(d_query) * sin_ref[rows]
            out_ref[rows, lanes] = d_query.astype(BF16)
    d_key = dk_ref[...]
    d_key = d_key + pltpu.roll(d_key, HEAD_DIM, 1)
    d_key = d_key * cos_ref[...] - turn(d_key) * sin_ref[...]
    d_value = dv_ref[...]
    d_value = d_value + pltpu.roll(d_value, HEAD_DIM, 1)
    out_ref[:, pairs * PAIR :] = jnp.where(
        left_lanes(d_key.shape), d_key, d_value
    ).astype(BF16)


def attend_back(saved, grad, cosine, sine, lengths):
    query, key, value, log_sums = saved
    slots, q_width = query.shape
    block = min(BLOCK, slots)
    full = pl.BlockSpec(memory_space=pltpu.VMEM)
    return pl.pallas_call(
        functools.partial(attend_back_kernel, block),
        out_shape=jax.ShapeDtypeStruct((slots, q_width + PAIR), BF16),
        in_specs=[pl.BlockSpec(memory_space=pltpu.SMEM)] + [full] * 7,
        out_specs=full,
        scratch_shapes=[pltpu.VMEM((slots, PAIR), F32)] * 2,
        compiler_params=pltpu.CompilerParams(vmem_limit_bytes=48 << 20),
        cost_estimate=pl.CostEstimate(
            flops=10 * slots * slots * q_width, bytes_accessed=12 * slots * q_width,
            transcendentals=slots * slots * q_width // HEAD_DIM,
        ),
    )(lengths, query, key, value, log_sums, grad, cosine, sine)


def flip(mask, size):
    return [(i, i ^ mask) for i in range(size)]


def send(value, mask):
    return lax.ppermute(value, "dp", flip(mask, lax.axis_size("dp")))


def gather_near(shard):
    if lax.axis_size("dp") != 4:
        return None
    half = shard.shape[0] // 2
    top, low = shard[:half], shard[half:]
    return (send(top, 1), send(low, 1), send(top, 2), send(low, 2))


def gather_far(near):
    if near is None:
        return None
    return (send(near[0], 2), send(near[3], 1))


def place(pieces, axis):
    me = lax.axis_index("dp")
    whole = None
    for mask, piece in enumerate(pieces):
        size = piece.shape[axis]
        if whole is None:
            shape = list(piece.shape)
            shape[axis] = 4 * size
            whole = jnp.zeros(shape, piece.dtype)
        whole = lax.dynamic_update_slice_in_dim(whole, piece, (me ^ mask) * size, axis)
    return whole


def gathered(shard, near, far, axis):
    if near is None:
        return lax.all_gather(shard, "dp", axis=axis, tiled=True)
    pieces = (shard,) + tuple(
        jnp.concatenate(pair, axis=0) for pair in (near[:2], near[2:], far)
    )
    return place(pieces, axis)


def gather_direct(shard, axis):
    if lax.axis_size("dp") != 4:
        return lax.all_gather(shard, "dp", axis=axis, tiled=True)
    return place((shard, send(shard, 1), send(shard, 2), send(shard, 3)), axis)


def dp_block(partial, mask, axis):
    place = lax.axis_index("dp") ^ mask
    if partial.ndim == 2:
        size = partial.shape[1] // 4
        return lax.dynamic_slice_in_dim(partial, place * size, size, 1)
    return lax.dynamic_index_in_dim(partial, place, axis, keepdims=False)


def scatter_first(partial, axis):
    if lax.axis_size("dp") != 4:
        return lax.psum_scatter(
            partial.astype(BF16), "dp", scatter_dimension=axis, tiled=partial.ndim == 2
        )
    half = (partial.shape[0] if axis else partial.shape[1]) // 2
    beside, across, far = (dp_block(partial, mask, axis) for mask in (1, 2, 3))
    top = jnp.stack([beside[:half], far[:half]]).astype(BF16)
    low = jnp.stack([across[half:], far[half:]]).astype(BF16)
    return (send(top, 1), send(low, 2))


def scatter_second(partial, got, axis):
    if lax.axis_size("dp") != 4:
        return got.astype(F32)
    half = (partial.shape[0] if axis else partial.shape[1]) // 2
    own, beside, across = (dp_block(partial, mask, axis) for mask in (0, 1, 2))
    top, low = (part.astype(F32) for part in got)
    third = send((across[:half].astype(F32) + top[1]).astype(BF16), 2)
    fourth = send((beside[half:].astype(F32) + low[1]).astype(BF16), 1)
    return jnp.concatenate(
        [
            own[:half].astype(F32) + top[0] + third.astype(F32),
            own[half:].astype(F32) + low[0] + fourth.astype(F32),
        ],
        axis=0,
    )


def exchange(blocks, axis_name):
    return lax.all_to_all(blocks, axis_name, split_axis=0, concat_axis=0, tiled=True)


def gather_seq(shard):
    return lax.all_gather(shard, "seq", axis=0, tiled=True)


def scatter_seq(partial):
    return lax.psum_scatter(
        partial.astype(BF16), "seq", scatter_dimension=0, tiled=True
    ).astype(F32)


def gate_up_kernel(me_ref, x_ref, *refs):
    pieces, (gate_ref, up_ref, whole_out, whole, sems, out_sem) = refs[:7], refs[7:]
    me = me_ref[0]
    seqs, _, sub, ff = pieces[0].shape
    half = seqs // 2
    places = [(0, 0, seqs)] + [(mask, part * half, half) for mask in (1, 2, 3) for part in (0, 1)]
    copies = []
    for index, (piece, (mask, first, count)) in enumerate(zip(pieces, places)):
        for part in range(2):
            copies.append(
                pltpu.make_async_copy(
                    piece.at[:, part],
                    whole.at[part, pl.ds(first, count), me ^ mask],
                    sems.at[index, part],
                )
            )
    for copy in copies:
        copy.start()
    for copy in copies:
        copy.wait()
    write = pltpu.make_async_copy(whole, whole_out, out_sem)
    write.start()
    depth = whole.shape[1] * whole.shape[2] * sub
    tile = min(512, ff)
    rows = min(256, x_ref.shape[0])

    @pl.loop(0, x_ref.shape[0] // rows)
    def _(step):
        span = pl.ds(pl.multiple_of(step * rows, rows), rows)
        for start in range(0, ff, tile):
            lanes = slice(start, start + tile)
            for part, out_ref in enumerate((gate_ref, up_ref)):
                out_ref[span, lanes] = dot(
                    x_ref[span, :], whole[part, :, :, :, lanes].reshape(depth, tile)
                )

    write.wait()


def gate_up_of(normed2, pieces):
    slots = normed2.shape[0]
    seqs, parts, sub, ff = pieces[0].shape
    whole = (parts, seqs, 4, sub, ff)
    full = pl.BlockSpec(memory_space=pltpu.VMEM)
    away = pl.BlockSpec(memory_space=pl.ANY)
    shape = jax.ShapeDtypeStruct
    me = lax.axis_index("dp").astype(jnp.int32).reshape(1)
    return pl.pallas_call(
        gate_up_kernel,
        out_shape=(shape((slots, ff), F32), shape((slots, ff), F32), shape(whole, BF16)),
        in_specs=[pl.BlockSpec(memory_space=pltpu.SMEM), full] + [away] * len(pieces),
        out_specs=(full, full, away),
        scratch_shapes=[
            pltpu.VMEM(whole, BF16),
            pltpu.SemaphoreType.DMA((len(pieces), 2)),
            pltpu.SemaphoreType.DMA,
        ],
        compiler_params=pltpu.CompilerParams(vmem_limit_bytes=56 << 20),
        cost_estimate=pl.CostEstimate(
            flops=2 * slots * normed2.shape[1] * 2 * ff,
            bytes_accessed=8 * slots * ff + 8 * ff * normed2.shape[1],
            transcendentals=0,
        ),
    )(me, normed2, *pieces)


def local(tokens, lengths, w_qkv, w_out, w_gate_up, w_down, gains, cotangent):
    tok_rows, width = tokens.shape[1:]
    seqs, ranks = lax.axis_size("seq"), lax.axis_size("dp")
    slots = tok_rows * seqs
    q_width = ATTN // seqs
    repeats = max(1, seqs // KV_HEADS)
    ff = FF // seqs
    sub = w_qkv.shape[0] // ranks

    first_slot = lax.axis_index("seq") * tok_rows
    length = lengths[0]
    valid = (jnp.arange(slots, dtype=jnp.int32) < length).astype(F32)[:, None]
    valid_rows = ((first_slot + jnp.arange(tok_rows)) < length).astype(F32)[:, None]
    cosine, sine = rotary_pair(slots)

    def split_qkv(rows):
        def heads(block):
            block = block.reshape(sub, KV_HEADS, HEAD_DIM)
            return jnp.repeat(block, repeats, axis=1)

        query = rows[:, :ATTN].reshape(sub, seqs, q_width)
        joined = jnp.concatenate(
            [query, heads(rows[:, ATTN : ATTN + KV]), heads(rows[:, ATTN + KV :])], axis=2
        )
        return joined.transpose(1, 0, 2)

    def join_qkv(blocks):
        def heads(block):
            block = block.reshape(sub, KV_HEADS, repeats, HEAD_DIM)
            if repeats > 1:
                block = block.astype(F32).sum(axis=2).astype(BF16)
            return block.reshape(sub, KV)

        blocks = blocks.transpose(1, 0, 2)
        key_part = heads(blocks[:, :, q_width : q_width + HEAD_DIM])
        value_part = heads(blocks[:, :, q_width + HEAD_DIM :])
        return jnp.concatenate([blocks[:, :, :q_width].reshape(sub, ATTN), key_part, value_part], axis=1)

    all_tokens = gather_seq(tokens[0])
    gain_rows = jnp.broadcast_to(gains.T, (seqs, 2, gains.shape[0]))
    all_gains = exchange(gain_rows, "seq").transpose(1, 0, 2).reshape(2, width).astype(F32)
    gain_first, gain_second = all_gains[0], all_gains[1]
    qkv_rows = lax.all_to_all(w_qkv, "dp", split_axis=0, concat_axis=1, tiled=True)
    qkv_mine = exchange(split_qkv(qkv_rows), "seq")
    my_qkv = gather_direct(qkv_mine[:, None], 1).reshape(width, q_width + PAIR)
    my_out = gather_direct(w_out, 1)

    per_block = w_gate_up.shape[1] // ff
    gu_rows = exchange(
        w_gate_up.reshape(ranks, sub, per_block, ff).transpose(0, 2, 1, 3), "dp"
    )
    all_tokens, gu_rows, my_qkv, all_gains = tie((all_tokens, gu_rows, my_qkv, all_gains))
    w_down, my_qkv = tie((w_down, my_qkv))
    gain_first, gain_second = all_gains[0], all_gains[1]
    gu_mine = exchange(gu_rows.reshape(2, seqs, sub, ff).transpose(1, 0, 2, 3), "seq")
    down_near = gather_near(w_down)

    x_all = all_tokens.astype(F32)
    inv_all = lax.rsqrt(jnp.mean(x_all * x_all, axis=1, keepdims=True) + EPSILON)
    normed = (x_all * inv_all * gain_first).astype(BF16)
    qkv = dot(normed, my_qkv)
    attended, *saved = attend(qkv, cosine, sine, lengths, q_width)
    attended, gu_mine, down_near, my_out = tie((attended, gu_mine, down_near, my_out))
    gu_near = gather_near(gu_mine)

    x = tokens[0].astype(F32)
    branch = scatter_seq(dot(attended, my_out))
    branch, gu_near = tie((branch, gu_near))
    gu_far, down_far = gather_far(gu_near), gather_far(down_near)
    hidden = x + RESIDUAL_SCALE * branch
    inv_second = lax.rsqrt(jnp.mean(hidden * hidden, axis=1, keepdims=True) + EPSILON)
    unit_second = hidden * inv_second
    normed2 = gather_seq((unit_second * gain_second).astype(BF16))
    normed2, gu_far = tie((normed2, gu_far))
    my_down = gathered(w_down, down_near, down_far, 1)
    late_cotangent, normed2 = tie((cotangent[0], normed2))
    all_cotangent = gather_seq(late_cotangent)

    if gu_near is None:
        my_gate_up = lax.all_gather(gu_mine, "dp", axis=1).transpose(2, 0, 1, 3, 4)
        my_gate, my_up = (my_gate_up[part].reshape(width, ff) for part in range(2))
        gate_vals, up_vals = dot(normed2, my_gate), dot(normed2, my_up)
    else:
        gate_vals, up_vals, my_gate_up = gate_up_of(normed2, (gu_mine,) + gu_near + gu_far)
        my_gate, my_up = (my_gate_up[part].reshape(width, ff) for part in range(2))
    sigmoid_gate = jax.nn.sigmoid(gate_vals)
    mixed = (gate_vals * sigmoid_gate * up_vals).astype(BF16)
    down_grad = (RESIDUAL_SCALE * (all_cotangent.astype(F32) * valid)).astype(BF16)
    mixed_grad = dot_nt(down_grad, my_down)
    gate_grad = (
        mixed_grad * up_vals * sigmoid_gate * (1.0 + gate_vals * (1.0 - sigmoid_gate))
    ).astype(BF16)
    up_grad = (mixed_grad * gate_vals * sigmoid_gate).astype(BF16)
    normed2_grad = scatter_seq(dot_nt(gate_grad, my_gate) + dot_nt(up_grad, my_up))
    w_grads = jnp.stack([dot_tn(normed2, gate_grad), dot_tn(normed2, up_grad)])
    gu_partial = w_grads.astype(BF16).reshape(2, seqs, ranks, sub, ff).transpose(1, 0, 2, 3, 4)
    gu_got = scatter_first(gu_partial, 2)
    normed2_grad, gu_got = tie((normed2_grad, gu_got))

    upstream = cotangent[0].astype(F32) * valid_rows
    unit_grad2 = normed2_grad * gain_second
    hidden_grad = upstream + inv_second * (
        unit_grad2 - unit_second * jnp.mean(unit_grad2 * unit_second, axis=1, keepdims=True)
    )
    gain_second_term = jnp.sum(normed2_grad * unit_second, axis=0)
    branch_grad = gather_seq((RESIDUAL_SCALE * hidden_grad).astype(BF16))
    gu_summed = scatter_second(gu_partial, gu_got, 2)
    branch_grad, gu_summed, mixed = tie((branch_grad, gu_summed.astype(BF16), mixed))
    down_out = scatter_seq(dot(mixed, my_down))
    output = (valid_rows * (hidden + RESIDUAL_SCALE * down_out)).astype(BF16)

    attended_grad = dot_nt(branch_grad, my_out).astype(BF16)
    qkv_grad = attend_back(saved, attended_grad, cosine, sine, lengths)
    gu_blocks = exchange(gu_summed, "seq")
    down_partial = dot_tn(mixed, down_grad).astype(BF16)
    down_got = scatter_first(down_partial, 1)
    qkv_grad, down_got = tie((qkv_grad, down_got))
    normed_partial = dot_nt(qkv_grad, my_qkv)
    normed_grad = scatter_seq(normed_partial)

    qkv_partial = dot_tn(normed, qkv_grad).astype(BF16).reshape(seqs, ranks, sub, -1)
    qkv_summed = scatter_second(qkv_partial, scatter_first(qkv_partial, 1), 1)
    qkv_back = join_qkv(exchange(qkv_summed.astype(BF16), "seq"))
    grad_qkv = lax.all_to_all(qkv_back, "dp", split_axis=1, concat_axis=0, tiled=True).astype(F32)
    out_partial = dot_tn(attended, branch_grad).astype(BF16)
    grad_out = scatter_second(out_partial, scatter_first(out_partial, 1), 1)
    grad_down = scatter_second(down_partial, down_got, 1)
    gu_back = exchange(
        gu_blocks.transpose(1, 0, 2, 3).reshape(ranks, per_block, sub, ff), "dp"
    )
    grad_gate_up = gu_back.transpose(0, 2, 1, 3).reshape(w_gate_up.shape).astype(F32)

    unit_all = x_all * inv_all
    gain_first_term = jnp.sum(normed_partial * unit_all, axis=0)
    gains_term = jnp.stack([gain_first_term, gain_second_term], axis=1)
    gain_blocks = exchange(gains_term.reshape(seqs, -1, 2), "seq")
    grad_gains = jnp.sum(gain_blocks, axis=0).T
    if ranks == 4:
        grad_gains = grad_gains + send(grad_gains, 1)
        grad_gains = (grad_gains + send(grad_gains, 2)).T
    else:
        grad_gains = lax.psum(grad_gains, "dp").T

    inv_first = lax.rsqrt(jnp.mean(x * x, axis=1, keepdims=True) + EPSILON)
    unit_first = x * inv_first
    unit_grad1 = normed_grad * gain_first
    token_grad = hidden_grad + inv_first * (
        unit_grad1 - unit_first * jnp.mean(unit_grad1 * unit_first, axis=1, keepdims=True)
    )
    return (output[None], token_grad[None], grad_qkv, grad_out, grad_gate_up, grad_down, grad_gains)


def solution(mesh):
    in_specs = (
        P("dp", "seq", None),
        P("dp"),
        P("seq", "dp"),
        P("seq", "dp"),
        P("seq", "dp"),
        P("seq", "dp"),
        P("seq", None),
        P("dp", "seq", None),
    )
    out_specs = (
        P("dp", "seq", None),
        P("dp", "seq", None),
        P("seq", "dp"),
        P("seq", "dp"),
        P("seq", "dp"),
        P("seq", "dp"),
        P("seq", None),
    )
    return jax.shard_map(local, mesh=mesh, in_specs=in_specs, out_specs=out_specs, check_vma=False)
```

time: 4260 us -> 702 us (0.16)
  waiting for transfers between devices: 3850 us -> 340 us
  matrix products: 340 us -> 76.9 us
  starting transfers between devices: 1.08 us -> 74.1 us
  other arithmetic: 15.4 us -> 65.2 us
    reduce_scatter x10 -> x4, waiting for transfers between devices: 2610 us -> 65.9 us  [scatter_seq(): lax.psum_scatter(partial.astype(BF16), 'seq', scatter_dimension=0, tiled=...]
    all_gather x10 -> x4, waiting for transfers between devices: 1220 us -> 38.7 us  [gather_seq(): return lax.all_gather(shard, 'seq', axis=0, tiled=True)]
    dot_general x68 -> x13, matrix products: 340 us -> 76.9 us  [the longest x5 32.6 us: dot_nt(): lax.dot_general(left, right, (((1,), (1,)), ((), ())), preferred_element_...]
    ppermute x0 -> x36, waiting for transfers between devices: none -> 160 us  [send(): return lax.ppermute(value, 'dp', flip(mask, lax.axis_size('dp')))]
    all_to_all x0 -> x8, waiting for transfers between devices: none -> 74.7 us  [the longest x7 72.9 us: exchange(): lax.all_to_all(blocks, axis_name, split_axis=0, concat_axis=0, tiled=True)]
  transfers between devices with their start and end apart: 21 -> 52, of which waited for: 21 -> 35; matrix products, arithmetic and copies ran while one was open for 5% -> 20% of each run, Pallas kernels for 0% -> 6%
where the time goes in v1:
time: 702 us; the launch traced here: 697 us
  waiting for transfers between devices  340 us (48%)
  matrix products  76.9 us (11%)
  starting transfers between devices  74.1 us (11%)
  other arithmetic  65.2 us (9%)
  local copies, waits for them, and re-layouts  51.5 us (7%)
  Pallas kernels  39 us (6%)
  blocking collectives  33.9 us (5%)
  between operations  15.9 us (2%)
    ppermute x36, waiting for transfers between devices, send(): return lax.ppermute(value, 'dp', flip(mask, lax.axis_size('dp')))  160 us
    all_to_all x7, waiting for transfers between devices, exchange(): lax.all_to_all(blocks, axis_name, split_axis=0, concat_axis=0, tiled=True)  72.9 us
    reduce_scatter x4, waiting for transfers between devices, scatter_seq(): lax.psum_scatter(partial.astype(BF16), 'seq', scatter_dimension=0, tiled=...  65.9 us
    ppermute x36, starting transfers between devices, send(): return lax.ppermute(value, 'dp', flip(mask, lax.axis_size('dp')))  42.3 us
    all_gather x4, waiting for transfers between devices, gather_seq(): return lax.all_gather(shard, 'seq', axis=0, tiled=True)  38.7 us
    dot_general x5, matrix products, dot_nt(): lax.dot_general(left, right, (((1,), (1,)), ((), ())), preferred_element_...  32.6 us
    all_to_all x7, starting transfers between devices, exchange(): lax.all_to_all(blocks, axis_name, split_axis=0, concat_axis=0, tiled=True)  27.2 us
    dot_general x5, matrix products, dot_tn(): lax.dot_general(left, right, (((0,), (0,)), ((), ())), preferred_element_...  26.3 us
  transfers between devices with their start and end apart: 52, of which 35 were waited for; matrix products, arithmetic and copies ran while one was open for 20% of the time, Pallas kernels for 6%

profile of v1, /device:TPU:0, one launch (start us, length us, event | category | flops | bytes accessed | tf_op | source)
XLA Modules:
  0.0 696.6 jit_solution(13432861321250107542)
XLA Ops:
  7.9 12.3 %all_to_all.72 = bf16[4,64,768]{2,1,0:T(8,128)(2,1)S(1)} all-to-all(bf16[4,64,768]{2,1,0:T(8,128)(2,1)} %bitcast.334), channel_id=1, replica_groups=mesh['dp'=4,'seq'=8] {'dp'}, dimensions={0} | all-to-all | bytes 786432 | tf_op jit(solution)/shard_map/all_to_all | solution.py:409
  21.5 4.9 all-to-all-start.3
  27.7 4.5 all-to-all-done.3
  32.2 3.5 all-to-all-start.2
  35.7 2.8 reshape.158
  38.4 20.2 %all-to-all-done.2 = bf16[8,64,384]{2,1,0:T(8,128)(2,1)S(1)} async-done(((bf16[8,64,384]{2,1,0:T(8,128)(2,1)}), bf16[8,64,384]{2,1,0:T(8,128)(2,1)S(1)}, u32[]{:S(2)}, u32[]{:S(2)}) %all-to-all-start.2) | async-done | bytes 393248 | tf_op jit(solution)/shard_map/all_to_all | solution.py:288
  58.7 3.6 all-to-all-start
  68.1 28.9 %collective-permute-done = bf16[8,1,64,384]{3,2,1,0:T(8,128)(2,1)S(1)} collective-permute-done((bf16[8,1,64,384]{3,2,1,0:T(8,128)(2,1)S(1)}, bf16[8,1,64,384]{3,2,1,0:T(8,128)(2,1)S(1)}, u32[]{:S(2)}, u32[]{:S(2)}) %collective-permute-start) | collective-permute-done | bytes 393248 | tf_op jit(solution)/shard_map/ppermute | solution.py:205
  98.6 7.0 %collective-permute-done.2 = bf16[8,1,64,384]{3,2,1,0:T(8,128)(2,1)S(1)} collective-permute-done((bf16[8,1,64,384]{3,2,1,0:T(8,128)(2,1)S(1)}, bf16[8,1,64,384]{3,2,1,0:T(8,128)(2,1)S(1)}, u32[]{:S(2)}, u32[]{:S(2)}) %collective-permute-start.2) | collective-permute-done | bytes 393248 | tf_op jit(solution)/shard_map/ppermute | solution.py:205
  108.5 4.5 all-to-all-start.4
  116.9 2.5 fusion.50
  123.1 4.5 collective-permute-done.8
  133.2 3.1 fusion.4
  136.3 3.8 fusion.23.qkv_ref
  140.1 9.6 %shard_map.135 = (bf16[1024,256]{1,0:T(8,128)(2,1)S(1)}, bf16[1024,256]{1,0:T(8,128)(2,1)S(1)}, bf16[1024,128]{1,0:T(8,128)(2,1)S(1)}, bf16[1024,128]{1,0:T(8,128)(2,1)S(1)}, f32[8,1024]{1,0:T(8,128)S(1)}) custom-call(s32[1]{0:T(128)} %copy.143.length_ref, f32[1024,384]{1,0:T(8,128)S(1)} %fusion.23.qkv_ref, f32[1024,128]{1,0:T(8,128)S(1)} %get-tuple-element.134.cos_ref, ...), custom_call_target="tpu_custom_call" | custom-call | flops 1073741824 | bytes 3145728 | tf_op jit(solution)/shard_map/pallas_call | solution.py:117
  149.7 3.2 collective-permute-done.4
  153.9 8.2 %all-to-all-done.4.refs_0_ = bf16[8,2,64,1024]{3,2,1,0:T(8,128)(2,1)} async-done(((bf16[8,2,64,1024]{3,2,1,0:T(8,128)(2,1)}), bf16[8,2,64,1024]{3,2,1,0:T(8,128)(2,1)}, u32[]{:S(2)}, u32[]{:S(2)}) %all-to-all-start.4) | async-done | bytes 2097184 | tf_op jit(solution)/shard_map/all_to_all | solution.py:288
  162.1 4.9 convolution_convert_fusion
  167.1 3.2 fusion.64
  174.3 40.5 %reduce-scatter.5.cloned.1.call-done = bf16[128,2048]{1,0:T(8,128)(2,1)} async-done(((bf16[1024,2048]{1,0:T(8,128)(2,1)}), bf16[128,2048]{1,0:T(8,128)(2,1)}) %reduce-scatter.5.cloned.1.call-update) | async-done | bytes 524304 | tf_op jit(solution)/shard_map/reduce_scatter | solution.py:296
  223.9 21.7 %collective-permute-done.14.refs_5_ = bf16[4,2,64,1024]{3,2,1,0:T(8,128)(2,1)} collective-permute-done((bf16[4,2,64,1024]{3,2,1,0:T(8,128)(2,1)}, bf16[4,2,64,1024]{3,2,1,0:T(8,128)(2,1)}, u32[]{:S(2)}, u32[]{:S(2)}) %collective-permute-start.14) | collective-permute-done | bytes 1048608 | tf_op jit(solution)/shard_map/ppermute | solution.py:205
  245.8 21.4 %all-gather.6.cloned.1.call-done.x_ref = bf16[1024,2048]{1,0:T(8,128)(2,1)} async-done(((bf16[128,2048]{1,0:T(8,128)(2,1)}), bf16[1024,2048]{1,0:T(8,128)(2,1)}) %all-gather.6.cloned.1.call-update) | async-done | bytes 4194320 | tf_op jit(solution)/shard_map/all_gather | solution.py:292
  270.3 2.5 broadcast_in_dim.34
  278.6 3.1 collective-permute-done.17
  283.9 18.5 %shard_map.136 = (f32[1024,1024]{1,0:T(8,128)}, f32[1024,1024]{1,0:T(8,128)}, bf16[2,8,4,64,1024]{4,3,2,1,0:T(8,128)(2,1)}) custom-call(s32[1]{0:T(128)} %bitcast.17.me_ref, bf16[1024,2048]{1,0:T(8,128)(2,1)} %all-gather.6.cloned.1.call-done.x_ref, bf16[8,2,64,1024]{3,2,1,0:T(8,128)(2,1)} %all-to-all-done.4.refs_0_, ...), custom_call_target="tpu_custom_call" | custom-call | flops 8589934592 | bytes 25165824 | tf_op jit(solution)/shard_map/pallas_call | solution.py:348
  302.5 6.3 fusion.63
  308.8 5.6 all-gather.8.cloned.1.call-done
  314.4 7.8 %fusion.21 = f32[1024,1024]{1,0:T(8,128)S(1)} fusion(bf16[1024,2048]{1,0:T(8,128)(2,1)} %maximum_dynamic-update-slice_fusion.2, bf16[1024,2048]{1,0:T(8,128)(2,1)} %all-gather.8.cloned.1.call-done, f32[1024]{0:T(1024)S(1)} %fusion.60), kind=kOutput, calls=%fused_computation.62 | convolution fusion | flops 4303355904 | bytes 12587008 | tf_op jit(solution)/shard_map/dot_general | solution.py:33
  322.2 3.7 multiply_convert_fusion.1
  326.0 6.7 fusion.69
  332.7 8.3 %add_convert_fusion = bf16[1024,2048]{1,0:T(8,128)(2,1)} fusion(f32[1024,2048]{1,0:T(8,128)} %fusion.69, bf16[1024,1024]{1,0:T(8,128)(2,1)S(1)} %get-tuple-element.97, bf16[2048,1024]{1,0:T(8,128)(2,1)S(1)} %bitcast.314), kind=kOutput, calls=%fused_computation.15 | convolution fusion | flops 4299161600 | bytes 18874368 | tf_op jit(solution)/shard_map/dot_general | solution.py:33
  341.3 7.6 %convolution_convert_fusion.4 = bf16[2048,1024]{1,0:T(8,128)(2,1)S(1)} fusion(bf16[1024,2048]{1,0:T(8,128)(2,1)} %all-gather.6.cloned.1.call-done.x_ref, bf16[1024,1024]{1,0:T(8,128)(2,1)} %copy-done.24), kind=kOutput, calls=%fused_computation.26 | convolution fusion | flops 4297064448 | bytes 10485760 | tf_op jit(solution)/shard_map/dot_general | solution.py:37
  348.9 4.9 convolution_convert_fusion.3
  364.7 25.3 %reduce-scatter.7.cloned.1.call-done = bf16[128,2048]{1,0:T(8,128)(2,1)} async-done(((bf16[1024,2048]{1,0:T(8,128)(2,1)}), bf16[128,2048]{1,0:T(8,128)(2,1)}) %reduce-scatter.7.cloned.1.call-update) | async-done | bytes 524304 | tf_op jit(solution)/shard_map/reduce_scatter | solution.py:296
  391.2 16.9 %collective-permute-done.18 = bf16[2,4,2,64,1024]{4,3,2,1,0:T(8,128)(2,1)} collective-permute-done((bf16[2,4,2,64,1024]{4,3,2,1,0:T(8,128)(2,1)}, bf16[2,4,2,64,1024]{4,3,2,1,0:T(8,128)(2,1)}, u32[]{:S(2)}, u32[]{:S(2)}) %collective-permute-start.18) | collective-permute-done | bytes 2097184 | tf_op jit(solution)/shard_map/ppermute | solution.py:205
  408.1 2.9 collective-permute-done.19
  421.7 19.3 %collective-permute-done.20 = bf16[4,2,64,1024]{3,2,1,0:T(8,128)(2,1)S(1)} collective-permute-done((bf16[4,2,64,1024]{3,2,1,0:T(8,128)(2,1)S(1)}, bf16[4,2,64,1024]{3,2,1,0:T(8,128)(2,1)S(1)}, u32[]{:S(2)}, u32[]{:S(2)}) %collective-permute-start.20) | collective-permute-done | bytes 1048608 | tf_op jit(solution)/shard_map/ppermute | solution.py:205
  441.0 3.7 collective-permute-done.21
  447.5 11.6 %all-gather.10.cloned.1.call-done = bf16[1024,2048]{1,0:T(8,128)(2,1)} async-done(((bf16[128,2048]{1,0:T(8,128)(2,1)}), bf16[1024,2048]{1,0:T(8,128)(2,1)}) %all-gather.10.cloned.1.call-update) | async-done | bytes 4194320 | tf_op jit(solution)/shard_map/all_gather | solution.py:292
  459.1 9.3 %convolution_convert_fusion.2 = bf16[1024,2048]{1,0:T(8,128)(2,1)} fusion(bf16[1024,1024]{1,0:T(8,128)(2,1)} %get-tuple-element.77, bf16[1024,2048]{1,0:T(8,128)(2,1)} %maximum_dynamic-update-slice_fusion.2), kind=kOutput, calls=%fused_computation.24 | convolution fusion | flops 4297064448 | bytes 10485760 | tf_op jit(solution)/shard_map/dot_general | solution.py:29
  468.9 7.7 %convolution_convert_fusion.1 = bf16[1024,2048]{1,0:T(8,128)(2,1)S(1)} fusion(bf16[1024,1024]{1,0:T(8,128)(2,1)} %get-tuple-element.77, bf16[1024,2048]{1,0:T(8,128)(2,1)} %all-gather.8.cloned.1.call-done, f32[1024]{0:T(1024)S(1)} %fusion.60), kind=kOutput, calls=%fused_computation.23 | convolution fusion | flops 4305453056 | bytes 10489856 | tf_op jit(solution)/shard_map/dot_general | solution.py:37
  482.2 3.8 convolution_convert_fusion.7.grad_ref
  486.1 10.9 %shard_map.137 = bf16[1024,384]{1,0:T(8,128)(2,1)S(1)} custom-call(s32[1]{0:T(128)} %copy.143.length_ref, bf16[1024,256]{1,0:T(8,128)(2,1)S(1)} %get-tuple-element.78.q_ref, bf16[1024,128]{1,0:T(8,128)(2,1)S(1)} %get-tuple-element.79.k_ref, bf16[1024,128]{1,0:T(8,128)(2,1)S(1)} %get-tuple-element.80.v_ref, f32[8,1024]{1,0:T(8,128)S(1)} %get-tuple-element.81.lse_ref, ...), custom_call_target="tpu_custom_call" | custom-call | flops 2684354560 | bytes 3145728 | tf_op jit(solution)/shard_map/pallas_call | solution.py:186
  497.0 6.8 collective-permute-done.22
  506.1 2.6 convolution_convert_fusion.5
  511.1 5.9 fusion.3
  517.0 3.5 collective-permute-done.24
  522.3 5.0 collective-permute-done.25
  528.7 3.3 all-to-all-start.9
  533.2 4.6 all-to-all-done.9
  537.9 21.6 %all_to_all.73 = bf16[8,64,384]{2,1,0:T(8,128)(2,1)S(1)} all-to-all(bf16[8,64,384]{2,1,0:T(8,128)(2,1)S(1)} %pad_maximum_fusion.10), channel_id=1, replica_groups=mesh['dp'=4,'seq'=8] {'seq'}, dimensions={0} | all-to-all | bytes 786432 | tf_op jit(solution)/shard_map/all_to_all | solution.py:288
  559.5 3.8 all-to-all-start.7
  563.3 3.5 convolution_convert_fusion.6
  569.1 6.5 collective-permute-done.28
  585.2 35.3 %all-to-all-done.7 = bf16[8,2,64,1024]{3,2,1,0:T(8,128)(2,1)S(1)} async-done(((bf16[8,2,64,1024]{3,2,1,0:T(8,128)(2,1)}), bf16[8,2,64,1024]{3,2,1,0:T(8,128)(2,1)S(1)}, u32[]{:S(2)}, u32[]{:S(2)}) %all-to-all-start.7) | async-done | bytes 2097184 | tf_op jit(solution)/shard_map/all_to_all | solution.py:288
  620.5 3.6 all-to-all-start.6
  632.1 3.6 all-to-all-start.8
  636.7 2.8 convert_element_type.349
  639.6 3.0 convert_element_type.354
  649.9 12.0 %collective-permute-done.34 = f32[2,256]{1,0:T(2,128)S(1)} collective-permute-done((f32[2,256]{1,0:T(2,128)S(1)}, f32[2,256]{1,0:T(2,128)S(1)}, u32[]{:S(2)}, u32[]{:S(2)}) %collective-permute-start.34) | collective-permute-done | bytes 2080 | tf_op jit(solution)/shard_map/ppermute | solution.py:205
  664.2 5.8 collective-permute-done.35
  675.2 2.7 copy.98
  677.9 5.8 copy.121
  687.2 2.4 fusion.29
  (246 shorter events, 131.4 us)
Async XLA Ops:
  7.2 28.5 %copy-start.26 = (bf16[256,4096]{1,0:T(8,128)(2,1)S(1)}, bf16[256,4096]{1,0:T(8,128)(2,1)}, u32[]{:S(2)}) copy-start(bf16[256,4096]{1,0:T(8,128)(2,1)} %param.12) | copy-start | bytes 6291460
  7.2 99.2 %all-gather.12.cloned.1.call-start = ((), (), s32[]{:S(2)}) async-start(), calls=%async_computation.21 | async-start | bytes 4718592 | tf_op jit(solution)/shard_map/all_gather | solution.py:292
  21.5 10.7 %all-to-all-start.3 = ((bf16[8,2,256]{2,1,0:T(2,128)(2,1)}), bf16[8,2,256]{2,1,0:T(2,128)(2,1)S(1)}, u32[]{:S(2)}, u32[]{:S(2)}) async-start(bf16[8,2,256]{2,1,0:T(2,128)(2,1)} %broadcast_in_dim.32), calls=%async_computation.3 | async-start | bytes 16384 | tf_op jit(solution)/shard_map/all_to_all | solution.py:288
  32.2 26.5 %all-to-all-start.2 = ((bf16[8,64,384]{2,1,0:T(8,128)(2,1)}), bf16[8,64,384]{2,1,0:T(8,128)(2,1)S(1)}, u32[]{:S(2)}, u32[]{:S(2)}) async-start(bf16[8,64,384]{2,1,0:T(8,128)(2,1)} %copy.84), calls=%async_computation.2 | async-start | bytes 786432 | tf_op jit(solution)/shard_map/all_to_all | solution.py:288
  58.7 47.7 %all-to-all-start = ((bf16[4,4,64,1024]{3,1,2,0:T(4,128)(2,1)}), bf16[4,4,64,1024]{3,1,2,0:T(4,128)(2,1)S(1)}, u32[]{:S(2)}, u32[]{:S(2)}) async-start(bf16[4,4,64,1024]{3,1,2,0:T(4,128)(2,1)} %bitcast.305), calls=%async_computation | async-start | bytes 4194304 | tf_op jit(solution)/shard_map/all_to_all | solution.py:288
  62.3 34.7 %collective-permute-start = (bf16[8,1,64,384]{3,2,1,0:T(8,128)(2,1)S(1)}, bf16[8,1,64,384]{3,2,1,0:T(8,128)(2,1)S(1)}, u32[]{:S(2)}, u32[]{:S(2)}) collective-permute-start(bf16[8,1,64,384]{3,2,1,0:T(8,128)(2,1)S(1)} %bitcast.327), channel_id=1, source_target_pairs={{0,8},{8,0},{16,24},{24,16},{1,9},{9,1},{17,25},{25,17},{2,10},{10... | collective-permute-start | bytes 1179656 | tf_op jit(solution)/shard_map/ppermute | solution.py:205
  64.3 33.5 %collective-permute-start.1 = (bf16[8,1,64,384]{3,2,1,0:T(8,128)(2,1)S(1)}, bf16[8,1,64,384]{3,2,1,0:T(8,128)(2,1)S(1)}, u32[]{:S(2)}, u32[]{:S(2)}) collective-permute-start(bf16[8,1,64,384]{3,2,1,0:T(8,128)(2,1)S(1)} %bitcast.328), channel_id=1, source_target_pairs={{0,16},{8,24},{16,0},{24,8},{1,17},{9,25},{17,1},{25,9},{2,18},{10... | collective-permute-start | bytes 1179656 | tf_op jit(solution)/shard_map/ppermute | solution.py:205
  65.8 39.8 %collective-permute-start.2 = (bf16[8,1,64,384]{3,2,1,0:T(8,128)(2,1)S(1)}, bf16[8,1,64,384]{3,2,1,0:T(8,128)(2,1)S(1)}, u32[]{:S(2)}, u32[]{:S(2)}) collective-permute-start(bf16[8,1,64,384]{3,2,1,0:T(8,128)(2,1)S(1)} %bitcast.329), channel_id=1, source_target_pairs={{0,24},{8,16},{16,8},{24,0},{1,25},{9,17},{17,9},{25,1},{2,26},{10... | collective-permute-start | bytes 1179656 | tf_op jit(solution)/shard_map/ppermute | solution.py:205
  108.5 20.5 %copy-start.15 = (bf16[1024,512]{1,0:T(8,128)(2,1)S(1)}, bf16[1024,512]{1,0:T(8,128)(2,1)}, u32[]{:S(2)}) copy-start(bf16[1024,512]{1,0:T(8,128)(2,1)} %param.13) | copy-start | bytes 3145732
  108.5 53.5 %all-to-all-start.4 = ((bf16[8,2,64,1024]{3,2,1,0:T(8,128)(2,1)}), bf16[8,2,64,1024]{3,2,1,0:T(8,128)(2,1)}, u32[]{:S(2)}, u32[]{:S(2)}) async-start(bf16[8,2,64,1024]{3,2,1,0:T(8,128)(2,1)} %copy_bitcast_fusion.4), calls=%async_computation.4 | async-start | bytes 4194304 | tf_op jit(solution)/shard_map/all_to_all | solution.py:288
  113.0 101.8 %reduce-scatter.5.cloned.1.call-start = ((), (), s32[]{:S(2)}) async-start(), calls=%async_computation.14 | async-start | bytes 4718592 | tf_op jit(solution)/shard_map/reduce_scatter | solution.py:296
  113.1 9.2 %collective-permute-start.7 = (bf16[256,512]{1,0:T(8,128)(2,1)S(1)}, bf16[256,512]{1,0:T(8,128)(2,1)S(1)}, u32[]{:S(2)}, u32[]{:S(2)}) collective-permute-start(bf16[256,512]{1,0:T(8,128)(2,1)S(1)} %copy-done.29), channel_id=1, source_target_pairs={{0,8},{8,0},{16,24},{24,16},{1,9},{9,1},{17,25},{25,17},{2,10},{10... | collective-permute-start | bytes 786440 | tf_op jit(solution)/shard_map/ppermute | solution.py:205
  113.7 13.9 %collective-permute-start.8 = (bf16[256,512]{1,0:T(8,128)(2,1)S(1)}, bf16[256,512]{1,0:T(8,128)(2,1)S(1)}, u32[]{:S(2)}, u32[]{:S(2)}) collective-permute-start(bf16[256,512]{1,0:T(8,128)(2,1)S(1)} %copy-done.29), channel_id=1, source_target_pairs={{0,16},{8,24},{16,0},{24,8},{1,17},{9,25},{17,1},{25,9},{2,18},{10... | collective-permute-start | bytes 786440 | tf_op jit(solution)/shard_map/ppermute | solution.py:205
  115.0 13.3 %collective-permute-start.9 = (bf16[256,512]{1,0:T(8,128)(2,1)S(1)}, bf16[256,512]{1,0:T(8,128)(2,1)S(1)}, u32[]{:S(2)}, u32[]{:S(2)}) collective-permute-start(bf16[256,512]{1,0:T(8,128)(2,1)S(1)} %copy-done.29), channel_id=1, source_target_pairs={{0,24},{8,16},{16,8},{24,0},{1,25},{9,17},{17,9},{25,1},{2,26},{10... | collective-permute-start | bytes 786440 | tf_op jit(solution)/shard_map/ppermute | solution.py:205
  121.8 14.5 %copy-start.13 = (bf16[1,1024,2048]{2,1,0:T(8,128)(2,1)S(1)}, bf16[1,1024,2048]{2,1,0:T(8,128)(2,1)}, u32[]{:S(2)}) copy-start(bf16[1,1024,2048]{2,1,0:T(8,128)(2,1)} %all-gather.12.cloned.1.call-done) | copy-start | bytes 12582916
  129.1 20.6 %collective-permute-start.3 = (bf16[512,512]{1,0:T(8,128)(2,1)S(1)}, bf16[512,512]{1,0:T(8,128)(2,1)}, u32[]{:S(2)}, u32[]{:S(2)}) collective-permute-start(bf16[512,512]{1,0:T(8,128)(2,1)S(1)} %get-tuple-element.131), channel_id=1, source_target_pairs={{0,8},{8,0},{16,24},{24,16},{1,9},{9,1},{17,25},{25,17},{2,10},{10... | collective-permute-start | bytes 1572872 | tf_op jit(solution)/shard_map/ppermute | solution.py:205
  130.7 22.2 %collective-permute-start.5 = (bf16[512,512]{1,0:T(8,128)(2,1)S(1)}, bf16[512,512]{1,0:T(8,128)(2,1)}, u32[]{:S(2)}, u32[]{:S(2)}) collective-permute-start(bf16[512,512]{1,0:T(8,128)(2,1)S(1)} %get-tuple-element.131), channel_id=1, source_target_pairs={{0,16},{8,24},{16,0},{24,8},{1,17},{9,25},{17,1},{25,9},{2,18},{10... | collective-permute-start | bytes 1572872 | tf_op jit(solution)/shard_map/ppermute | solution.py:205
  131.2 21.6 %collective-permute-start.4 = (bf16[512,512]{1,0:T(8,128)(2,1)S(1)}, bf16[512,512]{1,0:T(8,128)(2,1)}, u32[]{:S(2)}, u32[]{:S(2)}) collective-permute-start(bf16[512,512]{1,0:T(8,128)(2,1)S(1)} %get-tuple-element.130), channel_id=1, source_target_pairs={{0,8},{8,0},{16,24},{24,16},{1,9},{9,1},{17,25},{25,17},{2,10},{10... | collective-permute-start | bytes 1572872 | tf_op jit(solution)/shard_map/ppermute | solution.py:205
  132.5 21.4 %collective-permute-start.6 = (bf16[512,512]{1,0:T(8,128)(2,1)S(1)}, bf16[512,512]{1,0:T(8,128)(2,1)}, u32[]{:S(2)}, u32[]{:S(2)}) collective-permute-start(bf16[512,512]{1,0:T(8,128)(2,1)S(1)} %get-tuple-element.130), channel_id=1, source_target_pairs={{0,16},{8,24},{16,0},{24,8},{1,17},{9,25},{17,1},{25,9},{2,18},{10... | collective-permute-start | bytes 1572872 | tf_op jit(solution)/shard_map/ppermute | solution.py:205
  167.0 52.1 %copy-start.4 = (bf16[1,128,2048]{2,1,0:T(8,128)(2,1)S(1)}, bf16[1,128,2048]{2,1,0:T(8,128)(2,1)}, u32[]{:S(2)}) copy-start(bf16[1,128,2048]{2,1,0:T(8,128)(2,1)} %param.8) | copy-start | bytes 1572868
  167.0 100.2 %all-gather.6.cloned.1.call-start = ((), (), s32[]{:S(2)}) async-start(), calls=%async_computation.15 | async-start | bytes 4718592 | tf_op jit(solution)/shard_map/all_gather | solution.py:292
  170.3 45.7 %collective-permute-start.10 = (bf16[4,2,64,1024]{3,2,1,0:T(8,128)(2,1)}, bf16[4,2,64,1024]{3,2,1,0:T(8,128)(2,1)}, u32[]{:S(2)}, u32[]{:S(2)}) collective-permute-start(bf16[4,2,64,1024]{3,2,1,0:T(8,128)(2,1)} %get-tuple-element.117), channel_id=1, source_target_pairs={{0,8},{8,0},{16,24},{24,16},{1,9},{9,1},{17,25},{25,17},{2,10},{10... | collective-permute-start | bytes 3145736 | tf_op jit(solution)/shard_map/ppermute | solution.py:205
  170.8 46.9 %collective-permute-start.11 = (bf16[4,2,64,1024]{3,2,1,0:T(8,128)(2,1)}, bf16[4,2,64,1024]{3,2,1,0:T(8,128)(2,1)}, u32[]{:S(2)}, u32[]{:S(2)}) collective-permute-start(bf16[4,2,64,1024]{3,2,1,0:T(8,128)(2,1)} %get-tuple-element.116), channel_id=1, source_target_pairs={{0,8},{8,0},{16,24},{24,16},{1,9},{9,1},{17,25},{25,17},{2,10},{10... | collective-permute-start | bytes 3145736 | tf_op jit(solution)/shard_map/ppermute | solution.py:205
  172.3 45.4 %collective-permute-start.12 = (bf16[4,2,64,1024]{3,2,1,0:T(8,128)(2,1)}, bf16[4,2,64,1024]{3,2,1,0:T(8,128)(2,1)}, u32[]{:S(2)}, u32[]{:S(2)}) collective-permute-start(bf16[4,2,64,1024]{3,2,1,0:T(8,128)(2,1)} %get-tuple-element.117), channel_id=1, source_target_pairs={{0,16},{8,24},{16,0},{24,8},{1,17},{9,25},{17,1},{25,9},{2,18},{10... | collective-permute-start | bytes 3145736 | tf_op jit(solution)/shard_map/ppermute | solution.py:205
  172.8 46.3 %collective-permute-start.13 = (bf16[4,2,64,1024]{3,2,1,0:T(8,128)(2,1)}, bf16[4,2,64,1024]{3,2,1,0:T(8,128)(2,1)}, u32[]{:S(2)}, u32[]{:S(2)}) collective-permute-start(bf16[4,2,64,1024]{3,2,1,0:T(8,128)(2,1)} %get-tuple-element.116), channel_id=1, source_target_pairs={{0,16},{8,24},{16,0},{24,8},{1,17},{9,25},{17,1},{25,9},{2,18},{10... | collective-permute-start | bytes 3145736 | tf_op jit(solution)/shard_map/ppermute | solution.py:205
  222.0 92.5 %all-gather.8.cloned.1.call-start = ((), (), s32[]{:S(2)}) async-start(), calls=%async_computation.16 | async-start | bytes 4718592 | tf_op jit(solution)/shard_map/all_gather | solution.py:292
  222.0 23.6 %collective-permute-start.14 = (bf16[4,2,64,1024]{3,2,1,0:T(8,128)(2,1)}, bf16[4,2,64,1024]{3,2,1,0:T(8,128)(2,1)}, u32[]{:S(2)}, u32[]{:S(2)}) collective-permute-start(bf16[4,2,64,1024]{3,2,1,0:T(8,128)(2,1)} %collective-permute-done.10.refs_1_), channel_id=1, source_target_pairs={{0,16},{8,24},{16,0},{24,8},{1,17},{9,25},{17,1},{25,9},{2,18},{10... | collective-permute-start | bytes 3145736 | tf_op jit(solution)/shard_map/ppermute | solution.py:205
  222.6 23.2 %collective-permute-start.15 = (bf16[4,2,64,1024]{3,2,1,0:T(8,128)(2,1)}, bf16[4,2,64,1024]{3,2,1,0:T(8,128)(2,1)}, u32[]{:S(2)}, u32[]{:S(2)}) collective-permute-start(bf16[4,2,64,1024]{3,2,1,0:T(8,128)(2,1)} %collective-permute-done.13.refs_4_), channel_id=1, source_target_pairs={{0,8},{8,0},{16,24},{24,16},{1,9},{9,1},{17,25},{25,17},{2,10},{10... | collective-permute-start | bytes 3145736 | tf_op jit(solution)/shard_map/ppermute | solution.py:205
  267.3 122.7 %reduce-scatter.7.cloned.1.call-start = ((), (), s32[]{:S(2)}) async-start(), calls=%async_computation.17 | async-start | bytes 4718592 | tf_op jit(solution)/shard_map/reduce_scatter | solution.py:296
  267.3 14.3 %collective-permute-start.17 = (bf16[512,512]{1,0:T(8,128)(2,1)}, bf16[512,512]{1,0:T(8,128)(2,1)S(1)}, u32[]{:S(2)}, u32[]{:S(2)}) collective-permute-start(bf16[512,512]{1,0:T(8,128)(2,1)} %collective-permute-done.6), channel_id=1, source_target_pairs={{0,8},{8,0},{16,24},{24,16},{1,9},{9,1},{17,25},{25,17},{2,10},{10... | collective-permute-start | bytes 1572872 | tf_op jit(solution)/shard_map/ppermute | solution.py:205
  268.9 14.0 %collective-permute-start.16 = (bf16[512,512]{1,0:T(8,128)(2,1)}, bf16[512,512]{1,0:T(8,128)(2,1)S(1)}, u32[]{:S(2)}, u32[]{:S(2)}) collective-permute-start(bf16[512,512]{1,0:T(8,128)(2,1)} %collective-permute-done.3), channel_id=1, source_target_pairs={{0,16},{8,24},{16,0},{24,8},{1,17},{9,25},{17,1},{25,9},{2,18},{10... | collective-permute-start | bytes 1572872 | tf_op jit(solution)/shard_map/ppermute | solution.py:205
  341.1 118.0 %all-gather.10.cloned.1.call-start = ((), (), s32[]{:S(2)}) async-start(), calls=%async_computation.18 | async-start | bytes 4718592 | tf_op jit(solution)/shard_map/all_gather | solution.py:292
  360.0 48.1 %collective-permute-start.18 = (bf16[2,4,2,64,1024]{4,3,2,1,0:T(8,128)(2,1)}, bf16[2,4,2,64,1024]{4,3,2,1,0:T(8,128)(2,1)}, u32[]{:S(2)}, u32[]{:S(2)}) collective-permute-start(bf16[2,4,2,64,1024]{4,3,2,1,0:T(8,128)(2,1)} %pad_maximum_fusion), channel_id=1, source_target_pairs={{0,8},{8,0},{16,24},{24,16},{1,9},{9,1},{17,25},{25,17},{2,10},{10... | collective-permute-start | bytes 6291464 | tf_op jit(solution)/shard_map/ppermute | solution.py:205
  361.6 51.0 %copy-start.25 = (bf16[1,128,2048]{2,1,0:T(8,128)(2,1)S(1)}, bf16[1,128,2048]{2,1,0:T(8,128)(2,1)}, u32[]{:S(2)}) copy-start(bf16[1,128,2048]{2,1,0:T(8,128)(2,1)} %param.15) | copy-start | bytes 1572868
  363.2 47.8 %collective-permute-start.19 = (bf16[2,4,2,64,1024]{4,3,2,1,0:T(8,128)(2,1)}, bf16[2,4,2,64,1024]{4,3,2,1,0:T(8,128)(2,1)}, u32[]{:S(2)}, u32[]{:S(2)}) collective-permute-start(bf16[2,4,2,64,1024]{4,3,2,1,0:T(8,128)(2,1)} %pad_maximum_fusion.1), channel_id=1, source_target_pairs={{0,16},{8,24},{16,0},{24,8},{1,17},{9,25},{17,1},{25,9},{2,18},{10... | collective-permute-start | bytes 6291464 | tf_op jit(solution)/shard_map/ppermute | solution.py:205
  390.0 22.6 %copy-start.1 = (f32[128,2048]{1,0:T(8,128)S(1)}, f32[128,2048]{1,0:T(8,128)}, u32[]{:S(2)}) copy-start(f32[128,2048]{1,0:T(8,128)} %copy-done) | copy-start | bytes 3145732
  414.2 269.6 %reduce-scatter.9.cloned.1.call-start = ((), (), s32[]{:S(2)}) async-start(), calls=%async_computation.19 | async-start | bytes 4718592 | tf_op jit(solution)/shard_map/reduce_scatter | solution.py:296
  416.8 24.2 %collective-permute-start.20 = (bf16[4,2,64,1024]{3,2,1,0:T(8,128)(2,1)S(1)}, bf16[4,2,64,1024]{3,2,1,0:T(8,128)(2,1)S(1)}, u32[]{:S(2)}, u32[]{:S(2)}) collective-permute-start(bf16[4,2,64,1024]{3,2,1,0:T(8,128)(2,1)S(1)} %fusion.15), channel_id=1, source_target_pairs={{0,16},{8,24},{16,0},{24,8},{1,17},{9,25},{17,1},{25,9},{2,18},{10... | collective-permute-start | bytes 3145736 | tf_op jit(solution)/shard_map/ppermute | solution.py:205
  420.9 23.8 %collective-permute-start.21 = (bf16[4,2,64,1024]{3,2,1,0:T(8,128)(2,1)S(1)}, bf16[4,2,64,1024]{3,2,1,0:T(8,128)(2,1)S(1)}, u32[]{:S(2)}, u32[]{:S(2)}) collective-permute-start(bf16[4,2,64,1024]{3,2,1,0:T(8,128)(2,1)S(1)} %fusion.10), channel_id=1, source_target_pairs={{0,8},{8,0},{16,24},{24,16},{1,9},{9,1},{17,25},{25,17},{2,10},{10... | collective-permute-start | bytes 3145736 | tf_op jit(solution)/shard_map/ppermute | solution.py:205
  468.4 217.3 %reduce-scatter.11.cloned.1.call-start = ((), (), s32[]{:S(2)}) async-start(), calls=%async_computation.20 | async-start | bytes 4718592 | tf_op jit(solution)/shard_map/reduce_scatter | solution.py:296
  478.2 25.6 %collective-permute-start.22 = (bf16[2,512,512]{2,1,0:T(8,128)(2,1)}, bf16[2,512,512]{2,1,0:T(8,128)(2,1)}, u32[]{:S(2)}, u32[]{:S(2)}) collective-permute-start(bf16[2,512,512]{2,1,0:T(8,128)(2,1)} %pad_maximum_fusion.4), channel_id=1, source_target_pairs={{0,8},{8,0},{16,24},{24,16},{1,9},{9,1},{17,25},{25,17},{2,10},{10... | collective-permute-start | bytes 3145736 | tf_op jit(solution)/shard_map/ppermute | solution.py:205
  480.7 25.4 %collective-permute-start.23 = (bf16[2,512,512]{2,1,0:T(8,128)(2,1)}, bf16[2,512,512]{2,1,0:T(8,128)(2,1)}, u32[]{:S(2)}, u32[]{:S(2)}) collective-permute-start(bf16[2,512,512]{2,1,0:T(8,128)(2,1)} %pad_maximum_fusion.5), channel_id=1, source_target_pairs={{0,16},{8,24},{16,0},{24,8},{1,17},{9,25},{17,1},{25,9},{2,18},{10... | collective-permute-start | bytes 3145736 | tf_op jit(solution)/shard_map/ppermute | solution.py:205
  486.0 20.0 %copy-start.14 = (bf16[1,1024,2048]{2,1,0:T(8,128)(2,1)S(1)}, bf16[1,1024,2048]{2,1,0:T(8,128)(2,1)}, u32[]{:S(2)}) copy-start(bf16[1,1024,2048]{2,1,0:T(8,128)(2,1)} %all-gather.12.cloned.1.call-done) | copy-start | bytes 12582916
  508.9 13.3 %collective-permute-start.26 = (bf16[2,4,64,384]{3,2,1,0:T(8,128)(2,1)S(1)}, bf16[2,4,64,384]{3,2,1,0:T(8,128)(2,1)S(1)}, u32[]{:S(2)}, u32[]{:S(2)}) collective-permute-start(bf16[2,4,64,384]{3,2,1,0:T(8,128)(2,1)S(1)} %pad_maximum_fusion.9), channel_id=1, source_target_pairs={{0,16},{8,24},{16,0},{24,8},{1,17},{9,25},{17,1},{25,9},{2,18},{10... | collective-permute-start | bytes 1179656 | tf_op jit(solution)/shard_map/ppermute | solution.py:205
  510.4 10.0 %collective-permute-start.24 = (bf16[2,4,64,384]{3,2,1,0:T(8,128)(2,1)S(1)}, bf16[2,4,64,384]{3,2,1,0:T(8,128)(2,1)}, u32[]{:S(2)}, u32[]{:S(2)}) collective-permute-start(bf16[2,4,64,384]{3,2,1,0:T(8,128)(2,1)S(1)} %pad_maximum_fusion.8), channel_id=1, source_target_pairs={{0,8},{8,0},{16,24},{24,16},{1,9},{9,1},{17,25},{25,17},{2,10},{10... | collective-permute-start | bytes 1179656 | tf_op jit(solution)/shard_map/ppermute | solution.py:205
  521.5 5.7 collective-permute-start.25
  527.4 5.7 collective-permute-start.27
  528.7 9.2 %all-to-all-start.9 = ((f32[8,256,2]{1,2,0:T(2,128)}), f32[8,256,2]{1,2,0:T(2,128)S(1)}, u32[]{:S(2)}, u32[]{:S(2)}) async-start(f32[8,256,2]{1,2,0:T(2,128)} %copy.99), calls=%async_computation.13 | async-start | bytes 32768 | tf_op jit(solution)/shard_map/all_to_all | solution.py:288
  537.9 28.9 %copy-start.30 = (f32[8,256,2]{1,2,0:T(2,128)}, f32[8,256,2]{1,2,0:T(2,128)S(1)}, u32[]{:S(2)}) copy-start(f32[8,256,2]{1,2,0:T(2,128)S(1)} %all-to-all-done.9) | copy-start | bytes 49156
  559.5 61.0 %all-to-all-start.7 = ((bf16[8,2,64,1024]{3,2,1,0:T(8,128)(2,1)}), bf16[8,2,64,1024]{3,2,1,0:T(8,128)(2,1)S(1)}, u32[]{:S(2)}, u32[]{:S(2)}) async-start(bf16[8,2,64,1024]{3,2,1,0:T(8,128)(2,1)} %pad_maximum_fusion.2), calls=%async_computation.11 | async-start | bytes 4194304 | tf_op jit(solution)/shard_map/all_to_all | solution.py:288
  566.8 10.1 %copy-start.27 = (bf16[256,2048]{1,0:T(8,128)(2,1)}, bf16[256,2048]{1,0:T(8,128)(2,1)S(1)}, u32[]{:S(2)}) copy-start(bf16[256,2048]{1,0:T(8,128)(2,1)S(1)} %convolution_convert_fusion.6) | copy-start | bytes 3145732
  566.9 8.7 %collective-permute-start.28 = (bf16[2,128,512]{2,1,0:T(8,128)(2,1)S(1)}, bf16[2,128,512]{2,1,0:T(8,128)(2,1)S(1)}, u32[]{:S(2)}, u32[]{:S(2)}) collective-permute-start(bf16[2,128,512]{2,1,0:T(8,128)(2,1)S(1)} %pad_maximum_fusion.12), channel_id=1, source_target_pairs={{0,8},{8,0},{16,24},{24,16},{1,9},{9,1},{17,25},{25,17},{2,10},{10... | collective-permute-start | bytes 786440 | tf_op jit(solution)/shard_map/ppermute | solution.py:205
  568.5 8.5 %collective-permute-start.30 = (bf16[2,128,512]{2,1,0:T(8,128)(2,1)S(1)}, bf16[2,128,512]{2,1,0:T(8,128)(2,1)S(1)}, u32[]{:S(2)}, u32[]{:S(2)}) collective-permute-start(bf16[2,128,512]{2,1,0:T(8,128)(2,1)S(1)} %pad_maximum_fusion.13), channel_id=1, source_target_pairs={{0,16},{8,24},{16,0},{24,8},{1,17},{9,25},{17,1},{25,9},{2,18},{10... | collective-permute-start | bytes 786440 | tf_op jit(solution)/shard_map/ppermute | solution.py:205
  576.4 47.7 %collective-permute-start.29 = (bf16[128,512]{1,0:T(8,128)(2,1)}, bf16[128,512]{1,0:T(8,128)(2,1)}, u32[]{:S(2)}, u32[]{:S(2)}) collective-permute-start(bf16[128,512]{1,0:T(8,128)(2,1)} %fusion.57), channel_id=1, source_target_pairs={{0,16},{8,24},{16,0},{24,8},{1,17},{9,25},{17,1},{25,9},{2,18},{10... | collective-permute-start | bytes 393224 | tf_op jit(solution)/shard_map/ppermute | solution.py:205
  620.5 11.6 %all-to-all-start.6 = ((bf16[64,4,768]{2,0,1:T(8,128)(2,1)}), bf16[64,4,768]{2,0,1:T(8,128)(2,1)S(1)}, u32[]{:S(2)}, u32[]{:S(2)}) async-start(bf16[64,4,768]{2,0,1:T(8,128)(2,1)} %bitcast.295), calls=%async_computation.10 | async-start | bytes 786432 | tf_op jit(solution)/shard_map/all_to_all | solution.py:490
  626.0 9.7 %collective-permute-start.31 = (bf16[128,512]{1,0:T(8,128)(2,1)}, bf16[128,512]{1,0:T(8,128)(2,1)}, u32[]{:S(2)}, u32[]{:S(2)}) collective-permute-start(bf16[128,512]{1,0:T(8,128)(2,1)} %get-tuple-element.125), channel_id=1, source_target_pairs={{0,8},{8,0},{16,24},{24,16},{1,9},{9,1},{17,25},{25,17},{2,10},{10... | collective-permute-start | bytes 393224 | tf_op jit(solution)/shard_map/ppermute | solution.py:205
  632.1 42.6 %all-to-all-start.8 = ((bf16[4,4,64,1024]{3,2,1,0:T(8,128)(2,1)}), bf16[4,4,64,1024]{3,2,1,0:T(8,128)(2,1)S(1)}, u32[]{:S(2)}, u32[]{:S(2)}) async-start(bf16[4,4,64,1024]{3,2,1,0:T(8,128)(2,1)} %bitcast.302), calls=%async_computation.12 | async-start | bytes 4194304 | tf_op jit(solution)/shard_map/all_to_all | solution.py:288
  639.6 23.9 %copy-start.28 = (f32[128,512]{1,0:T(8,128)S(1)}, f32[128,512]{1,0:T(8,128)}, u32[]{:S(2)}) copy-start(f32[128,512]{1,0:T(8,128)} %get-tuple-element.124) | copy-start | bytes 786436
  643.3 27.4 %copy-start.8 = (f32[2,512,512]{2,1,0:T(8,128)S(1)}, f32[2,512,512]{2,1,0:T(8,128)}, u32[]{:S(2)}) copy-start(f32[2,512,512]{2,1,0:T(8,128)} %convert_element_type.349) | copy-start | bytes 6291460
  643.3 27.4 %copy-start.9 = (f32[2,512,512]{2,1,0:T(8,128)S(1)}, f32[2,512,512]{2,1,0:T(8,128)}, u32[]{:S(2)}) copy-start(f32[2,512,512]{2,1,0:T(8,128)} %convert_element_type.354) | copy-start | bytes 6291460
  643.3 18.7 %collective-permute-start.34 = (f32[2,256]{1,0:T(2,128)S(1)}, f32[2,256]{1,0:T(2,128)S(1)}, u32[]{:S(2)}, u32[]{:S(2)}) collective-permute-start(f32[2,256]{1,0:T(2,128)S(1)} %bitcast.343), channel_id=1, source_target_pairs={{0,8},{8,0},{16,24},{24,16},{1,9},{9,1},{17,25},{25,17},{2,10},{10... | collective-permute-start | bytes 6152 | tf_op jit(solution)/shard_map/ppermute | solution.py:205
  647.5 23.1 %collective-permute-start.32 = (bf16[512,512]{1,0:T(8,128)(2,1)S(1)}, bf16[512,512]{1,0:T(8,128)(2,1)S(1)}, u32[]{:S(2)}, u32[]{:S(2)}) collective-permute-start(bf16[512,512]{1,0:T(8,128)(2,1)S(1)} %get-tuple-element.106), channel_id=1, source_target_pairs={{0,16},{8,24},{16,0},{24,8},{1,17},{9,25},{17,1},{25,9},{2,18},{10... | collective-permute-start | bytes 1572872 | tf_op jit(solution)/shard_map/ppermute | solution.py:205
  649.1 21.6 %collective-permute-start.33 = (bf16[512,512]{1,0:T(8,128)(2,1)S(1)}, bf16[512,512]{1,0:T(8,128)(2,1)S(1)}, u32[]{:S(2)}, u32[]{:S(2)}) collective-permute-start(bf16[512,512]{1,0:T(8,128)(2,1)S(1)} %get-tuple-element.107), channel_id=1, source_target_pairs={{0,8},{8,0},{16,24},{24,16},{1,9},{9,1},{17,25},{25,17},{2,10},{10... | collective-permute-start | bytes 1572872 | tf_op jit(solution)/shard_map/ppermute | solution.py:205
  661.9 8.1 %collective-permute-start.35 = (f32[2,256]{1,0:T(2,128)S(1)}, f32[2,256]{1,0:T(2,128)S(1)}, u32[]{:S(2)}, u32[]{:S(2)}) collective-permute-start(f32[2,256]{1,0:T(2,128)S(1)} %bitcast_add_fusion), channel_id=1, source_target_pairs={{0,16},{8,24},{16,0},{24,8},{1,17},{9,25},{17,1},{25,9},{2,18},{10... | collective-permute-start | bytes 6152 | tf_op jit(solution)/shard_map/ppermute | solution.py:205
  (20 other events, 109.9 us)
Sparse Core Ops, SparseCore 0:
  9.6 58.1 all-gather.11
  167.2 47.6 reduce-scatter.4
  222.1 45.1 all-gather.5
  268.7 45.6 all-gather.7
  341.2 48.7 reduce-scatter.6
  414.3 44.7 all-gather.9
  468.6 48.7 reduce-scatter.8
  519.6 59.9 reduce-scatter.10

commit v2 on v1

--- a/solution.py
+++ b/solution.py
@@ -205,24 +205,24 @@
     return lax.ppermute(value, "dp", flip(mask, lax.axis_size("dp")))
 
 
-def gather_near(shard):
+def other(first):
+    return 3 - first
+
+
+def gather_near(shard, first):
     if lax.axis_size("dp") != 4:
         return None
-    half = shard.shape[0] // 2
-    top, low = shard[:half], shard[half:]
-    return (send(top, 1), send(low, 1), send(top, 2), send(low, 2))
-
-
-def gather_far(near):
-    if near is None:
-        return None
-    return (send(near[0], 2), send(near[3], 1))
-
-
-def place(pieces, axis):
+    return (send(shard, first), send(shard, other(first)))
+
+
+def gather_far(near, first):
+    return None if near is None else send(near[0], other(first))
+
+
+def place(pieces, masks, axis):
     me = lax.axis_index("dp")
     whole = None
-    for mask, piece in enumerate(pieces):
+    for mask, piece in zip(masks, pieces):
         size = piece.shape[axis]
         if whole is None:
             shape = list(piece.shape)
@@ -232,19 +232,10 @@
     return whole
 
 
-def gathered(shard, near, far, axis):
-    if near is None:
+def gather_direct(shard, axis):
+    if lax.axis_size("dp") != 4:
         return lax.all_gather(shard, "dp", axis=axis, tiled=True)
-    pieces = (shard,) + tuple(
-        jnp.concatenate(pair, axis=0) for pair in (near[:2], near[2:], far)
-    )
-    return place(pieces, axis)
-
-
-def gather_direct(shard, axis):
-    if lax.axis_size("dp") != 4:
-        return lax.all_gather(shard, "dp", axis=axis, tiled=True)
-    return place((shard, send(shard, 1), send(shard, 2), send(shard, 3)), axis)
+    return place((shard, send(shard, 1), send(shard, 2), send(shard, 3)), range(4), axis)
 
 
 def dp_block(partial, mask, axis):
@@ -255,33 +246,55 @@
     return lax.dynamic_index_in_dim(partial, place, axis, keepdims=False)
 
 
-def scatter_first(partial, axis):
+def gather_halves(shard, near):
+    if lax.axis_size("dp") != 4:
+        return None
+    half = shard.shape[0] // 2
+    if near is None:
+        return tuple(send(part, mask) for mask in (1, 2) for part in (shard[:half], shard[half:]))
+    return (send(near[0], 2), send(near[3], 1))
+
+
+def join_halves(shard, near, far, axis):
+    if near is None:
+        return lax.all_gather(shard, "dp", axis=axis, tiled=True)
+    pieces = (shard,) + tuple(
+        jnp.concatenate(pair, axis=0) for pair in (near[:2], near[2:], far)
+    )
+    return place(pieces, range(4), axis)
+
+
+def scatter_first(partial, axis, first):
     if lax.axis_size("dp") != 4:
         return lax.psum_scatter(
             partial.astype(BF16), "dp", scatter_dimension=axis, tiled=partial.ndim == 2
         )
-    half = (partial.shape[0] if axis else partial.shape[1]) // 2
-    beside, across, far = (dp_block(partial, mask, axis) for mask in (1, 2, 3))
-    top = jnp.stack([beside[:half], far[:half]]).astype(BF16)
-    low = jnp.stack([across[half:], far[half:]]).astype(BF16)
-    return (send(top, 1), send(low, 2))
-
-
-def scatter_second(partial, got, axis):
+    return send(dp_block(partial, 3, axis).astype(BF16), first)
+
+
+def scatter_second(partial, got, axis, first):
     if lax.axis_size("dp") != 4:
         return got.astype(F32)
-    half = (partial.shape[0] if axis else partial.shape[1]) // 2
-    own, beside, across = (dp_block(partial, mask, axis) for mask in (0, 1, 2))
-    top, low = (part.astype(F32) for part in got)
-    third = send((across[:half].astype(F32) + top[1]).astype(BF16), 2)
-    fourth = send((beside[half:].astype(F32) + low[1]).astype(BF16), 1)
-    return jnp.concatenate(
-        [
-            own[:half].astype(F32) + top[0] + third.astype(F32),
-            own[half:].astype(F32) + low[0] + fourth.astype(F32),
-        ],
-        axis=0,
-    )
+    beside = send(dp_block(partial, first, axis).astype(BF16), first)
+    passed = dp_block(partial, other(first), axis).astype(F32) + got.astype(F32)
+    last = send(passed.astype(BF16), other(first))
+    own = dp_block(partial, 0, axis).astype(F32)
+    return own + beside.astype(F32) + last.astype(F32)
+
+
+def scatter_direct(partial, axis):
+    if lax.axis_size("dp") != 4:
+        return scatter_second(partial, scatter_first(partial, axis, 1), axis, 1)
+    own = dp_block(partial, 0, axis).astype(F32)
+    parts = [send(dp_block(partial, mask, axis).astype(BF16), mask) for mask in (1, 2, 3)]
+    return own + parts[0].astype(F32) + parts[1].astype(F32) + parts[2].astype(F32)
+
+
+def swap_dp(blocks):
+    if lax.axis_size("dp") != 4:
+        return exchange(blocks, "dp")
+    parts = [dp_block(blocks, 0, 0)] + [send(dp_block(blocks, mask, 0), mask) for mask in (1, 2, 3)]
+    return place([part[None] for part in parts], range(4), 0)
 
 
 def exchange(blocks, axis_name):
@@ -299,21 +312,15 @@
 
 
 def gate_up_kernel(me_ref, x_ref, *refs):
-    pieces, (gate_ref, up_ref, whole_out, whole, sems, out_sem) = refs[:7], refs[7:]
+    pieces, (gate_ref, up_ref, whole_out, whole, sems, out_sem) = refs[:8], refs[8:]
     me = me_ref[0]
-    seqs, _, sub, ff = pieces[0].shape
-    half = seqs // 2
-    places = [(0, 0, seqs)] + [(mask, part * half, half) for mask in (1, 2, 3) for part in (0, 1)]
+    sub, ff = pieces[0].shape[1:]
     copies = []
-    for index, (piece, (mask, first, count)) in enumerate(zip(pieces, places)):
-        for part in range(2):
-            copies.append(
-                pltpu.make_async_copy(
-                    piece.at[:, part],
-                    whole.at[part, pl.ds(first, count), me ^ mask],
-                    sems.at[index, part],
-                )
-            )
+    for index, piece in enumerate(pieces):
+        part, mask = divmod(index, 4)
+        copies.append(
+            pltpu.make_async_copy(piece, whole.at[part, :, me ^ mask], sems.at[index])
+        )
     for copy in copies:
         copy.start()
     for copy in copies:
@@ -339,8 +346,8 @@
 
 def gate_up_of(normed2, pieces):
     slots = normed2.shape[0]
-    seqs, parts, sub, ff = pieces[0].shape
-    whole = (parts, seqs, 4, sub, ff)
+    seqs, sub, ff = pieces[0].shape
+    whole = (2, seqs, 4, sub, ff)
     full = pl.BlockSpec(memory_space=pltpu.VMEM)
     away = pl.BlockSpec(memory_space=pl.ANY)
     shape = jax.ShapeDtypeStruct
@@ -352,7 +359,7 @@
         out_specs=(full, full, away),
         scratch_shapes=[
             pltpu.VMEM(whole, BF16),
-            pltpu.SemaphoreType.DMA((len(pieces), 2)),
+            pltpu.SemaphoreType.DMA((len(pieces),)),
             pltpu.SemaphoreType.DMA,
         ],
         compiler_params=pltpu.CompilerParams(vmem_limit_bytes=56 << 20),
@@ -403,65 +410,79 @@
         return jnp.concatenate([blocks[:, :, :q_width].reshape(sub, ATTN), key_part, value_part], axis=1)
 
     all_tokens = gather_seq(tokens[0])
-    gain_rows = jnp.broadcast_to(gains.T, (seqs, 2, gains.shape[0]))
-    all_gains = exchange(gain_rows, "seq").transpose(1, 0, 2).reshape(2, width).astype(F32)
+    qkv_rows = swap_dp(w_qkv.reshape(ranks, sub, -1)).transpose(1, 0, 2).reshape(sub, -1)
+    per_block = w_gate_up.shape[1] // ff
+    gu_rows = swap_dp(
+        w_gate_up.reshape(ranks, sub, per_block, ff).transpose(0, 2, 1, 3)
+    ).reshape(2, seqs, sub, ff)
+    qkv_mine = exchange(split_qkv(qkv_rows), "seq")
+    qkv_mine, gu_rows = tie((qkv_mine, gu_rows))
+    gu_mine = exchange(gu_rows.transpose(1, 0, 2, 3), "seq")
+    all_tokens, late_gains = tie((all_tokens, gains.T.reshape(1, -1)))
+    all_gains = gather_seq(late_gains).reshape(seqs, 2, -1).transpose(1, 0, 2)
+    all_gains = all_gains.reshape(2, width).astype(F32)
     gain_first, gain_second = all_gains[0], all_gains[1]
-    qkv_rows = lax.all_to_all(w_qkv, "dp", split_axis=0, concat_axis=1, tiled=True)
-    qkv_mine = exchange(split_qkv(qkv_rows), "seq")
     my_qkv = gather_direct(qkv_mine[:, None], 1).reshape(width, q_width + PAIR)
+    my_qkv, w_out, w_down = tie((my_qkv, w_out, w_down))
     my_out = gather_direct(w_out, 1)
-
-    per_block = w_gate_up.shape[1] // ff
-    gu_rows = exchange(
-        w_gate_up.reshape(ranks, sub, per_block, ff).transpose(0, 2, 1, 3), "dp"
-    )
-    all_tokens, gu_rows, my_qkv, all_gains = tie((all_tokens, gu_rows, my_qkv, all_gains))
-    w_down, my_qkv = tie((w_down, my_qkv))
-    gain_first, gain_second = all_gains[0], all_gains[1]
-    gu_mine = exchange(gu_rows.reshape(2, seqs, sub, ff).transpose(1, 0, 2, 3), "seq")
-    down_near = gather_near(w_down)
+    down_near = gather_halves(w_down, None)
 
     x_all = all_tokens.astype(F32)
     inv_all = lax.rsqrt(jnp.mean(x_all * x_all, axis=1, keepdims=True) + EPSILON)
     normed = (x_all * inv_all * gain_first).astype(BF16)
     qkv = dot(normed, my_qkv)
     attended, *saved = attend(qkv, cosine, sine, lengths, q_width)
-    attended, gu_mine, down_near, my_out = tie((attended, gu_mine, down_near, my_out))
-    gu_near = gather_near(gu_mine)
+    attended, gu_mine, my_out, down_near = tie((attended, gu_mine, my_out, down_near))
+    gate_mine, up_mine = gu_mine[:, 0], gu_mine[:, 1]
+    gate_near, up_near = gather_near(gate_mine, 1), gather_near(up_mine, 2)
 
     x = tokens[0].astype(F32)
     branch = scatter_seq(dot(attended, my_out))
-    branch, gu_near = tie((branch, gu_near))
-    gu_far, down_far = gather_far(gu_near), gather_far(down_near)
+    branch, gate_near, up_near, down_near = tie((branch, gate_near, up_near, down_near))
+    gate_far, up_far = gather_far(gate_near, 1), gather_far(up_near, 2)
+    down_far = gather_halves(w_down, down_near)
     hidden = x + RESIDUAL_SCALE * branch
     inv_second = lax.rsqrt(jnp.mean(hidden * hidden, axis=1, keepdims=True) + EPSILON)
     unit_second = hidden * inv_second
     normed2 = gather_seq((unit_second * gain_second).astype(BF16))
-    normed2, gu_far = tie((normed2, gu_far))
-    my_down = gathered(w_down, down_near, down_far, 1)
-    late_cotangent, normed2 = tie((cotangent[0], normed2))
+    normed2, gate_far, up_far, down_far, late_cotangent = tie(
+        (normed2, gate_far, up_far, down_far, cotangent[0])
+    )
     all_cotangent = gather_seq(late_cotangent)
-
-    if gu_near is None:
-        my_gate_up = lax.all_gather(gu_mine, "dp", axis=1).transpose(2, 0, 1, 3, 4)
-        my_gate, my_up = (my_gate_up[part].reshape(width, ff) for part in range(2))
+    my_down = join_halves(w_down, down_near, down_far, 1)
+
+    if gate_near is None:
+        my_gate, my_up = (
+            lax.all_gather(mine, "dp", axis=1).reshape(width, ff) for mine in (gate_mine, up_mine)
+        )
         gate_vals, up_vals = dot(normed2, my_gate), dot(normed2, my_up)
     else:
-        gate_vals, up_vals, my_gate_up = gate_up_of(normed2, (gu_mine,) + gu_near + gu_far)
+        pieces = (gate_mine, *gate_near, gate_far, up_mine, up_near[1], up_near[0], up_far)
+        gate_vals, up_vals, my_gate_up = gate_up_of(normed2, pieces)
         my_gate, my_up = (my_gate_up[part].reshape(width, ff) for part in range(2))
     sigmoid_gate = jax.nn.sigmoid(gate_vals)
     mixed = (gate_vals * sigmoid_gate * up_vals).astype(BF16)
+    down_sum = dot(mixed, my_down).astype(BF16)
+    all_cotangent, down_sum = tie((all_cotangent, down_sum))
+    down_out = scatter_seq(down_sum)
     down_grad = (RESIDUAL_SCALE * (all_cotangent.astype(F32) * valid)).astype(BF16)
     mixed_grad = dot_nt(down_grad, my_down)
     gate_grad = (
         mixed_grad * up_vals * sigmoid_gate * (1.0 + gate_vals * (1.0 - sigmoid_gate))
     ).astype(BF16)
     up_grad = (mixed_grad * gate_vals * sigmoid_gate).astype(BF16)
-    normed2_grad = scatter_seq(dot_nt(gate_grad, my_gate) + dot_nt(up_grad, my_up))
-    w_grads = jnp.stack([dot_tn(normed2, gate_grad), dot_tn(normed2, up_grad)])
-    gu_partial = w_grads.astype(BF16).reshape(2, seqs, ranks, sub, ff).transpose(1, 0, 2, 3, 4)
-    gu_got = scatter_first(gu_partial, 2)
-    normed2_grad, gu_got = tie((normed2_grad, gu_got))
+    normed2_sum = (dot_nt(gate_grad, my_gate) + dot_nt(up_grad, my_up)).astype(BF16)
+    normed2_sum, down_out = tie((normed2_sum, down_out))
+    normed2_grad = scatter_seq(normed2_sum)
+
+    gate_partial = dot_tn(normed2, gate_grad).astype(BF16).reshape(seqs, ranks, sub, ff)
+    gate_got = scatter_first(gate_partial, 1, 1)
+    up_partial = dot_tn(normed2, up_grad).astype(BF16).reshape(seqs, ranks, sub, ff)
+    up_got = scatter_first(up_partial, 1, 2)
+    down_partial = dot_tn(mixed, down_grad).astype(BF16)
+    normed2_grad, gate_partial, up_partial, gate_got, up_got, down_partial = tie(
+        (normed2_grad, gate_partial, up_partial, gate_got, up_got, down_partial)
+    )
 
     upstream = cotangent[0].astype(F32) * valid_rows
     unit_grad2 = normed2_grad * gain_second
@@ -470,43 +491,51 @@
     )
     gain_second_term = jnp.sum(normed2_grad * unit_second, axis=0)
     branch_grad = gather_seq((RESIDUAL_SCALE * hidden_grad).astype(BF16))
-    gu_summed = scatter_second(gu_partial, gu_got, 2)
-    branch_grad, gu_summed, mixed = tie((branch_grad, gu_summed.astype(BF16), mixed))
-    down_out = scatter_seq(dot(mixed, my_down))
-    output = (valid_rows * (hidden + RESIDUAL_SCALE * down_out)).astype(BF16)
+    gate_summed = scatter_second(gate_partial, gate_got, 1, 1).astype(BF16)
+    up_summed = scatter_second(up_partial, up_got, 1, 2).astype(BF16)
+    branch_grad, gate_summed, up_summed, down_partial = tie(
+        (branch_grad, gate_summed, up_summed, down_partial)
+    )
+    gu_blocks = exchange(jnp.stack([gate_summed, up_summed], axis=1), "seq")
+    grad_down = scatter_direct(down_partial, 1)
 
     attended_grad = dot_nt(branch_grad, my_out).astype(BF16)
     qkv_grad = attend_back(saved, attended_grad, cosine, sine, lengths)
-    gu_blocks = exchange(gu_summed, "seq")
-    down_partial = dot_tn(mixed, down_grad).astype(BF16)
-    down_got = scatter_first(down_partial, 1)
-    qkv_grad, down_got = tie((qkv_grad, down_got))
     normed_partial = dot_nt(qkv_grad, my_qkv)
-    normed_grad = scatter_seq(normed_partial)
-
+    normed_sum, gu_blocks, grad_down = tie((normed_partial.astype(BF16), gu_blocks, grad_down))
+    normed_grad = scatter_seq(normed_sum)
+
+    qkv_grad, attended, normed_partial = tie((qkv_grad, attended, normed_partial))
     qkv_partial = dot_tn(normed, qkv_grad).astype(BF16).reshape(seqs, ranks, sub, -1)
-    qkv_summed = scatter_second(qkv_partial, scatter_first(qkv_partial, 1), 1)
-    qkv_back = join_qkv(exchange(qkv_summed.astype(BF16), "seq"))
-    grad_qkv = lax.all_to_all(qkv_back, "dp", split_axis=1, concat_axis=0, tiled=True).astype(F32)
+    qkv_summed = scatter_direct(qkv_partial, 1).astype(BF16)
     out_partial = dot_tn(attended, branch_grad).astype(BF16)
-    grad_out = scatter_second(out_partial, scatter_first(out_partial, 1), 1)
-    grad_down = scatter_second(down_partial, down_got, 1)
-    gu_back = exchange(
-        gu_blocks.transpose(1, 0, 2, 3).reshape(ranks, per_block, sub, ff), "dp"
+    grad_out = scatter_direct(out_partial, 1)
+    qkv_back = join_qkv(exchange(qkv_summed, "seq"))
+    grad_qkv = (
+        swap_dp(qkv_back.reshape(sub, ranks, -1).transpose(1, 0, 2))
+        .reshape(w_qkv.shape)
+        .astype(F32)
+    )
+    gu_back = swap_dp(
+        gu_blocks.transpose(1, 0, 2, 3).reshape(ranks, per_block, sub, ff)
     )
     grad_gate_up = gu_back.transpose(0, 2, 1, 3).reshape(w_gate_up.shape).astype(F32)
 
     unit_all = x_all * inv_all
     gain_first_term = jnp.sum(normed_partial * unit_all, axis=0)
-    gains_term = jnp.stack([gain_first_term, gain_second_term], axis=1)
-    gain_blocks = exchange(gains_term.reshape(seqs, -1, 2), "seq")
-    grad_gains = jnp.sum(gain_blocks, axis=0).T
+    gains_term = jnp.stack([gain_first_term, gain_second_term]).reshape(2, seqs, -1)
+    gain_blocks = exchange(gains_term.transpose(1, 0, 2), "seq")
+    grad_gains = jnp.sum(gain_blocks, axis=0)
     if ranks == 4:
         grad_gains = grad_gains + send(grad_gains, 1)
         grad_gains = (grad_gains + send(grad_gains, 2)).T
     else:
         grad_gains = lax.psum(grad_gains, "dp").T
 
+    normed_grad, grad_qkv, grad_out, grad_gate_up, grad_gains = tie(
+        (normed_grad, grad_qkv, grad_out, grad_gate_up, grad_gains)
+    )
+    output = (valid_rows * (hidden + RESIDUAL_SCALE * down_out)).astype(BF16)
     inv_first = lax.rsqrt(jnp.mean(x * x, axis=1, keepdims=True) + EPSILON)
     unit_first = x * inv_first
     unit_grad1 = normed_grad * gain_first

time: 702 us -> 619 us (0.88)
  waiting for transfers between devices: 340 us -> 270 us
  blocking collectives: 33.9 us -> 17 us
  other arithmetic: 65.2 us -> 49.4 us
  local copies, waits for them, and re-layouts: 51.5 us -> 61.9 us
  starting transfers between devices: 74.1 us -> 83 us
    all_to_all x7 -> x5, waiting for transfers between devices: 72.9 us -> 24.5 us  [exchange(): lax.all_to_all(blocks, axis_name, split_axis=0, concat_axis=0, tiled=True)]
    all_to_all x2 -> x0, blocking collectives: 33.9 us -> none  [the longest x1 21.6 us: exchange(): lax.all_to_all(blocks, axis_name, split_axis=0, concat_axis=0, tiled=True)]
    all_gather x4, waiting for transfers between devices: 38.7 us -> 16.3 us  [gather_seq(): return lax.all_gather(shard, 'seq', axis=0, tiled=True)]
    all_gather x0 -> x1, blocking collectives: none -> 17 us  [gather_seq(): return lax.all_gather(shard, 'seq', axis=0, tiled=True)]
    ppermute x36 -> x47, starting transfers between devices: 42.3 us -> 57.3 us  [send(): return lax.ppermute(value, 'dp', flip(mask, lax.axis_size('dp')))]
    reduce_scatter x4, waiting for transfers between devices: 65.9 us -> 78.9 us  [scatter_seq(): lax.psum_scatter(partial.astype(BF16), 'seq', scatter_dimension=0, tiled=...]
    ppermute x36 -> x47, waiting for transfers between devices: 160 us -> 149 us  [send(): return lax.ppermute(value, 'dp', flip(mask, lax.axis_size('dp')))]
    squeeze x0 -> x9, local copies, waits for them, and re-layouts: none -> 10 us  [the longest x8 6.89 us: dp_block(): return lax.dynamic_index_in_dim(partial, place, axis, keepdims=False)]
  transfers between devices with their start and end apart: 52 -> 60, of which waited for: 35 -> 26; matrix products, arithmetic and copies ran while one was open for 20% -> 26% of each run, Pallas kernels for 6% -> 7%
where the time goes in v2:
time: 619 us; the launch traced here: 612 us
  waiting for transfers between devices  270 us (44%)
  starting transfers between devices  83 us (13%)
  matrix products  74.1 us (12%)
  local copies, waits for them, and re-layouts  61.9 us (10%)
  other arithmetic  49.4 us (8%)
  Pallas kernels  40.6 us (7%)
  blocking collectives  17 us (3%)
  between operations  16.1 us (3%)
    ppermute x47, waiting for transfers between devices, send(): return lax.ppermute(value, 'dp', flip(mask, lax.axis_size('dp')))  149 us
    reduce_scatter x4, waiting for transfers between devices, scatter_seq(): lax.psum_scatter(partial.astype(BF16), 'seq', scatter_dimension=0, tiled=...  78.9 us
    ppermute x47, starting transfers between devices, send(): return lax.ppermute(value, 'dp', flip(mask, lax.axis_size('dp')))  57.3 us
    dot_general x5, matrix products, dot_nt(): lax.dot_general(left, right, (((1,), (1,)), ((), ())), preferred_element_...  33.2 us
    dot_general x5, matrix products, dot_tn(): lax.dot_general(left, right, (((0,), (0,)), ((), ())), preferred_element_...  27.6 us
    all_to_all x5, starting transfers between devices, exchange(): lax.all_to_all(blocks, axis_name, split_axis=0, concat_axis=0, tiled=True)  24.5 us
    all_to_all x5, waiting for transfers between devices, exchange(): lax.all_to_all(blocks, axis_name, split_axis=0, concat_axis=0, tiled=True)  24.5 us
    pallas_call x1, Pallas kernels, gate_up_of(): pl.pallas_call(gate_up_kernel, out_shape=(shape((slots, ff), F32), shape(...  20.3 us
  transfers between devices with their start and end apart: 60, of which 26 were waited for; matrix products, arithmetic and copies ran while one was open for 26% of the time, Pallas kernels for 7%

profile of v2, /device:TPU:0, one launch (start us, length us, event | category | flops | bytes accessed | tf_op | source)
XLA Modules:
  0.0 611.9 jit_solution(9074156232538538288)
XLA Ops:
  9.0 3.0 collective-permute-start
  13.6 3.3 reshape.151
  24.9 5.3 all-to-all-start
  30.3 3.5 collective-permute-done.3
  35.0 9.7 %collective-permute-done.4 = bf16[4,64,1024]{2,0,1:T(4,128)(2,1)} collective-permute-done((bf16[4,64,1024]{2,0,1:T(4,128)(2,1)}, bf16[4,64,1024]{2,0,1:T(4,128)(2,1)}, u32[]{:S(2)}, u32[]{:S(2)}) %collective-permute-start.4) | collective-permute-done | bytes 524320 | tf_op jit(solution)/shard_map/ppermute | solution.py:205
  47.1 6.1 all-to-all-done
  54.8 4.5 all-to-all-start.1
  62.7 2.3 fusion.27
  66.6 4.9 collective-permute-done.6
  71.5 9.3 %collective-permute-done.7 = bf16[8,1,64,384]{3,2,1,0:T(8,128)(2,1)} collective-permute-done((bf16[8,1,64,384]{3,2,1,0:T(8,128)(2,1)S(1)}, bf16[8,1,64,384]{3,2,1,0:T(8,128)(2,1)}, u32[]{:S(2)}, u32[]{:S(2)}) %collective-permute-start.7) | collective-permute-done | bytes 393248 | tf_op jit(solution)/shard_map/ppermute | solution.py:205
  82.0 2.0 collective-permute-start.10
  85.5 2.2 fusion.33
  95.8 2.8 collective-permute-start.15
  100.0 17.0 %all-gather.1 = bf16[8,1,512]{2,1,0:T(2,128)(2,1)S(1)} all-gather(bf16[1,1,512]{2,1,0:T(2,128)(2,1)S(1)} %bitcast.235), channel_id=1, replica_groups=mesh['dp'=4,'seq'=8] {'seq'}, dimensions={0}, use_global_device_ids=true | all-gather | bytes 9216 | tf_op jit(solution)/shard_map/all_gather | solution.py:305
  117.1 3.2 fusion.4
  120.5 2.4 fusion.15.qkv_ref
  122.9 9.6 %shard_map.135 = (bf16[1024,256]{1,0:T(8,128)(2,1)S(1)}, bf16[1024,256]{1,0:T(8,128)(2,1)S(1)}, bf16[1024,128]{1,0:T(8,128)(2,1)S(1)}, bf16[1024,128]{1,0:T(8,128)(2,1)S(1)}, f32[8,1024]{1,0:T(8,128)S(1)}) custom-call(s32[1]{0:T(128)} %copy.224.length_ref, f32[1024,384]{1,0:T(8,128)S(1)} %fusion.15.qkv_ref, f32[1024,128]{1,0:T(8,128)S(1)} %get-tuple-element.165.cos_ref, ...), custom_call_target="tpu_custom_call" | custom-call | flops 1073741824 | bytes 3145728 | tf_op jit(solution)/shard_map/pallas_call | solution.py:117
  132.5 4.9 convolution_convert_fusion
  137.5 3.1 slice_bitcast_fusion
  144.7 40.9 %reduce-scatter.5.cloned.1.call-done = bf16[128,2048]{1,0:T(8,128)(2,1)} async-done(((bf16[1024,2048]{1,0:T(8,128)(2,1)}), bf16[128,2048]{1,0:T(8,128)(2,1)}) %reduce-scatter.5.cloned.1.call-update) | async-done | bytes 524304 | tf_op jit(solution)/shard_map/reduce_scatter | solution.py:309
  186.8 3.2 collective-permute-done.18.refs_6_
  196.5 31.8 %collective-permute-done.22 = bf16[512,512]{1,0:T(8,128)(2,1)} collective-permute-done((bf16[512,512]{1,0:T(8,128)(2,1)}, bf16[512,512]{1,0:T(8,128)(2,1)}, u32[]{:S(2)}, u32[]{:S(2)}) %collective-permute-start.22) | collective-permute-done | bytes 524320 | tf_op jit(solution)/shard_map/ppermute | solution.py:205
  229.5 7.1 %all-gather.7.cloned.1.call-done.x_ref = bf16[1024,2048]{1,0:T(8,128)(2,1)} async-done(((bf16[128,2048]{1,0:T(8,128)(2,1)}), bf16[1024,2048]{1,0:T(8,128)(2,1)}) %all-gather.7.cloned.1.call-update) | async-done | bytes 4194320 | tf_op jit(solution)/shard_map/all_gather | solution.py:305
  242.0 20.3 %shard_map.136 = (f32[1024,1024]{1,0:T(8,128)}, f32[1024,1024]{1,0:T(8,128)}, bf16[2,8,4,64,1024]{4,3,2,1,0:T(8,128)(2,1)}) custom-call(s32[1]{0:T(128)} %bitcast.34.me_ref, bf16[1024,2048]{1,0:T(8,128)(2,1)} %all-gather.7.cloned.1.call-done.x_ref, bf16[8,64,1024]{2,1,0:T(8,128)(2,1)} %get-tuple-element.149.refs_0_, ...), custom_call_target="tpu_custom_call" | custom-call | flops 8589934592 | bytes 25165824 | tf_op jit(solution)/shard_map/pallas_call | solution.py:355
  262.4 4.9 multiply_convert_fusion.3
  268.6 6.0 convolution_convert_fusion.4
  274.6 9.2 %all-gather.9.cloned.1.call-done = bf16[1024,2048]{1,0:T(8,128)(2,1)} async-done(((bf16[128,2048]{1,0:T(8,128)(2,1)}), bf16[1024,2048]{1,0:T(8,128)(2,1)}) %all-gather.9.cloned.1.call-update) | async-done | bytes 4194320 | tf_op jit(solution)/shard_map/all_gather | solution.py:305
  284.3 7.3 %fusion.32 = (bf16[1,8,4,64,1024]{4,3,2,1,0:T(8,128)(2,1)}, bf16[1,8,4,64,1024]{4,3,2,1,0:T(8,128)(2,1)}) fusion(bf16[2,8,4,64,1024]{4,3,2,1,0:T(8,128)(2,1)} %get-tuple-element.102), kind=kLoop, calls=%fused_computation.143 | loop fusion | bytes 16777216 | tf_op jit(solution)/shard_map/slice | solution.py:462
  294.4 9.9 %multiply_convert_fusion.1 = (bf16[1024,1024]{1,0:T(8,128)(2,1)}, bf16[1024,1024]{1,0:T(8,128)(2,1)}) fusion(f32[1024,1024]{1,0:T(8,128)S(1)} %copy-done.13, f32[1024,1024]{1,0:T(8,128)S(1)} %copy-done.14, bf16[1024,2048]{1,0:T(8,128)(2,1)S(1)} %copy-done.16, bf16[1024,2048]{1,0:T(8,128)(2,1)} %all-gather.9.cloned.1.call-done, f32[1024]{0:T(1024)S(1)} %fusion.29), kind=kOutput, calls=%fused_computation.10 | convolution fusion | flops 4316987392 | bytes 20975616 | tf_op jit(solution)/shard_map/dot_general | solution.py:33
  304.3 7.2 %fusion.38 = f32[1024,2048]{1,0:T(8,128)S(1)} fusion(bf16[1024,1024]{1,0:T(8,128)(2,1)} %get-tuple-element.140, bf16[2048,1024]{1,0:T(8,128)(2,1)} %bitcast.206), kind=kOutput, calls=%fused_computation.149 | convolution fusion | flops 4294967296 | bytes 14680064 | tf_op jit(solution)/shard_map/dot_general | solution.py:33
  311.5 6.1 add_convert_fusion
  317.6 17.0 %reduce-scatter.7.cloned.1.call-done = bf16[128,2048]{1,0:T(8,128)(2,1)} async-done(((bf16[1024,2048]{1,0:T(8,128)(2,1)}), bf16[128,2048]{1,0:T(8,128)(2,1)}) %reduce-scatter.7.cloned.1.call-update) | async-done | bytes 524304 | tf_op jit(solution)/shard_map/reduce_scatter | solution.py:309
  334.7 2.1 convert_element_type.245
  337.1 7.6 %convolution_convert_fusion.3 = bf16[2048,1024]{1,0:T(8,128)(2,1)S(1)} fusion(bf16[1024,2048]{1,0:T(8,128)(2,1)} %all-gather.7.cloned.1.call-done.x_ref, bf16[1024,1024]{1,0:T(8,128)(2,1)} %get-tuple-element.140), kind=kOutput, calls=%fused_computation.17 | convolution fusion | flops 4297064448 | bytes 10485760 | tf_op jit(solution)/shard_map/dot_general | solution.py:37
  348.6 4.9 convolution_convert_fusion.2
  353.5 2.0 copy-done.8
  358.1 6.7 %convolution_convert_fusion.1 = bf16[1024,2048]{1,0:T(8,128)(2,1)} fusion(bf16[1024,1024]{1,0:T(8,128)(2,1)S(1)} %copy-done.20, bf16[1024,2048]{1,0:T(8,128)(2,1)S(1)} %copy-done.28, f32[1024]{0:T(1024)S(1)} %fusion.29), kind=kOutput, calls=%fused_computation.15 | convolution fusion | flops 4305453056 | bytes 10489856 | tf_op jit(solution)/shard_map/dot_general | solution.py:37
  364.8 21.0 %reduce-scatter.9.cloned.1.call-done = bf16[128,2048]{1,0:T(8,128)(2,1)} async-done(((bf16[1024,2048]{1,0:T(8,128)(2,1)}), bf16[128,2048]{1,0:T(8,128)(2,1)}) %reduce-scatter.9.cloned.1.call-update) | async-done | bytes 524304 | tf_op jit(solution)/shard_map/reduce_scatter | solution.py:309
  390.7 2.1 fusion.8
  400.1 18.7 %collective-permute-done.27 = bf16[8,64,1024]{2,1,0:T(8,128)(2,1)S(1)} collective-permute-done((bf16[8,64,1024]{2,1,0:T(8,128)(2,1)S(1)}, bf16[8,64,1024]{2,1,0:T(8,128)(2,1)S(1)}, u32[]{:S(2)}, u32[]{:S(2)}) %collective-permute-start.27) | collective-permute-done | bytes 1048608 | tf_op jit(solution)/shard_map/ppermute | solution.py:205
  418.9 2.9 collective-permute-done.26
  421.7 2.9 fusion.10
  424.6 16.3 %collective-permute-done.29 = bf16[8,64,1024]{2,1,0:T(8,128)(2,1)S(1)} collective-permute-done((bf16[8,64,1024]{2,1,0:T(8,128)(2,1)S(1)}, bf16[8,64,1024]{2,1,0:T(8,128)(2,1)S(1)}, u32[]{:S(2)}, u32[]{:S(2)}) %collective-permute-start.29) | collective-permute-done | bytes 1048608 | tf_op jit(solution)/shard_map/ppermute | solution.py:205
  442.5 3.1 pad_maximum_fusion
  445.6 4.4 all-to-all-start.2
  450.2 2.2 constant_dynamic-slice_fusion.9
  456.0 2.5 convolution_convert_fusion.7.grad_ref
  458.6 10.8 %shard_map.137 = bf16[1024,384]{1,0:T(8,128)(2,1)S(1)} custom-call(s32[1]{0:T(128)} %copy.224.length_ref, bf16[1024,256]{1,0:T(8,128)(2,1)S(1)} %get-tuple-element.107.q_ref, bf16[1024,128]{1,0:T(8,128)(2,1)S(1)} %get-tuple-element.108.k_ref, bf16[1024,128]{1,0:T(8,128)(2,1)S(1)} %get-tuple-element.109.v_ref, f32[8,1024]{1,0:T(8,128)S(1)} %get-tuple-element.110.lse_ref, ...), custom_call_target="tpu_custom_call" | custom-call | flops 2684354560 | bytes 3145728 | tf_op jit(solution)/shard_map/pallas_call | solution.py:186
  469.4 7.5 %fusion.37 = (bf16[1024,2048]{1,0:T(8,128)(2,1)}, f32[1024,2048]{1,0:T(8,128)}) fusion(bf16[1024,384]{1,0:T(8,128)(2,1)S(1)} %shard_map.137, bf16[2048,384]{1,0:T(8,128)(2,1)S(1)} %bitcast.193), kind=kOutput, calls=%fused_computation.148 | convolution fusion | flops 1612709888 | bytes 14942208 | tf_op jit(solution)/shard_map/dot_general | solution.py:33
  476.8 2.7 collective-permute-done.32
  479.5 21.8 %collective-permute-done.31 = bf16[1024,512]{1,0:T(8,128)(2,1)S(1)} collective-permute-done((bf16[1024,512]{1,0:T(8,128)(2,1)S(1)}, bf16[1024,512]{1,0:T(8,128)(2,1)S(1)}, u32[]{:S(2)}, u32[]{:S(2)}) %collective-permute-start.31) | collective-permute-done | bytes 1048608 | tf_op jit(solution)/shard_map/ppermute | solution.py:205
  501.3 3.1 convert_add_fusion.4
  504.5 4.9 convolution_convert_fusion.5
  514.9 4.7 all-to-all-start.4
  519.7 3.5 convolution_convert_fusion.6
  523.2 2.4 all-to-all-done.4
  533.0 2.2 fusion.25
  535.2 5.6 all-to-all-start.3
  544.0 16.0 %all-to-all-done.3 = bf16[8,64,384]{2,1,0:T(8,128)(2,1)S(1)} async-done(((bf16[8,64,384]{2,1,0:T(8,128)(2,1)}), bf16[8,64,384]{2,1,0:T(8,128)(2,1)S(1)}, u32[]{:S(2)}, u32[]{:S(2)}) %all-to-all-start.3) | async-done | bytes 393248 | tf_op jit(solution)/shard_map/all_to_all | solution.py:301
  569.6 2.2 collective-permute-start.43
  574.1 10.2 %collective-permute-done.42 = bf16[4,64,1024]{2,1,0:T(8,128)(2,1)S(1)} collective-permute-done((bf16[4,64,1024]{2,1,0:T(8,128)(2,1)S(1)}, bf16[4,64,1024]{2,1,0:T(8,128)(2,1)S(1)}, u32[]{:S(2)}, u32[]{:S(2)}) %collective-permute-start.42) | collective-permute-done | bytes 524320 | tf_op jit(solution)/shard_map/ppermute | solution.py:205
  584.4 8.6 %collective-permute-done.43 = bf16[4,64,1024]{2,1,0:T(8,128)(2,1)S(1)} collective-permute-done((bf16[4,64,1024]{2,1,0:T(8,128)(2,1)S(1)}, bf16[4,64,1024]{2,1,0:T(8,128)(2,1)S(1)}, u32[]{:S(2)}, u32[]{:S(2)}) %collective-permute-start.43) | collective-permute-done | bytes 524320 | tf_op jit(solution)/shard_map/ppermute | solution.py:205
  593.5 2.7 copy.164
  596.3 5.8 copy.174
  (262 shorter events, 111.6 us)
Async XLA Ops:
  7.2 92.9 %all-gather.13.cloned.1.call-start = ((), (), s32[]{:S(2)}) async-start(), calls=%async_computation.16 | async-start | bytes 4718592 | tf_op jit(solution)/shard_map/all_gather | solution.py:305
  9.0 13.5 %collective-permute-start = (bf16[64,768]{1,0:T(8,128)(2,1)S(1)}, bf16[64,768]{1,0:T(8,128)(2,1)}, u32[]{:S(2)}, u32[]{:S(2)}) collective-permute-start(bf16[64,768]{1,0:T(8,128)(2,1)S(1)} %get-tuple-element.176), channel_id=1, source_target_pairs={{0,8},{8,0},{16,24},{24,16},{1,9},{9,1},{17,25},{25,17},{2,10},{10... | collective-permute-start | bytes 294920 | tf_op jit(solution)/shard_map/ppermute | solution.py:205
  12.1 11.5 %collective-permute-start.1 = (bf16[64,768]{1,0:T(8,128)(2,1)S(1)}, bf16[64,768]{1,0:T(8,128)(2,1)S(1)}, u32[]{:S(2)}, u32[]{:S(2)}) collective-permute-start(bf16[64,768]{1,0:T(8,128)(2,1)S(1)} %get-tuple-element.175), channel_id=1, source_target_pairs={{0,16},{8,24},{16,0},{24,8},{1,17},{9,25},{17,1},{25,9},{2,18},{10... | collective-permute-start | bytes 294920 | tf_op jit(solution)/shard_map/ppermute | solution.py:205
  13.6 10.0 %collective-permute-start.2 = (bf16[64,768]{1,0:T(8,128)(2,1)S(1)}, bf16[64,768]{1,0:T(8,128)(2,1)S(1)}, u32[]{:S(2)}, u32[]{:S(2)}) collective-permute-start(bf16[64,768]{1,0:T(8,128)(2,1)S(1)} %get-tuple-element.174), channel_id=1, source_target_pairs={{0,24},{8,16},{16,8},{24,0},{1,25},{9,17},{17,9},{25,1},{2,26},{10... | collective-permute-start | bytes 294920 | tf_op jit(solution)/shard_map/ppermute | solution.py:205
  18.6 15.1 %collective-permute-start.3 = (bf16[4,64,1024]{2,0,1:T(4,128)(2,1)}, bf16[4,64,1024]{2,0,1:T(4,128)(2,1)}, u32[]{:S(2)}, u32[]{:S(2)}) collective-permute-start(bf16[4,64,1024]{2,0,1:T(4,128)(2,1)} %get-tuple-element.152), channel_id=1, source_target_pairs={{0,8},{8,0},{16,24},{24,16},{1,9},{9,1},{17,25},{25,17},{2,10},{10... | collective-permute-start | bytes 1572872 | tf_op jit(solution)/shard_map/ppermute | solution.py:205
  20.6 24.1 %collective-permute-start.4 = (bf16[4,64,1024]{2,0,1:T(4,128)(2,1)}, bf16[4,64,1024]{2,0,1:T(4,128)(2,1)}, u32[]{:S(2)}, u32[]{:S(2)}) collective-permute-start(bf16[4,64,1024]{2,0,1:T(4,128)(2,1)} %get-tuple-element.151), channel_id=1, source_target_pairs={{0,16},{8,24},{16,0},{24,8},{1,17},{9,25},{17,1},{25,9},{2,18},{10... | collective-permute-start | bytes 1572872 | tf_op jit(solution)/shard_map/ppermute | solution.py:205
  22.6 23.3 %collective-permute-start.5 = (bf16[4,64,1024]{2,0,1:T(4,128)(2,1)}, bf16[4,64,1024]{2,0,1:T(4,128)(2,1)}, u32[]{:S(2)}, u32[]{:S(2)}) collective-permute-start(bf16[4,64,1024]{2,0,1:T(4,128)(2,1)} %get-tuple-element.150), channel_id=1, source_target_pairs={{0,24},{8,16},{16,8},{24,0},{1,25},{9,17},{17,9},{25,1},{2,26},{10... | collective-permute-start | bytes 1572872 | tf_op jit(solution)/shard_map/ppermute | solution.py:205
  24.9 28.3 %all-to-all-start = ((bf16[8,64,384]{2,1,0:T(8,128)(2,1)}), bf16[8,64,384]{2,1,0:T(8,128)(2,1)S(1)}, u32[]{:S(2)}, u32[]{:S(2)}) async-start(bf16[8,64,384]{2,1,0:T(8,128)(2,1)} %copy.147), calls=%async_computation | async-start | bytes 786432 | tf_op jit(solution)/shard_map/all_to_all | solution.py:301
  54.8 77.7 %all-to-all-start.1 = ((bf16[8,2,64,1024]{3,2,1,0:T(8,128)(2,1)}), bf16[8,2,64,1024]{3,2,1,0:T(8,128)(2,1)}, u32[]{:S(2)}, u32[]{:S(2)}) async-start(bf16[8,2,64,1024]{3,2,1,0:T(8,128)(2,1)} %copy.152), calls=%async_computation.1 | async-start | bytes 4194304 | tf_op jit(solution)/shard_map/all_to_all | solution.py:301
  59.3 126.4 %reduce-scatter.5.cloned.1.call-start = ((), (), s32[]{:S(2)}) async-start(), calls=%async_computation.9 | async-start | bytes 4718592 | tf_op jit(solution)/shard_map/reduce_scatter | solution.py:309
  59.4 12.1 %collective-permute-start.6 = (bf16[8,1,64,384]{3,2,1,0:T(8,128)(2,1)S(1)}, bf16[8,1,64,384]{3,2,1,0:T(8,128)(2,1)S(1)}, u32[]{:S(2)}, u32[]{:S(2)}) collective-permute-start(bf16[8,1,64,384]{3,2,1,0:T(8,128)(2,1)S(1)} %bitcast.215), channel_id=1, source_target_pairs={{0,8},{8,0},{16,24},{24,16},{1,9},{9,1},{17,25},{25,17},{2,10},{10... | collective-permute-start | bytes 1179656 | tf_op jit(solution)/shard_map/ppermute | solution.py:205
  61.1 19.7 %collective-permute-start.7 = (bf16[8,1,64,384]{3,2,1,0:T(8,128)(2,1)S(1)}, bf16[8,1,64,384]{3,2,1,0:T(8,128)(2,1)}, u32[]{:S(2)}, u32[]{:S(2)}) collective-permute-start(bf16[8,1,64,384]{3,2,1,0:T(8,128)(2,1)S(1)} %bitcast.216), channel_id=1, source_target_pairs={{0,16},{8,24},{16,0},{24,8},{1,17},{9,25},{17,1},{25,9},{2,18},{10... | collective-permute-start | bytes 1179656 | tf_op jit(solution)/shard_map/ppermute | solution.py:205
  65.7 16.1 %collective-permute-start.8 = (bf16[8,1,64,384]{3,2,1,0:T(8,128)(2,1)S(1)}, bf16[8,1,64,384]{3,2,1,0:T(8,128)(2,1)S(1)}, u32[]{:S(2)}, u32[]{:S(2)}) collective-permute-start(bf16[8,1,64,384]{3,2,1,0:T(8,128)(2,1)S(1)} %bitcast.217), channel_id=1, source_target_pairs={{0,24},{8,16},{16,8},{24,0},{1,25},{9,17},{17,9},{25,1},{2,26},{10... | collective-permute-start | bytes 1179656 | tf_op jit(solution)/shard_map/ppermute | solution.py:205
  81.9 38.4 %copy-start.6 = (bf16[8,4,64,384]{3,2,1,0:T(8,128)(2,1)}, bf16[8,4,64,384]{3,2,1,0:T(8,128)(2,1)S(1)}, u32[]{:S(2)}) copy-start(bf16[8,4,64,384]{3,2,1,0:T(8,128)(2,1)S(1)} %constant_dynamic-update-slice_fusion.5) | copy-start | bytes 4718596
  81.9 10.6 %collective-permute-start.9 = (bf16[256,512]{1,0:T(8,128)(2,1)}, bf16[256,512]{1,0:T(8,128)(2,1)S(1)}, u32[]{:S(2)}, u32[]{:S(2)}) collective-permute-start(bf16[256,512]{1,0:T(8,128)(2,1)} %param.11), channel_id=1, source_target_pairs={{0,8},{8,0},{16,24},{24,16},{1,9},{9,1},{17,25},{25,17},{2,10},{10... | collective-permute-start | bytes 786440 | tf_op jit(solution)/shard_map/ppermute | solution.py:205
  82.0 13.8 %collective-permute-start.10 = (bf16[256,512]{1,0:T(8,128)(2,1)}, bf16[256,512]{1,0:T(8,128)(2,1)S(1)}, u32[]{:S(2)}, u32[]{:S(2)}) collective-permute-start(bf16[256,512]{1,0:T(8,128)(2,1)} %param.11), channel_id=1, source_target_pairs={{0,16},{8,24},{16,0},{24,8},{1,17},{9,25},{17,1},{25,9},{2,18},{10... | collective-permute-start | bytes 786440 | tf_op jit(solution)/shard_map/ppermute | solution.py:205
  84.1 15.3 %collective-permute-start.11 = (bf16[256,512]{1,0:T(8,128)(2,1)}, bf16[256,512]{1,0:T(8,128)(2,1)S(1)}, u32[]{:S(2)}, u32[]{:S(2)}) collective-permute-start(bf16[256,512]{1,0:T(8,128)(2,1)} %param.11), channel_id=1, source_target_pairs={{0,24},{8,16},{16,8},{24,0},{1,25},{9,17},{17,9},{25,1},{2,26},{10... | collective-permute-start | bytes 786440 | tf_op jit(solution)/shard_map/ppermute | solution.py:205
  87.7 44.7 %collective-permute-start.12 = (bf16[512,512]{1,0:T(8,128)(2,1)}, bf16[512,512]{1,0:T(8,128)(2,1)S(1)}, u32[]{:S(2)}, u32[]{:S(2)}) collective-permute-start(bf16[512,512]{1,0:T(8,128)(2,1)} %get-tuple-element.162), channel_id=1, source_target_pairs={{0,8},{8,0},{16,24},{24,16},{1,9},{9,1},{17,25},{25,17},{2,10},{10... | collective-permute-start | bytes 1572872 | tf_op jit(solution)/shard_map/ppermute | solution.py:205
  87.8 44.7 %collective-permute-start.14 = (bf16[512,512]{1,0:T(8,128)(2,1)}, bf16[512,512]{1,0:T(8,128)(2,1)}, u32[]{:S(2)}, u32[]{:S(2)}) collective-permute-start(bf16[512,512]{1,0:T(8,128)(2,1)} %get-tuple-element.162), channel_id=1, source_target_pairs={{0,16},{8,24},{16,0},{24,8},{1,17},{9,25},{17,1},{25,9},{2,18},{10... | collective-permute-start | bytes 1572872 | tf_op jit(solution)/shard_map/ppermute | solution.py:205
  92.5 40.0 %collective-permute-start.13 = (bf16[512,512]{1,0:T(8,128)(2,1)}, bf16[512,512]{1,0:T(8,128)(2,1)}, u32[]{:S(2)}, u32[]{:S(2)}) collective-permute-start(bf16[512,512]{1,0:T(8,128)(2,1)} %get-tuple-element.161), channel_id=1, source_target_pairs={{0,8},{8,0},{16,24},{24,16},{1,9},{9,1},{17,25},{25,17},{2,10},{10... | collective-permute-start | bytes 1572872 | tf_op jit(solution)/shard_map/ppermute | solution.py:205
  95.8 36.7 %collective-permute-start.15 = (bf16[512,512]{1,0:T(8,128)(2,1)}, bf16[512,512]{1,0:T(8,128)(2,1)}, u32[]{:S(2)}, u32[]{:S(2)}) collective-permute-start(bf16[512,512]{1,0:T(8,128)(2,1)} %get-tuple-element.161), channel_id=1, source_target_pairs={{0,16},{8,24},{16,0},{24,8},{1,17},{9,25},{17,1},{25,9},{2,18},{10... | collective-permute-start | bytes 1572872 | tf_op jit(solution)/shard_map/ppermute | solution.py:205
  137.5 52.6 %copy-start.4 = (bf16[1,128,2048]{2,1,0:T(8,128)(2,1)S(1)}, bf16[1,128,2048]{2,1,0:T(8,128)(2,1)}, u32[]{:S(2)}) copy-start(bf16[1,128,2048]{2,1,0:T(8,128)(2,1)} %param.8) | copy-start | bytes 1572868
  137.5 99.1 %all-gather.7.cloned.1.call-start = ((), (), s32[]{:S(2)}) async-start(), calls=%async_computation.10 | async-start | bytes 4718592 | tf_op jit(solution)/shard_map/all_gather | solution.py:305
  140.7 46.1 %collective-permute-start.16 = (bf16[8,64,1024]{2,1,0:T(8,128)(2,1)}, bf16[8,64,1024]{2,1,0:T(8,128)(2,1)}, u32[]{:S(2)}, u32[]{:S(2)}) collective-permute-start(bf16[8,64,1024]{2,1,0:T(8,128)(2,1)} %get-tuple-element.149.refs_0_), channel_id=1, source_target_pairs={{0,8},{8,0},{16,24},{24,16},{1,9},{9,1},{17,25},{25,17},{2,10},{10... | collective-permute-start | bytes 3145736 | tf_op jit(solution)/shard_map/ppermute | solution.py:205
  142.1 44.7 %collective-permute-start.17 = (bf16[8,64,1024]{2,1,0:T(8,128)(2,1)}, bf16[8,64,1024]{2,1,0:T(8,128)(2,1)}, u32[]{:S(2)}, u32[]{:S(2)}) collective-permute-start(bf16[8,64,1024]{2,1,0:T(8,128)(2,1)} %get-tuple-element.149.refs_0_), channel_id=1, source_target_pairs={{0,16},{8,24},{16,0},{24,8},{1,17},{9,25},{17,1},{25,9},{2,18},{10... | collective-permute-start | bytes 3145736 | tf_op jit(solution)/shard_map/ppermute | solution.py:205
  143.6 46.5 %collective-permute-start.18 = (bf16[8,64,1024]{2,1,0:T(8,128)(2,1)}, bf16[8,64,1024]{2,1,0:T(8,128)(2,1)}, u32[]{:S(2)}, u32[]{:S(2)}) collective-permute-start(bf16[8,64,1024]{2,1,0:T(8,128)(2,1)} %get-tuple-element.148.refs_4_), channel_id=1, source_target_pairs={{0,16},{8,24},{16,0},{24,8},{1,17},{9,25},{17,1},{25,9},{2,18},{10... | collective-permute-start | bytes 3145736 | tf_op jit(solution)/shard_map/ppermute | solution.py:205
  144.1 45.9 %collective-permute-start.19 = (bf16[8,64,1024]{2,1,0:T(8,128)(2,1)}, bf16[8,64,1024]{2,1,0:T(8,128)(2,1)}, u32[]{:S(2)}, u32[]{:S(2)}) collective-permute-start(bf16[8,64,1024]{2,1,0:T(8,128)(2,1)} %get-tuple-element.148.refs_4_), channel_id=1, source_target_pairs={{0,8},{8,0},{16,24},{24,16},{1,9},{9,1},{17,25},{25,17},{2,10},{10... | collective-permute-start | bytes 3145736 | tf_op jit(solution)/shard_map/ppermute | solution.py:205
  191.4 46.7 %copy-start.24 = (bf16[512,512]{1,0:T(8,128)(2,1)S(1)}, bf16[512,512]{1,0:T(8,128)(2,1)}, u32[]{:S(2)}) copy-start(bf16[512,512]{1,0:T(8,128)(2,1)} %copy-done.23) | copy-start | bytes 1572868
  192.3 91.4 %all-gather.9.cloned.1.call-start = ((), (), s32[]{:S(2)}) async-start(), calls=%async_computation.11 | async-start | bytes 4718592 | tf_op jit(solution)/shard_map/all_gather | solution.py:305
  192.4 37.1 %collective-permute-start.20 = (bf16[8,64,1024]{2,1,0:T(8,128)(2,1)}, bf16[8,64,1024]{2,1,0:T(8,128)(2,1)}, u32[]{:S(2)}, u32[]{:S(2)}) collective-permute-start(bf16[8,64,1024]{2,1,0:T(8,128)(2,1)} %collective-permute-done.16.refs_1_), channel_id=1, source_target_pairs={{0,16},{8,24},{16,0},{24,8},{1,17},{9,25},{17,1},{25,9},{2,18},{10... | collective-permute-start | bytes 3145736 | tf_op jit(solution)/shard_map/ppermute | solution.py:205
  193.9 35.6 %collective-permute-start.21 = (bf16[8,64,1024]{2,1,0:T(8,128)(2,1)}, bf16[8,64,1024]{2,1,0:T(8,128)(2,1)}, u32[]{:S(2)}, u32[]{:S(2)}) collective-permute-start(bf16[8,64,1024]{2,1,0:T(8,128)(2,1)} %collective-permute-done.18.refs_6_), channel_id=1, source_target_pairs={{0,8},{8,0},{16,24},{24,16},{1,9},{9,1},{17,25},{25,17},{2,10},{10... | collective-permute-start | bytes 3145736 | tf_op jit(solution)/shard_map/ppermute | solution.py:205
  194.4 33.8 %collective-permute-start.22 = (bf16[512,512]{1,0:T(8,128)(2,1)}, bf16[512,512]{1,0:T(8,128)(2,1)}, u32[]{:S(2)}, u32[]{:S(2)}) collective-permute-start(bf16[512,512]{1,0:T(8,128)(2,1)} %copy-done.23), channel_id=1, source_target_pairs={{0,16},{8,24},{16,0},{24,8},{1,17},{9,25},{17,1},{25,9},{2,18},{10... | collective-permute-start | bytes 1572872 | tf_op jit(solution)/shard_map/ppermute | solution.py:205
  195.1 34.3 %collective-permute-start.23 = (bf16[512,512]{1,0:T(8,128)(2,1)}, bf16[512,512]{1,0:T(8,128)(2,1)}, u32[]{:S(2)}, u32[]{:S(2)}) collective-permute-start(bf16[512,512]{1,0:T(8,128)(2,1)} %collective-permute-done.15), channel_id=1, source_target_pairs={{0,8},{8,0},{16,24},{24,16},{1,9},{9,1},{17,25},{25,17},{2,10},{10... | collective-permute-start | bytes 1572872 | tf_op jit(solution)/shard_map/ppermute | solution.py:205
  236.6 98.0 %reduce-scatter.7.cloned.1.call-start = ((), (), s32[]{:S(2)}) async-start(), calls=%async_computation.12 | async-start | bytes 4718592 | tf_op jit(solution)/shard_map/reduce_scatter | solution.py:309
  283.8 102.0 %reduce-scatter.9.cloned.1.call-start = ((), (), s32[]{:S(2)}) async-start(), calls=%async_computation.13 | async-start | bytes 4718592 | tf_op jit(solution)/shard_map/reduce_scatter | solution.py:309
  336.8 105.7 %all-gather.11.cloned.1.call-start = ((), (), s32[]{:S(2)}) async-start(), calls=%async_computation.14 | async-start | bytes 4718592 | tf_op jit(solution)/shard_map/all_gather | solution.py:305
  347.1 40.0 %collective-permute-start.24 = (bf16[8,64,1024]{2,1,0:T(8,128)(2,1)}, bf16[8,64,1024]{2,1,0:T(8,128)(2,1)}, u32[]{:S(2)}, u32[]{:S(2)}) collective-permute-start(bf16[8,64,1024]{2,1,0:T(8,128)(2,1)} %dynamic-slice_bitcast_fusion.3), channel_id=1, source_target_pairs={{0,8},{8,0},{16,24},{24,16},{1,9},{9,1},{17,25},{25,17},{2,10},{10... | collective-permute-start | bytes 3145736 | tf_op jit(solution)/shard_map/ppermute | solution.py:205
  356.6 30.5 %collective-permute-start.25 = (bf16[8,64,1024]{2,1,0:T(8,128)(2,1)}, bf16[8,64,1024]{2,1,0:T(8,128)(2,1)}, u32[]{:S(2)}, u32[]{:S(2)}) collective-permute-start(bf16[8,64,1024]{2,1,0:T(8,128)(2,1)} %dynamic-slice_bitcast_fusion.2), channel_id=1, source_target_pairs={{0,16},{8,24},{16,0},{24,8},{1,17},{9,25},{17,1},{25,9},{2,18},{10... | collective-permute-start | bytes 3145736 | tf_op jit(solution)/shard_map/ppermute | solution.py:205
  358.1 30.6 %copy-start.21 = (bf16[1,128,2048]{2,1,0:T(8,128)(2,1)S(1)}, bf16[1,128,2048]{2,1,0:T(8,128)(2,1)}, u32[]{:S(2)}) copy-start(bf16[1,128,2048]{2,1,0:T(8,128)(2,1)} %param.15) | copy-start | bytes 1572868
  392.8 26.1 %collective-permute-start.27 = (bf16[8,64,1024]{2,1,0:T(8,128)(2,1)S(1)}, bf16[8,64,1024]{2,1,0:T(8,128)(2,1)S(1)}, u32[]{:S(2)}, u32[]{:S(2)}) collective-permute-start(bf16[8,64,1024]{2,1,0:T(8,128)(2,1)S(1)} %fusion.8), channel_id=1, source_target_pairs={{0,16},{8,24},{16,0},{24,8},{1,17},{9,25},{17,1},{25,9},{2,18},{10... | collective-permute-start | bytes 3145736 | tf_op jit(solution)/shard_map/ppermute | solution.py:205
  395.6 26.1 %collective-permute-start.26 = (bf16[8,64,1024]{2,1,0:T(8,128)(2,1)S(1)}, bf16[8,64,1024]{2,1,0:T(8,128)(2,1)S(1)}, u32[]{:S(2)}, u32[]{:S(2)}) collective-permute-start(bf16[8,64,1024]{2,1,0:T(8,128)(2,1)S(1)} %dynamic-slice_bitcast_fusion.1), channel_id=1, source_target_pairs={{0,8},{8,0},{16,24},{24,16},{1,9},{9,1},{17,25},{25,17},{2,10},{10... | collective-permute-start | bytes 3145736 | tf_op jit(solution)/shard_map/ppermute | solution.py:205
  399.0 41.9 %collective-permute-start.29 = (bf16[8,64,1024]{2,1,0:T(8,128)(2,1)S(1)}, bf16[8,64,1024]{2,1,0:T(8,128)(2,1)S(1)}, u32[]{:S(2)}, u32[]{:S(2)}) collective-permute-start(bf16[8,64,1024]{2,1,0:T(8,128)(2,1)S(1)} %fusion.5), channel_id=1, source_target_pairs={{0,8},{8,0},{16,24},{24,16},{1,9},{9,1},{17,25},{25,17},{2,10},{10... | collective-permute-start | bytes 3145736 | tf_op jit(solution)/shard_map/ppermute | solution.py:205
  399.6 41.3 %collective-permute-start.28 = (bf16[8,64,1024]{2,1,0:T(8,128)(2,1)S(1)}, bf16[8,64,1024]{2,1,0:T(8,128)(2,1)S(1)}, u32[]{:S(2)}, u32[]{:S(2)}) collective-permute-start(bf16[8,64,1024]{2,1,0:T(8,128)(2,1)S(1)} %dynamic-slice_bitcast_fusion), channel_id=1, source_target_pairs={{0,16},{8,24},{16,0},{24,8},{1,17},{9,25},{17,1},{25,9},{2,18},{10... | collective-permute-start | bytes 3145736 | tf_op jit(solution)/shard_map/ppermute | solution.py:205
  445.6 58.8 %all-to-all-start.2 = ((bf16[8,2,64,1024]{3,2,1,0:T(8,128)(2,1)}), bf16[8,2,64,1024]{3,2,1,0:T(8,128)(2,1)}, u32[]{:S(2)}, u32[]{:S(2)}) async-start(bf16[8,2,64,1024]{3,2,1,0:T(8,128)(2,1)} %pad_maximum_fusion), calls=%async_computation.5 | async-start | bytes 4194304 | tf_op jit(solution)/shard_map/all_to_all | solution.py:301
  450.0 152.1 %reduce-scatter.11.cloned.1.call-start = ((), (), s32[]{:S(2)}) async-start(), calls=%async_computation.15 | async-start | bytes 4718592 | tf_op jit(solution)/shard_map/reduce_scatter | solution.py:309
  452.5 27.0 %collective-permute-start.32 = (bf16[1024,512]{1,0:T(8,128)(2,1)S(1)}, bf16[1024,512]{1,0:T(8,128)(2,1)S(1)}, u32[]{:S(2)}, u32[]{:S(2)}) collective-permute-start(bf16[1024,512]{1,0:T(8,128)(2,1)S(1)} %get-tuple-element.142), channel_id=1, source_target_pairs={{0,24},{8,16},{16,8},{24,0},{1,25},{9,17},{17,9},{25,1},{2,26},{10... | collective-permute-start | bytes 3145736 | tf_op jit(solution)/shard_map/ppermute | solution.py:205
  454.0 47.3 %collective-permute-start.31 = (bf16[1024,512]{1,0:T(8,128)(2,1)S(1)}, bf16[1024,512]{1,0:T(8,128)(2,1)S(1)}, u32[]{:S(2)}, u32[]{:S(2)}) collective-permute-start(bf16[1024,512]{1,0:T(8,128)(2,1)S(1)} %get-tuple-element.143), channel_id=1, source_target_pairs={{0,16},{8,24},{16,0},{24,8},{1,17},{9,25},{17,1},{25,9},{2,18},{10... | collective-permute-start | bytes 3145736 | tf_op jit(solution)/shard_map/ppermute | solution.py:205
  455.5 45.8 %collective-permute-start.30 = (bf16[1024,512]{1,0:T(8,128)(2,1)S(1)}, bf16[1024,512]{1,0:T(8,128)(2,1)S(1)}, u32[]{:S(2)}, u32[]{:S(2)}) collective-permute-start(bf16[1024,512]{1,0:T(8,128)(2,1)S(1)} %get-tuple-element.141), channel_id=1, source_target_pairs={{0,8},{8,0},{16,24},{24,16},{1,9},{9,1},{17,25},{25,17},{2,10},{10... | collective-permute-start | bytes 3145736 | tf_op jit(solution)/shard_map/ppermute | solution.py:205
  509.6 21.2 %collective-permute-start.35 = (bf16[8,64,384]{2,1,0:T(8,128)(2,1)S(1)}, bf16[8,64,384]{2,1,0:T(8,128)(2,1)S(1)}, u32[]{:S(2)}, u32[]{:S(2)}) collective-permute-start(bf16[8,64,384]{2,1,0:T(8,128)(2,1)S(1)} %get-tuple-element.155), channel_id=1, source_target_pairs={{0,24},{8,16},{16,8},{24,0},{1,25},{9,17},{17,9},{25,1},{2,26},{10... | collective-permute-start | bytes 1179656 | tf_op jit(solution)/shard_map/ppermute | solution.py:205
  511.1 20.3 %collective-permute-start.34 = (bf16[8,64,384]{2,1,0:T(8,128)(2,1)S(1)}, bf16[8,64,384]{2,1,0:T(8,128)(2,1)}, u32[]{:S(2)}, u32[]{:S(2)}) collective-permute-start(bf16[8,64,384]{2,1,0:T(8,128)(2,1)S(1)} %get-tuple-element.156), channel_id=1, source_target_pairs={{0,16},{8,24},{16,0},{24,8},{1,17},{9,25},{17,1},{25,9},{2,18},{10... | collective-permute-start | bytes 1179656 | tf_op jit(solution)/shard_map/ppermute | solution.py:205
  511.9 21.1 %collective-permute-start.33 = (bf16[8,64,384]{2,1,0:T(8,128)(2,1)S(1)}, bf16[8,64,384]{2,1,0:T(8,128)(2,1)}, u32[]{:S(2)}, u32[]{:S(2)}) collective-permute-start(bf16[8,64,384]{2,1,0:T(8,128)(2,1)S(1)} %get-tuple-element.154), channel_id=1, source_target_pairs={{0,8},{8,0},{16,24},{24,16},{1,9},{9,1},{17,25},{25,17},{2,10},{10... | collective-permute-start | bytes 1179656 | tf_op jit(solution)/shard_map/ppermute | solution.py:205
  514.9 10.7 %all-to-all-start.4 = ((f32[8,2,256]{2,1,0:T(2,128)}), f32[8,2,256]{2,1,0:T(2,128)S(1)}, u32[]{:S(2)}, u32[]{:S(2)}) async-start(f32[8,2,256]{2,1,0:T(2,128)} %maximum_bitcast_fusion.1), calls=%async_computation.8 | async-start | bytes 32768 | tf_op jit(solution)/shard_map/all_to_all | solution.py:301
  525.7 3.6 collective-permute-start.45
  526.6 15.4 %collective-permute-start.41 = (bf16[256,512]{1,0:T(8,128)(2,1)S(1)}, bf16[256,512]{1,0:T(8,128)(2,1)}, u32[]{:S(2)}, u32[]{:S(2)}) collective-permute-start(bf16[256,512]{1,0:T(8,128)(2,1)S(1)} %get-tuple-element.159), channel_id=1, source_target_pairs={{0,24},{8,16},{16,8},{24,0},{1,25},{9,17},{17,9},{25,1},{2,26},{10... | collective-permute-start | bytes 786440 | tf_op jit(solution)/shard_map/ppermute | solution.py:205
  529.3 12.7 %collective-permute-start.40 = (bf16[256,512]{1,0:T(8,128)(2,1)S(1)}, bf16[256,512]{1,0:T(8,128)(2,1)}, u32[]{:S(2)}, u32[]{:S(2)}) collective-permute-start(bf16[256,512]{1,0:T(8,128)(2,1)S(1)} %get-tuple-element.160), channel_id=1, source_target_pairs={{0,16},{8,24},{16,0},{24,8},{1,17},{9,25},{17,1},{25,9},{2,18},{10... | collective-permute-start | bytes 786440 | tf_op jit(solution)/shard_map/ppermute | solution.py:205
  530.8 11.2 %collective-permute-start.39 = (bf16[256,512]{1,0:T(8,128)(2,1)S(1)}, bf16[256,512]{1,0:T(8,128)(2,1)S(1)}, u32[]{:S(2)}, u32[]{:S(2)}) collective-permute-start(bf16[256,512]{1,0:T(8,128)(2,1)S(1)} %get-tuple-element.158), channel_id=1, source_target_pairs={{0,8},{8,0},{16,24},{24,16},{1,9},{9,1},{17,25},{25,17},{2,10},{10... | collective-permute-start | bytes 786440 | tf_op jit(solution)/shard_map/ppermute | solution.py:205
  531.4 10.0 %collective-permute-start.46 = (f32[2,256]{1,0:T(2,128)S(1)}, f32[2,256]{1,0:T(2,128)S(1)}, u32[]{:S(2)}, u32[]{:S(2)}) collective-permute-start(f32[2,256]{1,0:T(2,128)S(1)} %add.236), channel_id=1, source_target_pairs={{0,16},{8,24},{16,0},{24,8},{1,17},{9,25},{17,1},{25,9},{2,18},{10... | collective-permute-start | bytes 6152 | tf_op jit(solution)/shard_map/ppermute | solution.py:205
  535.2 24.8 %all-to-all-start.3 = ((bf16[8,64,384]{2,1,0:T(8,128)(2,1)}), bf16[8,64,384]{2,1,0:T(8,128)(2,1)S(1)}, u32[]{:S(2)}, u32[]{:S(2)}) async-start(bf16[8,64,384]{2,1,0:T(8,128)(2,1)} %fusion.25), calls=%async_computation.7 | async-start | bytes 786432 | tf_op jit(solution)/shard_map/all_to_all | solution.py:301
  561.8 5.3 collective-permute-start.36
  562.5 7.1 %collective-permute-start.37 = (bf16[64,768]{1,0:T(8,128)(2,1)S(1)}, bf16[64,768]{1,0:T(8,128)(2,1)S(1)}, u32[]{:S(2)}, u32[]{:S(2)}) collective-permute-start(bf16[64,768]{1,0:T(8,128)(2,1)S(1)} %bitcast.226), channel_id=1, source_target_pairs={{0,16},{8,24},{16,0},{24,8},{1,17},{9,25},{17,1},{25,9},{2,18},{10... | collective-permute-start | bytes 294920 | tf_op jit(solution)/shard_map/ppermute | solution.py:205
  564.0 7.8 %collective-permute-start.38 = (bf16[64,768]{1,0:T(8,128)(2,1)S(1)}, bf16[64,768]{1,0:T(8,128)(2,1)S(1)}, u32[]{:S(2)}, u32[]{:S(2)}) collective-permute-start(bf16[64,768]{1,0:T(8,128)(2,1)S(1)} %bitcast.225), channel_id=1, source_target_pairs={{0,24},{8,16},{16,8},{24,0},{1,25},{9,17},{17,9},{25,1},{2,26},{10... | collective-permute-start | bytes 294920 | tf_op jit(solution)/shard_map/ppermute | solution.py:205
  569.4 14.9 %collective-permute-start.42 = (bf16[4,64,1024]{2,1,0:T(8,128)(2,1)S(1)}, bf16[4,64,1024]{2,1,0:T(8,128)(2,1)S(1)}, u32[]{:S(2)}, u32[]{:S(2)}) collective-permute-start(bf16[4,64,1024]{2,1,0:T(8,128)(2,1)S(1)} %get-tuple-element.146), channel_id=1, source_target_pairs={{0,8},{8,0},{16,24},{24,16},{1,9},{9,1},{17,25},{25,17},{2,10},{10... | collective-permute-start | bytes 1572872 | tf_op jit(solution)/shard_map/ppermute | solution.py:205
  569.6 23.4 %collective-permute-start.43 = (bf16[4,64,1024]{2,1,0:T(8,128)(2,1)S(1)}, bf16[4,64,1024]{2,1,0:T(8,128)(2,1)S(1)}, u32[]{:S(2)}, u32[]{:S(2)}) collective-permute-start(bf16[4,64,1024]{2,1,0:T(8,128)(2,1)S(1)} %get-tuple-element.145), channel_id=1, source_target_pairs={{0,16},{8,24},{16,0},{24,8},{1,17},{9,25},{17,1},{25,9},{2,18},{10... | collective-permute-start | bytes 1572872 | tf_op jit(solution)/shard_map/ppermute | solution.py:205
  571.8 21.2 %collective-permute-start.44 = (bf16[4,64,1024]{2,1,0:T(8,128)(2,1)S(1)}, bf16[4,64,1024]{2,1,0:T(8,128)(2,1)S(1)}, u32[]{:S(2)}, u32[]{:S(2)}) collective-permute-start(bf16[4,64,1024]{2,1,0:T(8,128)(2,1)S(1)} %get-tuple-element.144), channel_id=1, source_target_pairs={{0,24},{8,16},{16,8},{24,0},{1,25},{9,17},{17,9},{25,1},{2,26},{10... | collective-permute-start | bytes 1572872 | tf_op jit(solution)/shard_map/ppermute | solution.py:205
  (29 other events, 212.6 us)
Sparse Core Ops, SparseCore 0:
  9.6 64.7 all-gather.12
  137.6 47.9 reduce-scatter.4
  192.5 44.0 all-gather.6
  238.1 45.6 all-gather.8
  285.9 48.7 reduce-scatter.6
  337.4 48.3 reduce-scatter.8
  390.8 45.3 all-gather.10
  504.6 56.6 reduce-scatter.10

commit v3 on v2

--- a/solution.py
+++ b/solution.py
@@ -269,25 +269,33 @@
         return lax.psum_scatter(
             partial.astype(BF16), "dp", scatter_dimension=axis, tiled=partial.ndim == 2
         )
-    return send(dp_block(partial, 3, axis).astype(BF16), first)
+    return tuple(send(dp_block(partial, mask, axis).astype(BF16), first) for mask in (3, first))
 
 
 def scatter_second(partial, got, axis, first):
     if lax.axis_size("dp") != 4:
         return got.astype(F32)
-    beside = send(dp_block(partial, first, axis).astype(BF16), first)
-    passed = dp_block(partial, other(first), axis).astype(F32) + got.astype(F32)
+    far, beside = got
+    passed = dp_block(partial, other(first), axis).astype(F32) + far.astype(F32)
     last = send(passed.astype(BF16), other(first))
     own = dp_block(partial, 0, axis).astype(F32)
     return own + beside.astype(F32) + last.astype(F32)
 
 
+def scatter_begin(partial, axis):
+    if lax.axis_size("dp") != 4:
+        return scatter_first(partial, axis, 1)
+    return tuple(send(dp_block(partial, mask, axis).astype(BF16), mask) for mask in (1, 2, 3))
+
+
+def scatter_end(partial, got, axis):
+    if lax.axis_size("dp") != 4:
+        return got.astype(F32)
+    return sum((part.astype(F32) for part in got), dp_block(partial, 0, axis).astype(F32))
+
+
 def scatter_direct(partial, axis):
-    if lax.axis_size("dp") != 4:
-        return scatter_second(partial, scatter_first(partial, axis, 1), axis, 1)
-    own = dp_block(partial, 0, axis).astype(F32)
-    parts = [send(dp_block(partial, mask, axis).astype(BF16), mask) for mask in (1, 2, 3)]
-    return own + parts[0].astype(F32) + parts[1].astype(F32) + parts[2].astype(F32)
+    return scatter_end(partial, scatter_begin(partial, axis), axis)
 
 
 def swap_dp(blocks):
@@ -312,7 +320,7 @@
 
 
 def gate_up_kernel(me_ref, x_ref, *refs):
-    pieces, (gate_ref, up_ref, whole_out, whole, sems, out_sem) = refs[:8], refs[8:]
+    pieces, (gate_ref, up_ref, *wholes, whole, sems, out_sems) = refs[:8], refs[8:]
     me = me_ref[0]
     sub, ff = pieces[0].shape[1:]
     copies = []
@@ -325,8 +333,11 @@
         copy.start()
     for copy in copies:
         copy.wait()
-    write = pltpu.make_async_copy(whole, whole_out, out_sem)
-    write.start()
+    writes = [
+        pltpu.make_async_copy(whole.at[part], wholes[part], out_sems.at[part]) for part in range(2)
+    ]
+    for write in writes:
+        write.start()
     depth = whole.shape[1] * whole.shape[2] * sub
     tile = min(512, ff)
     rows = min(256, x_ref.shape[0])
@@ -341,7 +352,8 @@
                     x_ref[span, :], whole[part, :, :, :, lanes].reshape(depth, tile)
                 )
 
-    write.wait()
+    for write in writes:
+        write.wait()
 
 
 def gate_up_of(normed2, pieces):
@@ -354,13 +366,13 @@
     me = lax.axis_index("dp").astype(jnp.int32).reshape(1)
     return pl.pallas_call(
         gate_up_kernel,
-        out_shape=(shape((slots, ff), F32), shape((slots, ff), F32), shape(whole, BF16)),
+        out_shape=(shape((slots, ff), F32),) * 2 + (shape(whole[1:], BF16),) * 2,
         in_specs=[pl.BlockSpec(memory_space=pltpu.SMEM), full] + [away] * len(pieces),
-        out_specs=(full, full, away),
+        out_specs=(full, full, away, away),
         scratch_shapes=[
             pltpu.VMEM(whole, BF16),
             pltpu.SemaphoreType.DMA((len(pieces),)),
-            pltpu.SemaphoreType.DMA,
+            pltpu.SemaphoreType.DMA((2,)),
         ],
         compiler_params=pltpu.CompilerParams(vmem_limit_bytes=56 << 20),
         cost_estimate=pl.CostEstimate(
@@ -382,7 +394,6 @@
 
     first_slot = lax.axis_index("seq") * tok_rows
     length = lengths[0]
-    valid = (jnp.arange(slots, dtype=jnp.int32) < length).astype(F32)[:, None]
     valid_rows = ((first_slot + jnp.arange(tok_rows)) < length).astype(F32)[:, None]
     cosine, sine = rotary_pair(slots)
 
@@ -412,18 +423,24 @@
     all_tokens = gather_seq(tokens[0])
     qkv_rows = swap_dp(w_qkv.reshape(ranks, sub, -1)).transpose(1, 0, 2).reshape(sub, -1)
     per_block = w_gate_up.shape[1] // ff
+    qkv_rows, w_gate_up = tie((qkv_rows, w_gate_up))
     gu_rows = swap_dp(
         w_gate_up.reshape(ranks, sub, per_block, ff).transpose(0, 2, 1, 3)
     ).reshape(2, seqs, sub, ff)
-    qkv_mine = exchange(split_qkv(qkv_rows), "seq")
-    qkv_mine, gu_rows = tie((qkv_mine, gu_rows))
+    def with_gains(blocks, pair):
+        rows = jnp.pad(pair, ((0, 0), (0, 6), (0, blocks.shape[2] - pair.shape[2])))
+        return jnp.concatenate([blocks, rows.astype(BF16)], axis=1)
+
+    gain_rows = jnp.broadcast_to(gains.T, (seqs, 2, gains.shape[0]))
+    qkv_got = exchange(with_gains(split_qkv(qkv_rows), gain_rows), "seq")
+    qkv_got, gu_rows = tie((qkv_got, gu_rows))
     gu_mine = exchange(gu_rows.transpose(1, 0, 2, 3), "seq")
-    all_tokens, late_gains = tie((all_tokens, gains.T.reshape(1, -1)))
-    all_gains = gather_seq(late_gains).reshape(seqs, 2, -1).transpose(1, 0, 2)
+    qkv_mine = qkv_got[:, :sub]
+    all_gains = qkv_got[:, sub : sub + 2, : gains.shape[0]].transpose(1, 0, 2)
     all_gains = all_gains.reshape(2, width).astype(F32)
     gain_first, gain_second = all_gains[0], all_gains[1]
     my_qkv = gather_direct(qkv_mine[:, None], 1).reshape(width, q_width + PAIR)
-    my_qkv, w_out, w_down = tie((my_qkv, w_out, w_down))
+    all_tokens, my_qkv, w_out, w_down = tie((all_tokens, my_qkv, w_out, w_down))
     my_out = gather_direct(w_out, 1)
     down_near = gather_halves(w_down, None)
 
@@ -445,10 +462,11 @@
     inv_second = lax.rsqrt(jnp.mean(hidden * hidden, axis=1, keepdims=True) + EPSILON)
     unit_second = hidden * inv_second
     normed2 = gather_seq((unit_second * gain_second).astype(BF16))
-    normed2, gate_far, up_far, down_far, late_cotangent = tie(
-        (normed2, gate_far, up_far, down_far, cotangent[0])
-    )
-    all_cotangent = gather_seq(late_cotangent)
+    upstream = cotangent[0].astype(F32) * valid_rows
+    normed2, gate_far, up_far, down_far, late_grad = tie(
+        (normed2, gate_far, up_far, down_far, (RESIDUAL_SCALE * upstream).astype(BF16))
+    )
+    down_grad = gather_seq(late_grad)
     my_down = join_halves(w_down, down_near, down_far, 1)
 
     if gate_near is None:
@@ -458,74 +476,80 @@
         gate_vals, up_vals = dot(normed2, my_gate), dot(normed2, my_up)
     else:
         pieces = (gate_mine, *gate_near, gate_far, up_mine, up_near[1], up_near[0], up_far)
-        gate_vals, up_vals, my_gate_up = gate_up_of(normed2, pieces)
-        my_gate, my_up = (my_gate_up[part].reshape(width, ff) for part in range(2))
+        gate_vals, up_vals, *wholes = gate_up_of(normed2, pieces)
+        my_gate, my_up = (whole.reshape(width, ff) for whole in wholes)
     sigmoid_gate = jax.nn.sigmoid(gate_vals)
     mixed = (gate_vals * sigmoid_gate * up_vals).astype(BF16)
     down_sum = dot(mixed, my_down).astype(BF16)
-    all_cotangent, down_sum = tie((all_cotangent, down_sum))
+    down_grad, down_sum = tie((down_grad, down_sum))
     down_out = scatter_seq(down_sum)
-    down_grad = (RESIDUAL_SCALE * (all_cotangent.astype(F32) * valid)).astype(BF16)
+    down_partial = dot_tn(mixed, down_grad).astype(BF16)
+    down_grad, down_partial = tie((down_grad, down_partial))
+    down_got = scatter_begin(down_partial, 1)
     mixed_grad = dot_nt(down_grad, my_down)
     gate_grad = (
         mixed_grad * up_vals * sigmoid_gate * (1.0 + gate_vals * (1.0 - sigmoid_gate))
     ).astype(BF16)
     up_grad = (mixed_grad * gate_vals * sigmoid_gate).astype(BF16)
     normed2_sum = (dot_nt(gate_grad, my_gate) + dot_nt(up_grad, my_up)).astype(BF16)
-    normed2_sum, down_out = tie((normed2_sum, down_out))
+
+    gate_partial = dot_tn(normed2, gate_grad).astype(BF16).reshape(seqs, ranks, sub, ff)
+    up_partial = dot_tn(normed2, up_grad).astype(BF16).reshape(seqs, ranks, sub, ff)
+    normed2_sum, down_out, gate_partial, up_partial, down_got = tie(
+        (normed2_sum, down_out, gate_partial, up_partial, down_got)
+    )
     normed2_grad = scatter_seq(normed2_sum)
-
-    gate_partial = dot_tn(normed2, gate_grad).astype(BF16).reshape(seqs, ranks, sub, ff)
     gate_got = scatter_first(gate_partial, 1, 1)
-    up_partial = dot_tn(normed2, up_grad).astype(BF16).reshape(seqs, ranks, sub, ff)
     up_got = scatter_first(up_partial, 1, 2)
-    down_partial = dot_tn(mixed, down_grad).astype(BF16)
-    normed2_grad, gate_partial, up_partial, gate_got, up_got, down_partial = tie(
-        (normed2_grad, gate_partial, up_partial, gate_got, up_got, down_partial)
-    )
-
-    upstream = cotangent[0].astype(F32) * valid_rows
+    normed2_grad, gate_got, up_got = tie((normed2_grad, gate_got, up_got))
+
     unit_grad2 = normed2_grad * gain_second
     hidden_grad = upstream + inv_second * (
         unit_grad2 - unit_second * jnp.mean(unit_grad2 * unit_second, axis=1, keepdims=True)
     )
     gain_second_term = jnp.sum(normed2_grad * unit_second, axis=0)
     branch_grad = gather_seq((RESIDUAL_SCALE * hidden_grad).astype(BF16))
-    gate_summed = scatter_second(gate_partial, gate_got, 1, 1).astype(BF16)
-    up_summed = scatter_second(up_partial, up_got, 1, 2).astype(BF16)
-    branch_grad, gate_summed, up_summed, down_partial = tie(
-        (branch_grad, gate_summed, up_summed, down_partial)
-    )
-    gu_blocks = exchange(jnp.stack([gate_summed, up_summed], axis=1), "seq")
-    grad_down = scatter_direct(down_partial, 1)
+    gu_summed = jnp.stack(
+        [
+            scatter_second(gate_partial, gate_got, 1, 1).astype(BF16),
+            scatter_second(up_partial, up_got, 1, 2).astype(BF16),
+        ],
+        axis=1,
+    )
+    gu_summed, down_partial = tie((gu_summed, down_partial))
+    grad_down = scatter_end(down_partial, down_got, 1)
+    branch_grad, gu_summed = tie((branch_grad, gu_summed))
+    gu_blocks = exchange(gu_summed, "seq")
 
     attended_grad = dot_nt(branch_grad, my_out).astype(BF16)
     qkv_grad = attend_back(saved, attended_grad, cosine, sine, lengths)
     normed_partial = dot_nt(qkv_grad, my_qkv)
-    normed_sum, gu_blocks, grad_down = tie((normed_partial.astype(BF16), gu_blocks, grad_down))
-    normed_grad = scatter_seq(normed_sum)
-
-    qkv_grad, attended, normed_partial = tie((qkv_grad, attended, normed_partial))
     qkv_partial = dot_tn(normed, qkv_grad).astype(BF16).reshape(seqs, ranks, sub, -1)
     qkv_summed = scatter_direct(qkv_partial, 1).astype(BF16)
     out_partial = dot_tn(attended, branch_grad).astype(BF16)
+    unit_all = x_all * inv_all
+    gain_first_term = jnp.sum(normed_partial * unit_all, axis=0)
+    gains_term = jnp.stack([gain_first_term, gain_second_term]).reshape(2, seqs, -1)
+    qkv_blocks = with_gains(qkv_summed, gains_term.transpose(1, 0, 2))
     grad_out = scatter_direct(out_partial, 1)
-    qkv_back = join_qkv(exchange(qkv_summed, "seq"))
+    normed_sum, gu_blocks, grad_down, qkv_blocks, grad_out = tie(
+        (normed_partial.astype(BF16), gu_blocks, grad_down, qkv_blocks, grad_out)
+    )
+    normed_grad = scatter_seq(normed_sum)
+    gu_back = swap_dp(
+        gu_blocks.transpose(1, 0, 2, 3).reshape(ranks, per_block, sub, ff)
+    )
+    qkv_back, gu_back = tie((exchange(qkv_blocks, "seq"), gu_back))
+    gain_blocks = qkv_back[:, sub : sub + 2, : gains.shape[0]]
+    qkv_back = join_qkv(qkv_back[:, :sub])
     grad_qkv = (
         swap_dp(qkv_back.reshape(sub, ranks, -1).transpose(1, 0, 2))
         .reshape(w_qkv.shape)
         .astype(F32)
     )
-    gu_back = swap_dp(
-        gu_blocks.transpose(1, 0, 2, 3).reshape(ranks, per_block, sub, ff)
-    )
     grad_gate_up = gu_back.transpose(0, 2, 1, 3).reshape(w_gate_up.shape).astype(F32)
 
-    unit_all = x_all * inv_all
-    gain_first_term = jnp.sum(normed_partial * unit_all, axis=0)
-    gains_term = jnp.stack([gain_first_term, gain_second_term]).reshape(2, seqs, -1)
-    gain_blocks = exchange(gains_term.transpose(1, 0, 2), "seq")
-    grad_gains = jnp.sum(gain_blocks, axis=0)
+    grad_gains = jnp.sum(gain_blocks.astype(F32), axis=0)
     if ranks == 4:
         grad_gains = grad_gains + send(grad_gains, 1)
         grad_gains = (grad_gains + send(grad_gains, 2)).T

time: 619 us -> 571 us (0.922)
  blocking collectives: 17 us -> 0 us
  waiting for transfers between devices: 270 us -> 255 us
  starting transfers between devices: 83 us -> 72.2 us
    ppermute x47, waiting for transfers between devices: 149 us -> 126 us  [send(): return lax.ppermute(value, 'dp', flip(mask, lax.axis_size('dp')))]
    all_gather x1 -> x0, blocking collectives: 17 us -> none  [gather_seq(): return lax.all_gather(shard, 'seq', axis=0, tiled=True)]
    all_to_all x5 -> x4, waiting for transfers between devices: 24.5 us -> 8.82 us  [exchange(): lax.all_to_all(blocks, axis_name, split_axis=0, concat_axis=0, tiled=True)]
    all_gather x4, waiting for transfers between devices: 16.3 us -> 30 us  [gather_seq(): return lax.all_gather(shard, 'seq', axis=0, tiled=True)]
    reduce_scatter x4, waiting for transfers between devices: 78.9 us -> 89.3 us  [scatter_seq(): lax.psum_scatter(partial.astype(BF16), 'seq', scatter_dimension=0, tiled=...]
    slice x1 -> x0, local copies, waits for them, and re-layouts: 7.28 us -> none  [local(): my_gate, my_up = (my_gate_up[part].reshape(width, ff) for part in range(2))]
    all_to_all x5 -> x4, starting transfers between devices: 24.5 us -> 18.7 us  [exchange(): lax.all_to_all(blocks, axis_name, split_axis=0, concat_axis=0, tiled=True)]
    unnamed x73 -> x65, local copies, waits for them, and re-layouts: 15.2 us -> 11 us
  transfers between devices with their start and end apart: 60 -> 59, of which waited for: 26 -> 26; matrix products, arithmetic and copies ran while one was open for 26% -> 29% of each run, Pallas kernels for 7% -> 7%
where the time goes in v3:
time: 571 us; the launch traced here: 565 us
  waiting for transfers between devices  255 us (45%)
  starting transfers between devices  72.2 us (13%)
  matrix products  71.5 us (13%)
  local copies, waits for them, and re-layouts  55.8 us (10%)
  other arithmetic  54.3 us (10%)
  Pallas kernels  40.9 us (7%)
  between operations  16 us (3%)
    ppermute x47, waiting for transfers between devices, send(): return lax.ppermute(value, 'dp', flip(mask, lax.axis_size('dp')))  126 us
    reduce_scatter x4, waiting for transfers between devices, scatter_seq(): lax.psum_scatter(partial.astype(BF16), 'seq', scatter_dimension=0, tiled=...  89.3 us
    ppermute x47, starting transfers between devices, send(): return lax.ppermute(value, 'dp', flip(mask, lax.axis_size('dp')))  52.8 us
    all_gather x4, waiting for transfers between devices, gather_seq(): return lax.all_gather(shard, 'seq', axis=0, tiled=True)  30 us
    dot_general x5, matrix products, dot_nt(): lax.dot_general(left, right, (((1,), (1,)), ((), ())), preferred_element_...  29.4 us
    dot_general x5, matrix products, dot_tn(): lax.dot_general(left, right, (((0,), (0,)), ((), ())), preferred_element_...  27.5 us
    pallas_call x1, Pallas kernels, gate_up_of(): pl.pallas_call(gate_up_kernel, out_shape=(shape((slots, ff), F32),) * 2 +...  20 us
    all_to_all x4, starting transfers between devices, exchange(): lax.all_to_all(blocks, axis_name, split_axis=0, concat_axis=0, tiled=True)  18.7 us
  transfers between devices with their start and end apart: 59, of which 26 were waited for; matrix products, arithmetic and copies ran while one was open for 29% of the time, Pallas kernels for 7%

profile of v3, /device:TPU:0, one launch (start us, length us, event | category | flops | bytes accessed | tf_op | source)
XLA Modules:
  0.0 565.1 jit_solution(17760023069682007865)
XLA Ops:
  9.0 4.0 collective-permute-start.2
  15.0 3.2 collective-permute-done
  18.4 3.5 reshape.149
  21.9 1.7 dynamic-slice_bitcast_fusion.7
  26.9 5.0 all-to-all-start
  33.8 4.1 collective-permute-done.3
  39.2 11.0 %collective-permute-done.4 = bf16[4,64,1024]{2,0,1:T(4,128)(2,1)} collective-permute-done((bf16[4,64,1024]{2,0,1:T(4,128)(2,1)}, bf16[4,64,1024]{2,0,1:T(4,128)(2,1)}, u32[]{:S(2)}, u32[]{:S(2)}) %collective-permute-start.4) | collective-permute-done | bytes 524320 | tf_op jit(solution)/shard_map/ppermute | solution.py:205
  51.7 6.7 %all-to-all-done = bf16[8,72,384]{2,1,0:T(8,128)(2,1)S(1)} async-done(((bf16[8,72,384]{2,1,0:T(8,128)(2,1)}), bf16[8,72,384]{2,1,0:T(8,128)(2,1)S(1)}, u32[]{:S(2)}, u32[]{:S(2)}) %all-to-all-start) | async-done | bytes 442400 | tf_op jit(solution)/shard_map/all_to_all | solution.py:309
  60.0 4.4 all-to-all-start.1
  64.6 2.5 fusion.33
  68.7 2.0 collective-permute-start.8
  73.0 7.7 %collective-permute-done.6 = bf16[8,1,64,384]{3,2,1,0:T(8,128)(2,1)S(1)} collective-permute-done((bf16[8,1,64,384]{3,2,1,0:T(8,128)(2,1)S(1)}, bf16[8,1,64,384]{3,2,1,0:T(8,128)(2,1)S(1)}, u32[]{:S(2)}, u32[]{:S(2)}) %collective-permute-start.6) | collective-permute-done | bytes 393248 | tf_op jit(solution)/shard_map/ppermute | solution.py:205
  82.2 6.0 %collective-permute-done.8 = bf16[8,1,64,384]{3,2,1,0:T(8,128)(2,1)S(1)} collective-permute-done((bf16[8,1,64,384]{3,2,1,0:T(8,128)(2,1)S(1)}, bf16[8,1,64,384]{3,2,1,0:T(8,128)(2,1)S(1)}, u32[]{:S(2)}, u32[]{:S(2)}) %collective-permute-start.8) | collective-permute-done | bytes 393248 | tf_op jit(solution)/shard_map/ppermute | solution.py:205
  95.5 3.1 fusion.4
  98.6 3.8 fusion.14.qkv_ref
  106.3 10.0 %shard_map.135 = (bf16[1024,256]{1,0:T(8,128)(2,1)S(1)}, bf16[1024,256]{1,0:T(8,128)(2,1)S(1)}, bf16[1024,128]{1,0:T(8,128)(2,1)S(1)}, bf16[1024,128]{1,0:T(8,128)(2,1)S(1)}, f32[8,1024]{1,0:T(8,128)S(1)}) custom-call(s32[1]{0:T(128)} %copy.230.length_ref, f32[1024,384]{1,0:T(8,128)S(1)} %fusion.14.qkv_ref, f32[1024,128]{1,0:T(8,128)S(1)} %get-tuple-element.187.cos_ref, ...), custom_call_target="tpu_custom_call" | custom-call | flops 1073741824 | bytes 3145728 | tf_op jit(solution)/shard_map/pallas_call | solution.py:117
  117.7 8.0 %collective-permute-done.11 = bf16[256,512]{1,0:T(8,128)(2,1)S(1)} collective-permute-done((bf16[256,512]{1,0:T(8,128)(2,1)S(1)}, bf16[256,512]{1,0:T(8,128)(2,1)S(1)}, u32[]{:S(2)}, u32[]{:S(2)}) %collective-permute-start.11) | collective-permute-done | bytes 262176 | tf_op jit(solution)/shard_map/ppermute | solution.py:205
  126.6 4.7 convolution_convert_fusion
  131.3 3.2 slice_bitcast_fusion
  138.6 42.7 %reduce-scatter.5.cloned.1.call-done = bf16[128,2048]{1,0:T(8,128)(2,1)} async-done(((bf16[1024,2048]{1,0:T(8,128)(2,1)}), bf16[128,2048]{1,0:T(8,128)(2,1)}) %reduce-scatter.5.cloned.1.call-update) | async-done | bytes 524304 | tf_op jit(solution)/shard_map/reduce_scatter | solution.py:317
  189.5 2.0 fusion.26
  191.5 28.5 %collective-permute-done.22 = bf16[512,512]{1,0:T(8,128)(2,1)} collective-permute-done((bf16[512,512]{1,0:T(8,128)(2,1)}, bf16[512,512]{1,0:T(8,128)(2,1)}, u32[]{:S(2)}, u32[]{:S(2)}) %collective-permute-start.22) | collective-permute-done | bytes 524320 | tf_op jit(solution)/shard_map/ppermute | solution.py:205
  221.2 10.1 %all-gather.6.cloned.1.call-done.x_ref = bf16[1024,2048]{1,0:T(8,128)(2,1)} async-done(((bf16[128,2048]{1,0:T(8,128)(2,1)}), bf16[1024,2048]{1,0:T(8,128)(2,1)}) %all-gather.6.cloned.1.call-update) | async-done | bytes 4194320 | tf_op jit(solution)/shard_map/all_gather | solution.py:313
  236.7 20.0 %shard_map.136 = (f32[1024,1024]{1,0:T(8,128)}, f32[1024,1024]{1,0:T(8,128)}, bf16[8,4,64,1024]{3,2,1,0:T(8,128)(2,1)}, bf16[8,4,64,1024]{3,2,1,0:T(8,128)(2,1)}) custom-call(s32[1]{0:T(128)} %bitcast.33.me_ref, bf16[1024,2048]{1,0:T(8,128)(2,1)} %all-gather.6.cloned.1.call-done.x_ref, bf16[8,64,1024]{2,1,0:T(8,128)(2,1)} %get-tuple-element.171.refs_0_, ...), custom_call_target="tpu_custom_call" | custom-call | flops 8589934592 | bytes 25165824 | tf_op jit(solution)/shard_map/pallas_call | solution.py:367
  256.7 4.9 multiply_convert_fusion.2
  262.9 6.0 %convolution_convert_fusion.4 = bf16[1024,2048]{1,0:T(8,128)(2,1)} fusion(bf16[1024,1024]{1,0:T(8,128)(2,1)S(1)} %multiply_convert_fusion.2, bf16[1024,2048]{1,0:T(8,128)(2,1)S(1)} %maximum_dynamic-update-slice_fusion.2), kind=kOutput, calls=%fused_computation.17 | convolution fusion | flops 4297064448 | bytes 10485760 | tf_op jit(solution)/shard_map/dot_general | solution.py:29
  269.0 10.0 %all-gather.8.cloned.1.call-done = bf16[1024,2048]{1,0:T(8,128)(2,1)} async-done(((bf16[128,2048]{1,0:T(8,128)(2,1)}), bf16[1024,2048]{1,0:T(8,128)(2,1)}) %all-gather.8.cloned.1.call-update) | async-done | bytes 4194320 | tf_op jit(solution)/shard_map/all_gather | solution.py:313
  279.1 7.5 %convolution_convert_fusion.3 = bf16[1024,2048]{1,0:T(8,128)(2,1)S(1)} fusion(bf16[1024,1024]{1,0:T(8,128)(2,1)} %copy-done.15, bf16[1024,2048]{1,0:T(8,128)(2,1)} %all-gather.8.cloned.1.call-done), kind=kOutput, calls=%fused_computation.16 | convolution fusion | flops 4297064448 | bytes 10485760 | tf_op jit(solution)/shard_map/dot_general | solution.py:37
  286.6 2.0 copy-done.9
  288.7 1.9 constant_dynamic-slice_fusion.6
  290.5 2.4 collective-permute-start.26
  294.0 7.2 %multiply_convert_fusion = (bf16[1024,1024]{1,0:T(8,128)(2,1)}, bf16[1024,1024]{1,0:T(8,128)(2,1)S(1)}) fusion(f32[1024,1024]{1,0:T(8,128)S(1)} %copy-done.10, f32[1024,1024]{1,0:T(8,128)S(1)} %copy-done.11, bf16[1024,2048]{1,0:T(8,128)(2,1)S(1)} %copy-done.24, bf16[1024,2048]{1,0:T(8,128)(2,1)S(1)} %copy-done.13), kind=kOutput, calls=%fused_computation.9 | convolution fusion | flops 4308598784 | bytes 20971520 | tf_op jit(solution)/shard_map/dot_general | solution.py:33
  301.2 7.2 %fusion.40 = f32[1024,2048]{1,0:T(8,128)S(1)} fusion(bf16[1024,1024]{1,0:T(8,128)(2,1)S(1)} %get-tuple-element.158, bf16[2048,1024]{1,0:T(8,128)(2,1)} %bitcast.222), kind=kOutput, calls=%fused_computation.153 | convolution fusion | flops 4294967296 | bytes 14680064 | tf_op jit(solution)/shard_map/dot_general | solution.py:33
  308.4 6.1 %add_convert_fusion = bf16[1024,2048]{1,0:T(8,128)(2,1)} fusion(f32[1024,2048]{1,0:T(8,128)S(1)} %fusion.40, bf16[1024,1024]{1,0:T(8,128)(2,1)S(1)} %copy-done.28, bf16[2048,1024]{1,0:T(8,128)(2,1)S(1)} %bitcast.221), kind=kOutput, calls=%fused_computation.7 | convolution fusion | flops 4299161600 | bytes 18874368 | tf_op jit(solution)/shard_map/dot_general | solution.py:33
  314.6 9.6 %convolution_convert_fusion.1 = bf16[2048,1024]{1,0:T(8,128)(2,1)} fusion(bf16[1024,2048]{1,0:T(8,128)(2,1)} %all-gather.6.cloned.1.call-done.x_ref, bf16[1024,1024]{1,0:T(8,128)(2,1)} %get-tuple-element.157), kind=kOutput, calls=%fused_computation.14 | convolution fusion | flops 4297064448 | bytes 10485760 | tf_op jit(solution)/shard_map/dot_general | solution.py:37
  324.1 6.5 %convolution_convert_fusion.2 = bf16[2048,1024]{1,0:T(8,128)(2,1)} fusion(bf16[1024,2048]{1,0:T(8,128)(2,1)S(1)} %copy-done.22, bf16[1024,1024]{1,0:T(8,128)(2,1)S(1)} %copy-done.27), kind=kOutput, calls=%fused_computation.15 | convolution fusion | flops 4297064448 | bytes 10485760 | tf_op jit(solution)/shard_map/dot_general | solution.py:37
  330.7 2.1 convert_element_type.243
  332.8 6.7 %collective-permute-done.25 = bf16[1024,512]{1,0:T(8,128)(2,1)} collective-permute-done((bf16[1024,512]{1,0:T(8,128)(2,1)}, bf16[1024,512]{1,0:T(8,128)(2,1)}, u32[]{:S(2)}, u32[]{:S(2)}) %collective-permute-start.25) | collective-permute-done | bytes 1048608 | tf_op jit(solution)/shard_map/ppermute | solution.py:205
  339.6 3.2 dynamic-slice_bitcast_fusion.2
  348.4 39.5 %reduce-scatter.9.cloned.1.call-done = bf16[128,2048]{1,0:T(8,128)(2,1)} async-done(((bf16[1024,2048]{1,0:T(8,128)(2,1)}), bf16[128,2048]{1,0:T(8,128)(2,1)}) %reduce-scatter.9.cloned.1.call-update) | async-done | bytes 524304 | tf_op jit(solution)/shard_map/reduce_scatter | solution.py:317
  390.7 3.0 collective-permute-done.29
  395.3 2.9 multiply_convert_fusion.3
  398.2 3.0 fusion.5
  402.6 3.1 fusion.8
  405.9 19.2 %collective-permute-done.32 = bf16[8,64,1024]{2,1,0:T(8,128)(2,1)} collective-permute-done((bf16[8,64,1024]{2,1,0:T(8,128)(2,1)}, bf16[8,64,1024]{2,1,0:T(8,128)(2,1)}, u32[]{:S(2)}, u32[]{:S(2)}) %collective-permute-start.32) | collective-permute-done | bytes 1048608 | tf_op jit(solution)/shard_map/ppermute | solution.py:205
  425.1 2.5 fusion.23
  429.2 2.5 fusion.22
  433.3 9.9 %all-gather.10.cloned.1.call-done = bf16[1024,2048]{1,0:T(8,128)(2,1)} async-done(((bf16[128,2048]{1,0:T(8,128)(2,1)}), bf16[1024,2048]{1,0:T(8,128)(2,1)}) %all-gather.10.cloned.1.call-update) | async-done | bytes 4194320 | tf_op jit(solution)/shard_map/all_gather | solution.py:313
  443.2 4.3 all-to-all-start.2
  448.0 4.2 convert_add_fusion.4
  457.9 2.5 convolution_convert_fusion.7.grad_ref
  460.4 10.9 %shard_map.137 = bf16[1024,384]{1,0:T(8,128)(2,1)S(1)} custom-call(s32[1]{0:T(128)} %copy.230.length_ref, bf16[1024,256]{1,0:T(8,128)(2,1)S(1)} %get-tuple-element.122.q_ref, bf16[1024,128]{1,0:T(8,128)(2,1)S(1)} %get-tuple-element.123.k_ref, bf16[1024,128]{1,0:T(8,128)(2,1)S(1)} %get-tuple-element.124.v_ref, f32[8,1024]{1,0:T(8,128)S(1)} %get-tuple-element.125.lse_ref, ...), custom_call_target="tpu_custom_call" | custom-call | flops 2684354560 | bytes 3145728 | tf_op jit(solution)/shard_map/pallas_call | solution.py:186
  471.3 2.6 convolution_convert_fusion.5
  477.7 6.4 %fusion.3 = (bf16[2048]{0:T(1024)(128)(2,1)}, bf16[1024,2048]{1,0:T(8,128)(2,1)}) fusion(bf16[1024,2048]{1,0:T(8,128)(2,1)S(1)} %bitcast.198, f32[1024]{0:T(1024)S(1)} %add_rsqrt_fusion, bf16[1024,384]{1,0:T(8,128)(2,1)S(1)} %shard_map.137, bf16[2048,384]{1,0:T(8,128)(2,1)} %bitcast.25), kind=kOutput, calls=%fused_computation.5 | convolution fusion | flops 1621096448 | bytes 10756096 | tf_op jit(solution)/shard_map/dot_general | solution.py:33
  484.9 2.1 convert_add_fusion.7
  487.0 7.3 %collective-permute-done.35 = bf16[8,64,384]{2,1,0:T(8,128)(2,1)} collective-permute-done((bf16[8,64,384]{2,1,0:T(8,128)(2,1)S(1)}, bf16[8,64,384]{2,1,0:T(8,128)(2,1)}, u32[]{:S(2)}, u32[]{:S(2)}) %collective-permute-start.35) | collective-permute-done | bytes 393248 | tf_op jit(solution)/shard_map/ppermute | solution.py:205
  497.9 1.8 copy.165
  503.2 5.0 all-to-all-start.3
  509.7 4.7 collective-permute-done.39
  515.5 10.4 %collective-permute-done.40 = bf16[4,64,1024]{2,1,0:T(8,128)(2,1)} collective-permute-done((bf16[4,64,1024]{2,1,0:T(8,128)(2,1)}, bf16[4,64,1024]{2,1,0:T(8,128)(2,1)}, u32[]{:S(2)}, u32[]{:S(2)}) %collective-permute-start.40) | collective-permute-done | bytes 524320 | tf_op jit(solution)/shard_map/ppermute | solution.py:205
  527.1 2.1 all-to-all-done.3
  537.9 2.7 copy.169
  540.6 5.8 %copy.179 = f32[32,8,4,1024]{3,1,2,0:T(8,128)} copy(f32[32,8,4,1024]{3,2,1,0:T(4,128)S(1)} %bitcast.186) | data formatting | bytes 8388608
  548.1 7.2 %reduce-scatter.11.cloned.1.call-done = bf16[128,2048]{1,0:T(8,128)(2,1)} async-done(((bf16[1024,2048]{1,0:T(8,128)(2,1)}), bf16[128,2048]{1,0:T(8,128)(2,1)}) %reduce-scatter.11.cloned.1.call-update) | async-done | bytes 524304 | tf_op jit(solution)/shard_map/reduce_scatter | solution.py:317
  (253 shorter events, 102.4 us)
Async XLA Ops:
  7.2 81.8 %all-gather.12.cloned.1.call-start = ((), (), s32[]{:S(2)}) async-start(), calls=%async_computation.15 | async-start | bytes 4718592 | tf_op jit(solution)/shard_map/all_gather | solution.py:313
  9.0 9.3 %collective-permute-start.2 = (bf16[64,768]{1,0:T(8,128)(2,1)S(1)}, bf16[64,768]{1,0:T(8,128)(2,1)S(1)}, u32[]{:S(2)}, u32[]{:S(2)}) collective-permute-start(bf16[64,768]{1,0:T(8,128)(2,1)S(1)} %get-tuple-element.196), channel_id=1, source_target_pairs={{0,24},{8,16},{16,8},{24,0},{1,25},{9,17},{17,9},{25,1},{2,26},{10... | collective-permute-start | bytes 294920 | tf_op jit(solution)/shard_map/ppermute | solution.py:205
  13.0 5.2 collective-permute-start.1
  13.5 4.7 collective-permute-start
  23.6 14.4 %collective-permute-start.3 = (bf16[4,64,1024]{2,0,1:T(4,128)(2,1)}, bf16[4,64,1024]{2,0,1:T(4,128)(2,1)}, u32[]{:S(2)}, u32[]{:S(2)}) collective-permute-start(bf16[4,64,1024]{2,0,1:T(4,128)(2,1)} %get-tuple-element.174), channel_id=1, source_target_pairs={{0,8},{8,0},{16,24},{24,16},{1,9},{9,1},{17,25},{25,17},{2,10},{10... | collective-permute-start | bytes 1572872 | tf_op jit(solution)/shard_map/ppermute | solution.py:205
  25.3 24.9 %collective-permute-start.4 = (bf16[4,64,1024]{2,0,1:T(4,128)(2,1)}, bf16[4,64,1024]{2,0,1:T(4,128)(2,1)}, u32[]{:S(2)}, u32[]{:S(2)}) collective-permute-start(bf16[4,64,1024]{2,0,1:T(4,128)(2,1)} %get-tuple-element.173), channel_id=1, source_target_pairs={{0,16},{8,24},{16,0},{24,8},{1,17},{9,25},{17,1},{25,9},{2,18},{10... | collective-permute-start | bytes 1572872 | tf_op jit(solution)/shard_map/ppermute | solution.py:205
  26.9 31.5 %all-to-all-start = ((bf16[8,72,384]{2,1,0:T(8,128)(2,1)}), bf16[8,72,384]{2,1,0:T(8,128)(2,1)S(1)}, u32[]{:S(2)}, u32[]{:S(2)}) async-start(bf16[8,72,384]{2,1,0:T(8,128)(2,1)} %copy.151), calls=%async_computation | async-start | bytes 884736 | tf_op jit(solution)/shard_map/all_to_all | solution.py:309
  31.9 19.5 %collective-permute-start.5 = (bf16[4,64,1024]{2,0,1:T(4,128)(2,1)}, bf16[4,64,1024]{2,0,1:T(4,128)(2,1)S(1)}, u32[]{:S(2)}, u32[]{:S(2)}) collective-permute-start(bf16[4,64,1024]{2,0,1:T(4,128)(2,1)} %get-tuple-element.172), channel_id=1, source_target_pairs={{0,24},{8,16},{16,8},{24,0},{1,25},{9,17},{17,9},{25,1},{2,26},{10... | collective-permute-start | bytes 1572872 | tf_op jit(solution)/shard_map/ppermute | solution.py:205
  60.0 66.5 %all-to-all-start.1 = ((bf16[8,2,64,1024]{3,2,1,0:T(8,128)(2,1)}), bf16[8,2,64,1024]{3,2,1,0:T(8,128)(2,1)}, u32[]{:S(2)}, u32[]{:S(2)}) async-start(bf16[8,2,64,1024]{3,2,1,0:T(8,128)(2,1)} %copy.156), calls=%async_computation.1 | async-start | bytes 4194304 | tf_op jit(solution)/shard_map/all_to_all | solution.py:309
  64.3 24.6 %copy-start.19 = (bf16[256,512]{1,0:T(8,128)(2,1)S(1)}, bf16[256,512]{1,0:T(8,128)(2,1)}, u32[]{:S(2)}) copy-start(bf16[256,512]{1,0:T(8,128)(2,1)} %param.11) | copy-start | bytes 786436
  64.4 26.5 %copy-start.7 = (bf16[1024,512]{1,0:T(8,128)(2,1)S(1)}, bf16[1024,512]{1,0:T(8,128)(2,1)}, u32[]{:S(2)}) copy-start(bf16[1024,512]{1,0:T(8,128)(2,1)} %param.13) | copy-start | bytes 3145732
  64.4 116.9 %reduce-scatter.5.cloned.1.call-start = ((), (), s32[]{:S(2)}) async-start(), calls=%async_computation.8 | async-start | bytes 4718592 | tf_op jit(solution)/shard_map/reduce_scatter | solution.py:317
  67.1 14.3 %collective-permute-start.7 = (bf16[8,1,64,384]{3,2,1,0:T(8,128)(2,1)S(1)}, bf16[8,1,64,384]{3,2,1,0:T(8,128)(2,1)S(1)}, u32[]{:S(2)}, u32[]{:S(2)}) collective-permute-start(bf16[8,1,64,384]{3,2,1,0:T(8,128)(2,1)S(1)} %slice_bitcast_fusion.3), channel_id=1, source_target_pairs={{0,16},{8,24},{16,0},{24,8},{1,17},{9,25},{17,1},{25,9},{2,18},{10... | collective-permute-start | bytes 1179656 | tf_op jit(solution)/shard_map/ppermute | solution.py:205
  68.6 12.0 %collective-permute-start.6 = (bf16[8,1,64,384]{3,2,1,0:T(8,128)(2,1)S(1)}, bf16[8,1,64,384]{3,2,1,0:T(8,128)(2,1)S(1)}, u32[]{:S(2)}, u32[]{:S(2)}) collective-permute-start(bf16[8,1,64,384]{3,2,1,0:T(8,128)(2,1)S(1)} %slice_bitcast_fusion.3), channel_id=1, source_target_pairs={{0,8},{8,0},{16,24},{24,16},{1,9},{9,1},{17,25},{25,17},{2,10},{10... | collective-permute-start | bytes 1179656 | tf_op jit(solution)/shard_map/ppermute | solution.py:205
  68.7 19.5 %collective-permute-start.8 = (bf16[8,1,64,384]{3,2,1,0:T(8,128)(2,1)S(1)}, bf16[8,1,64,384]{3,2,1,0:T(8,128)(2,1)S(1)}, u32[]{:S(2)}, u32[]{:S(2)}) collective-permute-start(bf16[8,1,64,384]{3,2,1,0:T(8,128)(2,1)S(1)} %slice_bitcast_fusion.3), channel_id=1, source_target_pairs={{0,24},{8,16},{16,8},{24,0},{1,25},{9,17},{17,9},{25,1},{2,26},{10... | collective-permute-start | bytes 1179656 | tf_op jit(solution)/shard_map/ppermute | solution.py:205
  89.0 13.4 %collective-permute-start.10 = (bf16[256,512]{1,0:T(8,128)(2,1)S(1)}, bf16[256,512]{1,0:T(8,128)(2,1)S(1)}, u32[]{:S(2)}, u32[]{:S(2)}) collective-permute-start(bf16[256,512]{1,0:T(8,128)(2,1)S(1)} %copy-done.19), channel_id=1, source_target_pairs={{0,16},{8,24},{16,0},{24,8},{1,17},{9,25},{17,1},{25,9},{2,18},{10... | collective-permute-start | bytes 786440 | tf_op jit(solution)/shard_map/ppermute | solution.py:205
  90.4 14.3 %collective-permute-start.9 = (bf16[256,512]{1,0:T(8,128)(2,1)S(1)}, bf16[256,512]{1,0:T(8,128)(2,1)S(1)}, u32[]{:S(2)}, u32[]{:S(2)}) collective-permute-start(bf16[256,512]{1,0:T(8,128)(2,1)S(1)} %copy-done.19), channel_id=1, source_target_pairs={{0,8},{8,0},{16,24},{24,16},{1,9},{9,1},{17,25},{25,17},{2,10},{10... | collective-permute-start | bytes 786440 | tf_op jit(solution)/shard_map/ppermute | solution.py:205
  91.9 34.7 %collective-permute-start.15 = (bf16[512,512]{1,0:T(8,128)(2,1)}, bf16[512,512]{1,0:T(8,128)(2,1)S(1)}, u32[]{:S(2)}, u32[]{:S(2)}) collective-permute-start(bf16[512,512]{1,0:T(8,128)(2,1)} %get-tuple-element.183), channel_id=1, source_target_pairs={{0,16},{8,24},{16,0},{24,8},{1,17},{9,25},{17,1},{25,9},{2,18},{10... | collective-permute-start | bytes 1572872 | tf_op jit(solution)/shard_map/ppermute | solution.py:205
  93.5 33.0 %collective-permute-start.13 = (bf16[512,512]{1,0:T(8,128)(2,1)}, bf16[512,512]{1,0:T(8,128)(2,1)}, u32[]{:S(2)}, u32[]{:S(2)}) collective-permute-start(bf16[512,512]{1,0:T(8,128)(2,1)} %get-tuple-element.183), channel_id=1, source_target_pairs={{0,8},{8,0},{16,24},{24,16},{1,9},{9,1},{17,25},{25,17},{2,10},{10... | collective-permute-start | bytes 1572872 | tf_op jit(solution)/shard_map/ppermute | solution.py:205
  94.1 32.5 %collective-permute-start.14 = (bf16[512,512]{1,0:T(8,128)(2,1)}, bf16[512,512]{1,0:T(8,128)(2,1)}, u32[]{:S(2)}, u32[]{:S(2)}) collective-permute-start(bf16[512,512]{1,0:T(8,128)(2,1)} %get-tuple-element.184), channel_id=1, source_target_pairs={{0,16},{8,24},{16,0},{24,8},{1,17},{9,25},{17,1},{25,9},{2,18},{10... | collective-permute-start | bytes 1572872 | tf_op jit(solution)/shard_map/ppermute | solution.py:205
  102.4 24.1 %collective-permute-start.12 = (bf16[512,512]{1,0:T(8,128)(2,1)}, bf16[512,512]{1,0:T(8,128)(2,1)}, u32[]{:S(2)}, u32[]{:S(2)}) collective-permute-start(bf16[512,512]{1,0:T(8,128)(2,1)} %get-tuple-element.184), channel_id=1, source_target_pairs={{0,8},{8,0},{16,24},{24,16},{1,9},{9,1},{17,25},{25,17},{2,10},{10... | collective-permute-start | bytes 1572872 | tf_op jit(solution)/shard_map/ppermute | solution.py:205
  104.7 21.1 %collective-permute-start.11 = (bf16[256,512]{1,0:T(8,128)(2,1)S(1)}, bf16[256,512]{1,0:T(8,128)(2,1)S(1)}, u32[]{:S(2)}, u32[]{:S(2)}) collective-permute-start(bf16[256,512]{1,0:T(8,128)(2,1)S(1)} %copy-done.19), channel_id=1, source_target_pairs={{0,24},{8,16},{16,8},{24,0},{1,25},{9,17},{17,9},{25,1},{2,26},{10... | collective-permute-start | bytes 786440 | tf_op jit(solution)/shard_map/ppermute | solution.py:205
  131.2 51.3 %copy-start.2 = (bf16[1,128,2048]{2,1,0:T(8,128)(2,1)S(1)}, bf16[1,128,2048]{2,1,0:T(8,128)(2,1)}, u32[]{:S(2)}) copy-start(bf16[1,128,2048]{2,1,0:T(8,128)(2,1)} %param.8) | copy-start | bytes 1572868
  131.3 100.0 %all-gather.6.cloned.1.call-start = ((), (), s32[]{:S(2)}) async-start(), calls=%async_computation.9 | async-start | bytes 4718592 | tf_op jit(solution)/shard_map/all_gather | solution.py:313
  134.6 47.9 %collective-permute-start.19 = (bf16[8,64,1024]{2,1,0:T(8,128)(2,1)}, bf16[8,64,1024]{2,1,0:T(8,128)(2,1)}, u32[]{:S(2)}, u32[]{:S(2)}) collective-permute-start(bf16[8,64,1024]{2,1,0:T(8,128)(2,1)} %get-tuple-element.170.refs_4_), channel_id=1, source_target_pairs={{0,8},{8,0},{16,24},{24,16},{1,9},{9,1},{17,25},{25,17},{2,10},{10... | collective-permute-start | bytes 3145736 | tf_op jit(solution)/shard_map/ppermute | solution.py:205
  136.0 46.5 %collective-permute-start.18 = (bf16[8,64,1024]{2,1,0:T(8,128)(2,1)}, bf16[8,64,1024]{2,1,0:T(8,128)(2,1)}, u32[]{:S(2)}, u32[]{:S(2)}) collective-permute-start(bf16[8,64,1024]{2,1,0:T(8,128)(2,1)} %get-tuple-element.170.refs_4_), channel_id=1, source_target_pairs={{0,16},{8,24},{16,0},{24,8},{1,17},{9,25},{17,1},{25,9},{2,18},{10... | collective-permute-start | bytes 3145736 | tf_op jit(solution)/shard_map/ppermute | solution.py:205
  136.7 45.8 %collective-permute-start.17 = (bf16[8,64,1024]{2,1,0:T(8,128)(2,1)}, bf16[8,64,1024]{2,1,0:T(8,128)(2,1)}, u32[]{:S(2)}, u32[]{:S(2)}) collective-permute-start(bf16[8,64,1024]{2,1,0:T(8,128)(2,1)} %get-tuple-element.171.refs_0_), channel_id=1, source_target_pairs={{0,16},{8,24},{16,0},{24,8},{1,17},{9,25},{17,1},{25,9},{2,18},{10... | collective-permute-start | bytes 3145736 | tf_op jit(solution)/shard_map/ppermute | solution.py:205
  138.0 44.5 %collective-permute-start.16 = (bf16[8,64,1024]{2,1,0:T(8,128)(2,1)}, bf16[8,64,1024]{2,1,0:T(8,128)(2,1)}, u32[]{:S(2)}, u32[]{:S(2)}) collective-permute-start(bf16[8,64,1024]{2,1,0:T(8,128)(2,1)} %get-tuple-element.171.refs_0_), channel_id=1, source_target_pairs={{0,8},{8,0},{16,24},{24,16},{1,9},{9,1},{17,25},{25,17},{2,10},{10... | collective-permute-start | bytes 3145736 | tf_op jit(solution)/shard_map/ppermute | solution.py:205
  185.3 93.7 %all-gather.8.cloned.1.call-start = ((), (), s32[]{:S(2)}) async-start(), calls=%async_computation.10 | async-start | bytes 4718592 | tf_op jit(solution)/shard_map/all_gather | solution.py:313
  185.3 35.8 %collective-permute-start.20 = (bf16[8,64,1024]{2,1,0:T(8,128)(2,1)}, bf16[8,64,1024]{2,1,0:T(8,128)(2,1)}, u32[]{:S(2)}, u32[]{:S(2)}) collective-permute-start(bf16[8,64,1024]{2,1,0:T(8,128)(2,1)} %collective-permute-done.16.refs_1_), channel_id=1, source_target_pairs={{0,16},{8,24},{16,0},{24,8},{1,17},{9,25},{17,1},{25,9},{2,18},{10... | collective-permute-start | bytes 3145736 | tf_op jit(solution)/shard_map/ppermute | solution.py:205
  186.9 34.3 %collective-permute-start.21 = (bf16[8,64,1024]{2,1,0:T(8,128)(2,1)}, bf16[8,64,1024]{2,1,0:T(8,128)(2,1)}, u32[]{:S(2)}, u32[]{:S(2)}) collective-permute-start(bf16[8,64,1024]{2,1,0:T(8,128)(2,1)} %collective-permute-done.18.refs_6_), channel_id=1, source_target_pairs={{0,8},{8,0},{16,24},{24,16},{1,9},{9,1},{17,25},{25,17},{2,10},{10... | collective-permute-start | bytes 3145736 | tf_op jit(solution)/shard_map/ppermute | solution.py:205
  188.4 31.6 %collective-permute-start.22 = (bf16[512,512]{1,0:T(8,128)(2,1)}, bf16[512,512]{1,0:T(8,128)(2,1)}, u32[]{:S(2)}, u32[]{:S(2)}) collective-permute-start(bf16[512,512]{1,0:T(8,128)(2,1)} %collective-permute-done.12), channel_id=1, source_target_pairs={{0,16},{8,24},{16,0},{24,8},{1,17},{9,25},{17,1},{25,9},{2,18},{10... | collective-permute-start | bytes 1572872 | tf_op jit(solution)/shard_map/ppermute | solution.py:205
  188.9 32.3 %collective-permute-start.23 = (bf16[512,512]{1,0:T(8,128)(2,1)}, bf16[512,512]{1,0:T(8,128)(2,1)}, u32[]{:S(2)}, u32[]{:S(2)}) collective-permute-start(bf16[512,512]{1,0:T(8,128)(2,1)} %copy-done.17), channel_id=1, source_target_pairs={{0,8},{8,0},{16,24},{24,16},{1,9},{9,1},{17,25},{25,17},{2,10},{10... | collective-permute-start | bytes 1572872 | tf_op jit(solution)/shard_map/ppermute | solution.py:205
  231.3 99.4 %reduce-scatter.7.cloned.1.call-start = ((), (), s32[]{:S(2)}) async-start(), calls=%async_computation.11 | async-start | bytes 4718592 | tf_op jit(solution)/shard_map/reduce_scatter | solution.py:317
  236.7 24.9 %copy-start.12 = (bf16[1024,2048]{1,0:T(8,128)(2,1)}, bf16[1024,2048]{1,0:T(8,128)(2,1)S(1)}, u32[]{:S(2)}) copy-start(bf16[1024,2048]{1,0:T(8,128)(2,1)S(1)} %maximum_dynamic-update-slice_fusion.2) | copy-start | bytes 12582916
  279.0 108.9 %reduce-scatter.9.cloned.1.call-start = ((), (), s32[]{:S(2)}) async-start(), calls=%async_computation.12 | async-start | bytes 4718592 | tf_op jit(solution)/shard_map/reduce_scatter | solution.py:317
  279.0 15.0 %copy-start.11 = (f32[1024,1024]{1,0:T(8,128)S(1)}, f32[1024,1024]{1,0:T(8,128)}, u32[]{:S(2)}) copy-start(f32[1024,1024]{1,0:T(8,128)} %get-tuple-element.106) | copy-start | bytes 12582916
  290.5 42.3 %collective-permute-start.26 = (bf16[1024,512]{1,0:T(8,128)(2,1)}, bf16[1024,512]{1,0:T(8,128)(2,1)}, u32[]{:S(2)}, u32[]{:S(2)}) collective-permute-start(bf16[1024,512]{1,0:T(8,128)(2,1)} %get-tuple-element.163), channel_id=1, source_target_pairs={{0,24},{8,16},{16,8},{24,0},{1,25},{9,17},{17,9},{25,1},{2,26},{10... | collective-permute-start | bytes 3145736 | tf_op jit(solution)/shard_map/ppermute | solution.py:205
  292.9 46.6 %collective-permute-start.25 = (bf16[1024,512]{1,0:T(8,128)(2,1)}, bf16[1024,512]{1,0:T(8,128)(2,1)}, u32[]{:S(2)}, u32[]{:S(2)}) collective-permute-start(bf16[1024,512]{1,0:T(8,128)(2,1)} %get-tuple-element.164), channel_id=1, source_target_pairs={{0,16},{8,24},{16,0},{24,8},{1,17},{9,25},{17,1},{25,9},{2,18},{10... | collective-permute-start | bytes 3145736 | tf_op jit(solution)/shard_map/ppermute | solution.py:205
  293.4 46.1 %collective-permute-start.24 = (bf16[1024,512]{1,0:T(8,128)(2,1)}, bf16[1024,512]{1,0:T(8,128)(2,1)}, u32[]{:S(2)}, u32[]{:S(2)}) collective-permute-start(bf16[1024,512]{1,0:T(8,128)(2,1)} %get-tuple-element.165), channel_id=1, source_target_pairs={{0,8},{8,0},{16,24},{24,16},{1,9},{9,1},{17,25},{25,17},{2,10},{10... | collective-permute-start | bytes 3145736 | tf_op jit(solution)/shard_map/ppermute | solution.py:205
  339.6 103.6 %all-gather.10.cloned.1.call-start = ((), (), s32[]{:S(2)}) async-start(), calls=%async_computation.13 | async-start | bytes 4718592 | tf_op jit(solution)/shard_map/all_gather | solution.py:313
  342.9 46.3 %collective-permute-start.28 = (bf16[8,64,1024]{2,1,0:T(8,128)(2,1)}, bf16[8,64,1024]{2,1,0:T(8,128)(2,1)}, u32[]{:S(2)}, u32[]{:S(2)}) collective-permute-start(bf16[8,64,1024]{2,1,0:T(8,128)(2,1)} %get-tuple-element.161), channel_id=1, source_target_pairs={{0,8},{8,0},{16,24},{24,16},{1,9},{9,1},{17,25},{25,17},{2,10},{10... | collective-permute-start | bytes 3145736 | tf_op jit(solution)/shard_map/ppermute | solution.py:205
  344.3 46.3 %collective-permute-start.27 = (bf16[8,64,1024]{2,1,0:T(8,128)(2,1)}, bf16[8,64,1024]{2,1,0:T(8,128)(2,1)}, u32[]{:S(2)}, u32[]{:S(2)}) collective-permute-start(bf16[8,64,1024]{2,1,0:T(8,128)(2,1)} %get-tuple-element.162), channel_id=1, source_target_pairs={{0,8},{8,0},{16,24},{24,16},{1,9},{9,1},{17,25},{25,17},{2,10},{10... | collective-permute-start | bytes 3145736 | tf_op jit(solution)/shard_map/ppermute | solution.py:205
  346.4 44.3 %collective-permute-start.30 = (bf16[8,64,1024]{2,1,0:T(8,128)(2,1)}, bf16[8,64,1024]{2,1,0:T(8,128)(2,1)}, u32[]{:S(2)}, u32[]{:S(2)}) collective-permute-start(bf16[8,64,1024]{2,1,0:T(8,128)(2,1)} %get-tuple-element.159), channel_id=1, source_target_pairs={{0,16},{8,24},{16,0},{24,8},{1,17},{9,25},{17,1},{25,9},{2,18},{10... | collective-permute-start | bytes 3145736 | tf_op jit(solution)/shard_map/ppermute | solution.py:205
  347.8 45.8 %collective-permute-start.29 = (bf16[8,64,1024]{2,1,0:T(8,128)(2,1)}, bf16[8,64,1024]{2,1,0:T(8,128)(2,1)}, u32[]{:S(2)}, u32[]{:S(2)}) collective-permute-start(bf16[8,64,1024]{2,1,0:T(8,128)(2,1)} %get-tuple-element.160), channel_id=1, source_target_pairs={{0,16},{8,24},{16,0},{24,8},{1,17},{9,25},{17,1},{25,9},{2,18},{10... | collective-permute-start | bytes 3145736 | tf_op jit(solution)/shard_map/ppermute | solution.py:205
  401.2 23.9 %collective-permute-start.32 = (bf16[8,64,1024]{2,1,0:T(8,128)(2,1)}, bf16[8,64,1024]{2,1,0:T(8,128)(2,1)}, u32[]{:S(2)}, u32[]{:S(2)}) collective-permute-start(bf16[8,64,1024]{2,1,0:T(8,128)(2,1)} %fusion.5), channel_id=1, source_target_pairs={{0,8},{8,0},{16,24},{24,16},{1,9},{9,1},{17,25},{25,17},{2,10},{10... | collective-permute-start | bytes 3145736 | tf_op jit(solution)/shard_map/ppermute | solution.py:205
  405.7 23.5 %collective-permute-start.31 = (bf16[8,64,1024]{2,1,0:T(8,128)(2,1)}, bf16[8,64,1024]{2,1,0:T(8,128)(2,1)}, u32[]{:S(2)}, u32[]{:S(2)}) collective-permute-start(bf16[8,64,1024]{2,1,0:T(8,128)(2,1)} %fusion.8), channel_id=1, source_target_pairs={{0,16},{8,24},{16,0},{24,8},{1,17},{9,25},{17,1},{25,9},{2,18},{10... | collective-permute-start | bytes 3145736 | tf_op jit(solution)/shard_map/ppermute | solution.py:205
  443.2 54.7 %all-to-all-start.2 = ((bf16[8,2,64,1024]{3,2,1,0:T(8,128)(2,1)}), bf16[8,2,64,1024]{3,2,1,0:T(8,128)(2,1)}, u32[]{:S(2)}, u32[]{:S(2)}) async-start(bf16[8,2,64,1024]{3,2,1,0:T(8,128)(2,1)} %pad_maximum_fusion), calls=%async_computation.5 | async-start | bytes 4194304 | tf_op jit(solution)/shard_map/all_to_all | solution.py:309
  447.5 107.7 %reduce-scatter.11.cloned.1.call-start = ((), (), s32[]{:S(2)}) async-start(), calls=%async_computation.14 | async-start | bytes 4718592 | tf_op jit(solution)/shard_map/reduce_scatter | solution.py:317
  454.4 22.8 %collective-permute-start.36 = (bf16[256,512]{1,0:T(8,128)(2,1)S(1)}, bf16[256,512]{1,0:T(8,128)(2,1)S(1)}, u32[]{:S(2)}, u32[]{:S(2)}) collective-permute-start(bf16[256,512]{1,0:T(8,128)(2,1)S(1)} %get-tuple-element.180), channel_id=1, source_target_pairs={{0,8},{8,0},{16,24},{24,16},{1,9},{9,1},{17,25},{25,17},{2,10},{10... | collective-permute-start | bytes 786440 | tf_op jit(solution)/shard_map/ppermute | solution.py:205
  455.8 29.0 %collective-permute-start.38 = (bf16[256,512]{1,0:T(8,128)(2,1)}, bf16[256,512]{1,0:T(8,128)(2,1)}, u32[]{:S(2)}, u32[]{:S(2)}) collective-permute-start(bf16[256,512]{1,0:T(8,128)(2,1)} %get-tuple-element.181), channel_id=1, source_target_pairs={{0,24},{8,16},{16,8},{24,0},{1,25},{9,17},{17,9},{25,1},{2,26},{10... | collective-permute-start | bytes 786440 | tf_op jit(solution)/shard_map/ppermute | solution.py:205
  457.3 27.5 %collective-permute-start.37 = (bf16[256,512]{1,0:T(8,128)(2,1)S(1)}, bf16[256,512]{1,0:T(8,128)(2,1)}, u32[]{:S(2)}, u32[]{:S(2)}) collective-permute-start(bf16[256,512]{1,0:T(8,128)(2,1)S(1)} %get-tuple-element.182), channel_id=1, source_target_pairs={{0,16},{8,24},{16,0},{24,8},{1,17},{9,25},{17,1},{25,9},{2,18},{10... | collective-permute-start | bytes 786440 | tf_op jit(solution)/shard_map/ppermute | solution.py:205
  474.1 12.8 %collective-permute-start.33 = (bf16[8,64,384]{2,1,0:T(8,128)(2,1)S(1)}, bf16[8,64,384]{2,1,0:T(8,128)(2,1)}, u32[]{:S(2)}, u32[]{:S(2)}) collective-permute-start(bf16[8,64,384]{2,1,0:T(8,128)(2,1)S(1)} %get-tuple-element.176), channel_id=1, source_target_pairs={{0,8},{8,0},{16,24},{24,16},{1,9},{9,1},{17,25},{25,17},{2,10},{10... | collective-permute-start | bytes 1179656 | tf_op jit(solution)/shard_map/ppermute | solution.py:205
  475.7 18.6 %collective-permute-start.35 = (bf16[8,64,384]{2,1,0:T(8,128)(2,1)S(1)}, bf16[8,64,384]{2,1,0:T(8,128)(2,1)}, u32[]{:S(2)}, u32[]{:S(2)}) collective-permute-start(bf16[8,64,384]{2,1,0:T(8,128)(2,1)S(1)} %get-tuple-element.177), channel_id=1, source_target_pairs={{0,24},{8,16},{16,8},{24,0},{1,25},{9,17},{17,9},{25,1},{2,26},{10... | collective-permute-start | bytes 1179656 | tf_op jit(solution)/shard_map/ppermute | solution.py:205
  477.1 18.5 %collective-permute-start.34 = (bf16[8,64,384]{2,1,0:T(8,128)(2,1)S(1)}, bf16[8,64,384]{2,1,0:T(8,128)(2,1)}, u32[]{:S(2)}, u32[]{:S(2)}) collective-permute-start(bf16[8,64,384]{2,1,0:T(8,128)(2,1)S(1)} %get-tuple-element.178), channel_id=1, source_target_pairs={{0,16},{8,24},{16,0},{24,8},{1,17},{9,25},{17,1},{25,9},{2,18},{10... | collective-permute-start | bytes 1179656 | tf_op jit(solution)/shard_map/ppermute | solution.py:205
  501.1 13.3 %collective-permute-start.39 = (bf16[4,64,1024]{2,1,0:T(8,128)(2,1)}, bf16[4,64,1024]{2,1,0:T(8,128)(2,1)}, u32[]{:S(2)}, u32[]{:S(2)}) collective-permute-start(bf16[4,64,1024]{2,1,0:T(8,128)(2,1)} %get-tuple-element.168), channel_id=1, source_target_pairs={{0,8},{8,0},{16,24},{24,16},{1,9},{9,1},{17,25},{25,17},{2,10},{10... | collective-permute-start | bytes 1572872 | tf_op jit(solution)/shard_map/ppermute | solution.py:205
  502.6 23.3 %collective-permute-start.40 = (bf16[4,64,1024]{2,1,0:T(8,128)(2,1)}, bf16[4,64,1024]{2,1,0:T(8,128)(2,1)}, u32[]{:S(2)}, u32[]{:S(2)}) collective-permute-start(bf16[4,64,1024]{2,1,0:T(8,128)(2,1)} %get-tuple-element.167), channel_id=1, source_target_pairs={{0,16},{8,24},{16,0},{24,8},{1,17},{9,25},{17,1},{25,9},{2,18},{10... | collective-permute-start | bytes 1572872 | tf_op jit(solution)/shard_map/ppermute | solution.py:205
  503.2 26.0 %all-to-all-start.3 = ((bf16[8,72,384]{2,1,0:T(8,128)(2,1)}), bf16[8,72,384]{2,1,0:T(8,128)(2,1)S(1)}, u32[]{:S(2)}, u32[]{:S(2)}) async-start(bf16[8,72,384]{2,1,0:T(8,128)(2,1)} %fusion.32), calls=%async_computation.7 | async-start | bytes 884736 | tf_op jit(solution)/shard_map/all_to_all | solution.py:309
  508.2 18.8 %collective-permute-start.41 = (bf16[4,64,1024]{2,1,0:T(8,128)(2,1)}, bf16[4,64,1024]{2,1,0:T(8,128)(2,1)S(1)}, u32[]{:S(2)}, u32[]{:S(2)}) collective-permute-start(bf16[4,64,1024]{2,1,0:T(8,128)(2,1)} %get-tuple-element.166), channel_id=1, source_target_pairs={{0,24},{8,16},{16,8},{24,0},{1,25},{9,17},{17,9},{25,1},{2,26},{10... | collective-permute-start | bytes 1572872 | tf_op jit(solution)/shard_map/ppermute | solution.py:205
  529.2 6.6 %collective-permute-start.45 = (f32[2,256]{1,0:T(2,128)S(1)}, f32[2,256]{1,0:T(2,128)}, u32[]{:S(2)}, u32[]{:S(2)}) collective-permute-start(f32[2,256]{1,0:T(2,128)S(1)} %convert_reduce_fusion), channel_id=1, source_target_pairs={{0,8},{8,0},{16,24},{24,16},{1,9},{9,1},{17,25},{25,17},{2,10},{10... | collective-permute-start | bytes 6152 | tf_op jit(solution)/shard_map/ppermute | solution.py:205
  531.7 15.3 %collective-permute-start.42 = (bf16[64,768]{1,0:T(8,128)(2,1)S(1)}, bf16[64,768]{1,0:T(8,128)(2,1)S(1)}, u32[]{:S(2)}, u32[]{:S(2)}) collective-permute-start(bf16[64,768]{1,0:T(8,128)(2,1)S(1)} %bitcast.215), channel_id=1, source_target_pairs={{0,8},{8,0},{16,24},{24,16},{1,9},{9,1},{17,25},{25,17},{2,10},{10... | collective-permute-start | bytes 294920 | tf_op jit(solution)/shard_map/ppermute | solution.py:205
  533.2 13.8 %collective-permute-start.43 = (bf16[64,768]{1,0:T(8,128)(2,1)S(1)}, bf16[64,768]{1,0:T(8,128)(2,1)S(1)}, u32[]{:S(2)}, u32[]{:S(2)}) collective-permute-start(bf16[64,768]{1,0:T(8,128)(2,1)S(1)} %bitcast.214), channel_id=1, source_target_pairs={{0,16},{8,24},{16,0},{24,8},{1,17},{9,25},{17,1},{25,9},{2,18},{10... | collective-permute-start | bytes 294920 | tf_op jit(solution)/shard_map/ppermute | solution.py:205
  534.7 12.4 %collective-permute-start.44 = (bf16[64,768]{1,0:T(8,128)(2,1)S(1)}, bf16[64,768]{1,0:T(8,128)(2,1)S(1)}, u32[]{:S(2)}, u32[]{:S(2)}) collective-permute-start(bf16[64,768]{1,0:T(8,128)(2,1)S(1)} %bitcast.213), channel_id=1, source_target_pairs={{0,24},{8,16},{16,8},{24,0},{1,25},{9,17},{17,9},{25,1},{2,26},{10... | collective-permute-start | bytes 294920 | tf_op jit(solution)/shard_map/ppermute | solution.py:205
  536.4 10.0 %collective-permute-start.46 = (f32[2,256]{1,0:T(2,128)S(1)}, f32[2,256]{1,0:T(2,128)S(1)}, u32[]{:S(2)}, u32[]{:S(2)}) collective-permute-start(f32[2,256]{1,0:T(2,128)S(1)} %add.240), channel_id=1, source_target_pairs={{0,16},{8,24},{16,0},{24,8},{1,17},{9,25},{17,1},{25,9},{2,18},{10... | collective-permute-start | bytes 6152 | tf_op jit(solution)/shard_map/ppermute | solution.py:205
  (24 other events, 165.0 us)
Sparse Core Ops, SparseCore 0:
  9.6 59.0 all-gather.11
  131.4 49.8 reduce-scatter.4
  185.4 45.7 all-gather.5
  233.3 45.6 all-gather.7
  281.1 48.7 reduce-scatter.6
  339.7 48.1 reduce-scatter.8
  398.3 44.7 all-gather.9
  498.0 57.1 reduce-scatter.10

commit v4 on v3

--- a/solution.py
+++ b/solution.py
@@ -294,6 +294,40 @@
     return sum((part.astype(F32) for part in got), dp_block(partial, 0, axis).astype(F32))
 
 
+def scatter_halves(partial):
+    if lax.axis_size("dp") != 4:
+        return scatter_first(partial, 1, 1)
+    half = partial.shape[0] // 2
+    beside, across, far = (dp_block(partial, mask, 1) for mask in (1, 2, 3))
+    top = jnp.stack([beside[:half], far[:half]])
+    low = jnp.stack([across[half:], far[half:]])
+    return (send(top, 1), send(low, 2))
+
+
+def halves_next(partial, got):
+    if lax.axis_size("dp") != 4:
+        return got
+    half = partial.shape[0] // 2
+    beside, across = (dp_block(partial, mask, 1).astype(F32) for mask in (1, 2))
+    top, low = (part[1].astype(F32) for part in got)
+    return (
+        send((across[:half] + top).astype(BF16), 2),
+        send((beside[half:] + low).astype(BF16), 1),
+    )
+
+
+def halves_end(partial, got, last):
+    if lax.axis_size("dp") != 4:
+        return got.astype(F32)
+    half = partial.shape[0] // 2
+    own = dp_block(partial, 0, 1).astype(F32)
+    sums = [
+        rows + first[0].astype(F32) + second.astype(F32)
+        for rows, first, second in zip((own[:half], own[half:]), got, last)
+    ]
+    return jnp.concatenate(sums, axis=0)
+
+
 def scatter_direct(partial, axis):
     return scatter_end(partial, scatter_begin(partial, axis), axis)
 
@@ -485,7 +519,7 @@
     down_out = scatter_seq(down_sum)
     down_partial = dot_tn(mixed, down_grad).astype(BF16)
     down_grad, down_partial = tie((down_grad, down_partial))
-    down_got = scatter_begin(down_partial, 1)
+    down_got = scatter_halves(down_partial)
     mixed_grad = dot_nt(down_grad, my_down)
     gate_grad = (
         mixed_grad * up_vals * sigmoid_gate * (1.0 + gate_vals * (1.0 - sigmoid_gate))
@@ -516,22 +550,27 @@
         ],
         axis=1,
     )
-    gu_summed, down_partial = tie((gu_summed, down_partial))
-    grad_down = scatter_end(down_partial, down_got, 1)
+    down_last = halves_next(down_partial, down_got)
+    gu_summed, down_last = tie((gu_summed, down_last))
     branch_grad, gu_summed = tie((branch_grad, gu_summed))
     gu_blocks = exchange(gu_summed, "seq")
 
+    out_partial = dot_tn(attended, branch_grad).astype(BF16)
     attended_grad = dot_nt(branch_grad, my_out).astype(BF16)
+    attended_grad, out_partial = tie((attended_grad, out_partial))
+    out_got = scatter_begin(out_partial, 1)
     qkv_grad = attend_back(saved, attended_grad, cosine, sine, lengths)
+    qkv_grad, down_last = tie((qkv_grad, down_last))
+    grad_down = halves_end(down_partial, down_got, down_last)
+    qkv_partial = dot_tn(normed, qkv_grad).astype(BF16).reshape(seqs, ranks, sub, -1)
+    qkv_partial, qkv_grad = tie((qkv_partial, qkv_grad))
+    qkv_summed = scatter_direct(qkv_partial, 1).astype(BF16)
     normed_partial = dot_nt(qkv_grad, my_qkv)
-    qkv_partial = dot_tn(normed, qkv_grad).astype(BF16).reshape(seqs, ranks, sub, -1)
-    qkv_summed = scatter_direct(qkv_partial, 1).astype(BF16)
-    out_partial = dot_tn(attended, branch_grad).astype(BF16)
     unit_all = x_all * inv_all
     gain_first_term = jnp.sum(normed_partial * unit_all, axis=0)
     gains_term = jnp.stack([gain_first_term, gain_second_term]).reshape(2, seqs, -1)
     qkv_blocks = with_gains(qkv_summed, gains_term.transpose(1, 0, 2))
-    grad_out = scatter_direct(out_partial, 1)
+    grad_out = scatter_end(out_partial, out_got, 1)
     normed_sum, gu_blocks, grad_down, qkv_blocks, grad_out = tie(
         (normed_partial.astype(BF16), gu_blocks, grad_down, qkv_blocks, grad_out)
     )

time: 571 us -> 575 us (level)
  matrix products: 71.5 us -> 79.2 us
  waiting for transfers between devices: 255 us -> 248 us
    all_gather x4, waiting for transfers between devices: 30 us -> 22.9 us  [gather_seq(): return lax.all_gather(shard, 'seq', axis=0, tiled=True)]
    ppermute x47 -> x48, starting transfers between devices: 52.8 us -> 54.7 us  [send(): return lax.ppermute(value, 'dp', flip(mask, lax.axis_size('dp')))]
    ppermute x47 -> x48, waiting for transfers between devices: 126 us -> 125 us  [send(): return lax.ppermute(value, 'dp', flip(mask, lax.axis_size('dp')))]
  transfers between devices with their start and end apart: 59 -> 60, of which waited for: 26 -> 27; matrix products, arithmetic and copies ran while one was open for 29% -> 31% of each run, Pallas kernels for 7% -> 7%
where the time goes in v4:
time: 575 us; the launch traced here: 569 us
  waiting for transfers between devices  248 us (43%)
  matrix products  79.2 us (14%)
  starting transfers between devices  74.1 us (13%)
  other arithmetic  59.1 us (10%)
  local copies, waits for them, and re-layouts  52.1 us (9%)
  Pallas kernels  40.9 us (7%)
  between operations  16 us (3%)
    ppermute x48, waiting for transfers between devices, send(): return lax.ppermute(value, 'dp', flip(mask, lax.axis_size('dp')))  125 us
    reduce_scatter x4, waiting for transfers between devices, scatter_seq(): lax.psum_scatter(partial.astype(BF16), 'seq', scatter_dimension=0, tiled=...  90 us
    ppermute x48, starting transfers between devices, send(): return lax.ppermute(value, 'dp', flip(mask, lax.axis_size('dp')))  54.7 us
    dot_general x5, matrix products, dot_nt(): lax.dot_general(left, right, (((1,), (1,)), ((), ())), preferred_element_...  33.6 us
    dot_general x5, matrix products, dot_tn(): lax.dot_general(left, right, (((0,), (0,)), ((), ())), preferred_element_...  31.1 us
    all_gather x4, waiting for transfers between devices, gather_seq(): return lax.all_gather(shard, 'seq', axis=0, tiled=True)  22.9 us
    pallas_call x1, Pallas kernels, gate_up_of(): pl.pallas_call(gate_up_kernel, out_shape=(shape((slots, ff), F32),) * 2 +...  20.1 us
    all_to_all x4, starting transfers between devices, exchange(): lax.all_to_all(blocks, axis_name, split_axis=0, concat_axis=0, tiled=True)  18.7 us
  transfers between devices with their start and end apart: 60, of which 27 were waited for; matrix products, arithmetic and copies ran while one was open for 31% of the time, Pallas kernels for 7%

profile of v4, /device:TPU:0, one launch (start us, length us, event | category | flops | bytes accessed | tf_op | source)
XLA Modules:
  0.0 569.5 jit_solution(9717465023170736389)
XLA Ops:
  9.0 4.0 collective-permute-start.2
  15.0 3.2 collective-permute-done
  18.4 3.5 reshape.157
  26.9 5.0 all-to-all-start
  33.8 4.1 collective-permute-done.3
  39.2 11.0 %collective-permute-done.4 = bf16[4,64,1024]{2,0,1:T(4,128)(2,1)} collective-permute-done((bf16[4,64,1024]{2,0,1:T(4,128)(2,1)}, bf16[4,64,1024]{2,0,1:T(4,128)(2,1)}, u32[]{:S(2)}, u32[]{:S(2)}) %collective-permute-start.4) | collective-permute-done | bytes 524320 | tf_op jit(solution)/shard_map/ppermute | solution.py:205
  51.7 6.7 %all-to-all-done = bf16[8,72,384]{2,1,0:T(8,128)(2,1)S(1)} async-done(((bf16[8,72,384]{2,1,0:T(8,128)(2,1)}), bf16[8,72,384]{2,1,0:T(8,128)(2,1)S(1)}, u32[]{:S(2)}, u32[]{:S(2)}) %all-to-all-start) | async-done | bytes 442400 | tf_op jit(solution)/shard_map/all_to_all | solution.py:343
  60.0 4.3 all-to-all-start.1
  64.6 2.5 fusion.37
  68.7 2.0 collective-permute-start.8
  72.9 7.7 %collective-permute-done.6 = bf16[8,1,64,384]{3,2,1,0:T(8,128)(2,1)S(1)} collective-permute-done((bf16[8,1,64,384]{3,2,1,0:T(8,128)(2,1)S(1)}, bf16[8,1,64,384]{3,2,1,0:T(8,128)(2,1)S(1)}, u32[]{:S(2)}, u32[]{:S(2)}) %collective-permute-start.6) | collective-permute-done | bytes 393248 | tf_op jit(solution)/shard_map/ppermute | solution.py:205
  82.2 6.0 %collective-permute-done.8 = bf16[8,1,64,384]{3,2,1,0:T(8,128)(2,1)S(1)} collective-permute-done((bf16[8,1,64,384]{3,2,1,0:T(8,128)(2,1)S(1)}, bf16[8,1,64,384]{3,2,1,0:T(8,128)(2,1)S(1)}, u32[]{:S(2)}, u32[]{:S(2)}) %collective-permute-start.8) | collective-permute-done | bytes 393248 | tf_op jit(solution)/shard_map/ppermute | solution.py:205
  95.5 3.1 fusion.4
  98.6 3.8 fusion.14.qkv_ref
  106.4 10.0 %shard_map.135 = (bf16[1024,256]{1,0:T(8,128)(2,1)S(1)}, bf16[1024,256]{1,0:T(8,128)(2,1)S(1)}, bf16[1024,128]{1,0:T(8,128)(2,1)S(1)}, bf16[1024,128]{1,0:T(8,128)(2,1)S(1)}, f32[8,1024]{1,0:T(8,128)S(1)}) custom-call(s32[1]{0:T(128)} %copy.231.length_ref, f32[1024,384]{1,0:T(8,128)S(1)} %fusion.14.qkv_ref, f32[1024,128]{1,0:T(8,128)S(1)} %get-tuple-element.206.cos_ref, ...), custom_call_target="tpu_custom_call" | custom-call | flops 1073741824 | bytes 3145728 | tf_op jit(solution)/shard_map/pallas_call | solution.py:117
  117.8 8.0 %collective-permute-done.11 = bf16[256,512]{1,0:T(8,128)(2,1)S(1)} collective-permute-done((bf16[256,512]{1,0:T(8,128)(2,1)S(1)}, bf16[256,512]{1,0:T(8,128)(2,1)S(1)}, u32[]{:S(2)}, u32[]{:S(2)}) %collective-permute-start.11) | collective-permute-done | bytes 262176 | tf_op jit(solution)/shard_map/ppermute | solution.py:205
  126.6 4.7 convolution_convert_fusion
  131.3 3.2 slice_bitcast_fusion
  138.5 42.7 %reduce-scatter.5.cloned.1.call-done = bf16[128,2048]{1,0:T(8,128)(2,1)} async-done(((bf16[1024,2048]{1,0:T(8,128)(2,1)}), bf16[128,2048]{1,0:T(8,128)(2,1)}) %reduce-scatter.5.cloned.1.call-update) | async-done | bytes 524304 | tf_op jit(solution)/shard_map/reduce_scatter | solution.py:351
  189.0 2.0 fusion.30
  191.0 28.5 %collective-permute-done.22 = bf16[512,512]{1,0:T(8,128)(2,1)} collective-permute-done((bf16[512,512]{1,0:T(8,128)(2,1)}, bf16[512,512]{1,0:T(8,128)(2,1)}, u32[]{:S(2)}, u32[]{:S(2)}) %collective-permute-start.22) | collective-permute-done | bytes 524320 | tf_op jit(solution)/shard_map/ppermute | solution.py:205
  220.7 10.0 %all-gather.6.cloned.1.call-done.x_ref = bf16[1024,2048]{1,0:T(8,128)(2,1)} async-done(((bf16[128,2048]{1,0:T(8,128)(2,1)}), bf16[1024,2048]{1,0:T(8,128)(2,1)}) %all-gather.6.cloned.1.call-update) | async-done | bytes 4194320 | tf_op jit(solution)/shard_map/all_gather | solution.py:347
  236.1 20.1 %shard_map.136 = (f32[1024,1024]{1,0:T(8,128)}, f32[1024,1024]{1,0:T(8,128)}, bf16[8,4,64,1024]{3,2,1,0:T(8,128)(2,1)}, bf16[8,4,64,1024]{3,2,1,0:T(8,128)(2,1)}) custom-call(s32[1]{0:T(128)} %bitcast.33.me_ref, bf16[1024,2048]{1,0:T(8,128)(2,1)} %all-gather.6.cloned.1.call-done.x_ref, bf16[8,64,1024]{2,1,0:T(8,128)(2,1)} %get-tuple-element.190.refs_0_, ...), custom_call_target="tpu_custom_call" | custom-call | flops 8589934592 | bytes 25165824 | tf_op jit(solution)/shard_map/pallas_call | solution.py:401
  256.2 4.9 multiply_convert_fusion.2
  262.4 6.0 %convolution_convert_fusion.4 = bf16[1024,2048]{1,0:T(8,128)(2,1)} fusion(bf16[1024,1024]{1,0:T(8,128)(2,1)S(1)} %multiply_convert_fusion.2, bf16[1024,2048]{1,0:T(8,128)(2,1)S(1)} %maximum_dynamic-update-slice_fusion.2), kind=kOutput, calls=%fused_computation.17 | convolution fusion | flops 4297064448 | bytes 10485760 | tf_op jit(solution)/shard_map/dot_general | solution.py:29
  268.4 10.0 %all-gather.8.cloned.1.call-done = bf16[1024,2048]{1,0:T(8,128)(2,1)} async-done(((bf16[128,2048]{1,0:T(8,128)(2,1)}), bf16[1024,2048]{1,0:T(8,128)(2,1)}) %all-gather.8.cloned.1.call-update) | async-done | bytes 4194320 | tf_op jit(solution)/shard_map/all_gather | solution.py:347
  278.5 7.5 %convolution_convert_fusion.3 = bf16[1024,2048]{1,0:T(8,128)(2,1)S(1)} fusion(bf16[1024,1024]{1,0:T(8,128)(2,1)} %copy-done.17, bf16[1024,2048]{1,0:T(8,128)(2,1)} %all-gather.8.cloned.1.call-done), kind=kOutput, calls=%fused_computation.16 | convolution fusion | flops 4297064448 | bytes 10485760 | tf_op jit(solution)/shard_map/dot_general | solution.py:37
  291.7 9.6 %multiply_convert_fusion = (bf16[1024,1024]{1,0:T(8,128)(2,1)}, bf16[1024,1024]{1,0:T(8,128)(2,1)S(1)}) fusion(f32[1024,1024]{1,0:T(8,128)S(1)} %copy-done.10, f32[1024,1024]{1,0:T(8,128)S(1)} %copy-done.11, bf16[1024,2048]{1,0:T(8,128)(2,1)} %all-gather.8.cloned.1.call-done, bf16[1024,2048]{1,0:T(8,128)(2,1)S(1)} %copy-done.13), kind=kOutput, calls=%fused_computation.9 | convolution fusion | flops 4308598784 | bytes 20971520 | tf_op jit(solution)/shard_map/dot_general | solution.py:33
  301.4 6.7 %fusion.44 = f32[1024,2048]{1,0:T(8,128)} fusion(bf16[1024,1024]{1,0:T(8,128)(2,1)S(1)} %get-tuple-element.172, bf16[2048,1024]{1,0:T(8,128)(2,1)S(1)} %bitcast.240), kind=kOutput, calls=%fused_computation.165 | convolution fusion | flops 4294967296 | bytes 14680064 | tf_op jit(solution)/shard_map/dot_general | solution.py:33
  308.2 8.4 %add_convert_fusion = bf16[1024,2048]{1,0:T(8,128)(2,1)} fusion(f32[1024,2048]{1,0:T(8,128)} %fusion.44, bf16[1024,1024]{1,0:T(8,128)(2,1)S(1)} %copy-done.28, bf16[2048,1024]{1,0:T(8,128)(2,1)S(1)} %bitcast.239), kind=kOutput, calls=%fused_computation.7 | convolution fusion | flops 4299161600 | bytes 18874368 | tf_op jit(solution)/shard_map/dot_general | solution.py:33
  316.5 9.7 %convolution_convert_fusion.1 = bf16[2048,1024]{1,0:T(8,128)(2,1)} fusion(bf16[1024,2048]{1,0:T(8,128)(2,1)} %all-gather.6.cloned.1.call-done.x_ref, bf16[1024,1024]{1,0:T(8,128)(2,1)} %get-tuple-element.171), kind=kOutput, calls=%fused_computation.14 | convolution fusion | flops 4297064448 | bytes 10485760 | tf_op jit(solution)/shard_map/dot_general | solution.py:37
  326.2 6.4 %convolution_convert_fusion.2 = bf16[2048,1024]{1,0:T(8,128)(2,1)} fusion(bf16[1024,2048]{1,0:T(8,128)(2,1)S(1)} %copy-done.22, bf16[1024,1024]{1,0:T(8,128)(2,1)S(1)} %copy-done.27), kind=kOutput, calls=%fused_computation.15 | convolution fusion | flops 4297064448 | bytes 10485760 | tf_op jit(solution)/shard_map/dot_general | solution.py:37
  332.7 2.1 convert_element_type.272
  334.9 3.2 dynamic-slice_bitcast_fusion.2
  343.7 40.1 %reduce-scatter.9.cloned.1.call-done = bf16[128,2048]{1,0:T(8,128)(2,1)} async-done(((bf16[1024,2048]{1,0:T(8,128)(2,1)}), bf16[128,2048]{1,0:T(8,128)(2,1)}) %reduce-scatter.9.cloned.1.call-update) | async-done | bytes 524304 | tf_op jit(solution)/shard_map/reduce_scatter | solution.py:351
  386.3 3.0 collective-permute-done.28
  390.9 2.9 multiply_convert_fusion.3
  393.8 3.1 fusion.5
  398.4 3.1 fusion.8
  404.4 2.5 fusion.26
  408.1 15.2 %collective-permute-done.31 = bf16[8,64,1024]{2,1,0:T(8,128)(2,1)} collective-permute-done((bf16[8,64,1024]{2,1,0:T(8,128)(2,1)}, bf16[8,64,1024]{2,1,0:T(8,128)(2,1)}, u32[]{:S(2)}, u32[]{:S(2)}) %collective-permute-start.31) | collective-permute-done | bytes 1048608 | tf_op jit(solution)/shard_map/ppermute | solution.py:205
  423.3 2.5 fusion.23
  425.8 2.0 collective-permute-done.30
  427.8 2.5 fusion.22
  432.5 4.1 collective-permute-done.32
  436.6 3.0 all-gather.10.cloned.1.call-done
  439.6 4.4 all-to-all-start.2
  444.4 3.6 convolution_convert_fusion.6
  448.0 2.9 convolution_convert_fusion.7.grad_ref
  451.0 10.9 %shard_map.137 = bf16[1024,384]{1,0:T(8,128)(2,1)S(1)} custom-call(s32[1]{0:T(128)} %copy.231.length_ref, bf16[1024,256]{1,0:T(8,128)(2,1)S(1)} %get-tuple-element.129.q_ref, bf16[1024,128]{1,0:T(8,128)(2,1)S(1)} %get-tuple-element.130.k_ref, bf16[1024,128]{1,0:T(8,128)(2,1)S(1)} %get-tuple-element.131.v_ref, f32[8,1024]{1,0:T(8,128)S(1)} %get-tuple-element.132.lse_ref, ...), custom_call_target="tpu_custom_call" | custom-call | flops 2684354560 | bytes 3145728 | tf_op jit(solution)/shard_map/pallas_call | solution.py:186
  465.5 3.8 convolution_convert_fusion.5
  469.4 6.0 %fusion.3 = (bf16[2048]{0:T(1024)(128)(2,1)S(1)}, bf16[1024,2048]{1,0:T(8,128)(2,1)}) fusion(bf16[1024,2048]{1,0:T(8,128)(2,1)S(1)} %bitcast.216, f32[1024]{0:T(1024)S(1)} %add_rsqrt_fusion, bf16[1024,384]{1,0:T(8,128)(2,1)S(1)} %shard_map.137, bf16[2048,384]{1,0:T(8,128)(2,1)} %bitcast.25), kind=kOutput, calls=%fused_computation.5 | convolution fusion | flops 1621096448 | bytes 10756096 | tf_op jit(solution)/shard_map/dot_general | solution.py:33
  479.8 1.9 fusion.25
  483.8 2.1 convert_add_fusion.8
  485.9 2.9 collective-permute-done.34
  488.8 8.0 %collective-permute-done.36 = bf16[8,64,384]{2,1,0:T(8,128)(2,1)S(1)} collective-permute-done((bf16[8,64,384]{2,1,0:T(8,128)(2,1)S(1)}, bf16[8,64,384]{2,1,0:T(8,128)(2,1)S(1)}, u32[]{:S(2)}, u32[]{:S(2)}) %collective-permute-start.36) | collective-permute-done | bytes 393248 | tf_op jit(solution)/shard_map/ppermute | solution.py:205
  496.8 3.4 collective-permute-done.35
  507.5 5.0 all-to-all-start.3
  514.0 4.5 collective-permute-done.40
  519.6 10.5 %collective-permute-done.41 = bf16[4,64,1024]{2,1,0:T(8,128)(2,1)} collective-permute-done((bf16[4,64,1024]{2,1,0:T(8,128)(2,1)}, bf16[4,64,1024]{2,1,0:T(8,128)(2,1)}, u32[]{:S(2)}, u32[]{:S(2)}) %collective-permute-start.41) | collective-permute-done | bytes 524320 | tf_op jit(solution)/shard_map/ppermute | solution.py:205
  531.3 2.2 all-to-all-done.3
  542.3 2.7 copy.169
  545.0 5.8 %copy.178 = f32[32,8,4,1024]{3,1,2,0:T(8,128)} copy(f32[32,8,4,1024]{3,2,1,0:T(4,128)S(1)} %bitcast.204) | data formatting | bytes 8388608
  552.4 7.2 %reduce-scatter.11.cloned.1.call-done = bf16[128,2048]{1,0:T(8,128)(2,1)} async-done(((bf16[1024,2048]{1,0:T(8,128)(2,1)}), bf16[128,2048]{1,0:T(8,128)(2,1)}) %reduce-scatter.11.cloned.1.call-update) | async-done | bytes 524304 | tf_op jit(solution)/shard_map/reduce_scatter | solution.py:351
  (260 shorter events, 111.0 us)
Async XLA Ops:
  7.2 81.8 %all-gather.12.cloned.1.call-start = ((), (), s32[]{:S(2)}) async-start(), calls=%async_computation.15 | async-start | bytes 4718592 | tf_op jit(solution)/shard_map/all_gather | solution.py:347
  9.0 9.3 %collective-permute-start.2 = (bf16[64,768]{1,0:T(8,128)(2,1)S(1)}, bf16[64,768]{1,0:T(8,128)(2,1)S(1)}, u32[]{:S(2)}, u32[]{:S(2)}) collective-permute-start(bf16[64,768]{1,0:T(8,128)(2,1)S(1)} %get-tuple-element.215), channel_id=1, source_target_pairs={{0,24},{8,16},{16,8},{24,0},{1,25},{9,17},{17,9},{25,1},{2,26},{10... | collective-permute-start | bytes 294920 | tf_op jit(solution)/shard_map/ppermute | solution.py:205
  13.0 5.2 collective-permute-start.1
  13.5 4.7 collective-permute-start
  23.6 14.4 %collective-permute-start.3 = (bf16[4,64,1024]{2,0,1:T(4,128)(2,1)}, bf16[4,64,1024]{2,0,1:T(4,128)(2,1)}, u32[]{:S(2)}, u32[]{:S(2)}) collective-permute-start(bf16[4,64,1024]{2,0,1:T(4,128)(2,1)} %get-tuple-element.193), channel_id=1, source_target_pairs={{0,8},{8,0},{16,24},{24,16},{1,9},{9,1},{17,25},{25,17},{2,10},{10... | collective-permute-start | bytes 1572872 | tf_op jit(solution)/shard_map/ppermute | solution.py:205
  25.3 24.9 %collective-permute-start.4 = (bf16[4,64,1024]{2,0,1:T(4,128)(2,1)}, bf16[4,64,1024]{2,0,1:T(4,128)(2,1)}, u32[]{:S(2)}, u32[]{:S(2)}) collective-permute-start(bf16[4,64,1024]{2,0,1:T(4,128)(2,1)} %get-tuple-element.192), channel_id=1, source_target_pairs={{0,16},{8,24},{16,0},{24,8},{1,17},{9,25},{17,1},{25,9},{2,18},{10... | collective-permute-start | bytes 1572872 | tf_op jit(solution)/shard_map/ppermute | solution.py:205
  26.9 31.5 %all-to-all-start = ((bf16[8,72,384]{2,1,0:T(8,128)(2,1)}), bf16[8,72,384]{2,1,0:T(8,128)(2,1)S(1)}, u32[]{:S(2)}, u32[]{:S(2)}) async-start(bf16[8,72,384]{2,1,0:T(8,128)(2,1)} %copy.151), calls=%async_computation | async-start | bytes 884736 | tf_op jit(solution)/shard_map/all_to_all | solution.py:343
  31.9 19.5 %collective-permute-start.5 = (bf16[4,64,1024]{2,0,1:T(4,128)(2,1)}, bf16[4,64,1024]{2,0,1:T(4,128)(2,1)S(1)}, u32[]{:S(2)}, u32[]{:S(2)}) collective-permute-start(bf16[4,64,1024]{2,0,1:T(4,128)(2,1)} %get-tuple-element.191), channel_id=1, source_target_pairs={{0,24},{8,16},{16,8},{24,0},{1,25},{9,17},{17,9},{25,1},{2,26},{10... | collective-permute-start | bytes 1572872 | tf_op jit(solution)/shard_map/ppermute | solution.py:205
  60.0 66.6 %all-to-all-start.1 = ((bf16[8,2,64,1024]{3,2,1,0:T(8,128)(2,1)}), bf16[8,2,64,1024]{3,2,1,0:T(8,128)(2,1)}, u32[]{:S(2)}, u32[]{:S(2)}) async-start(bf16[8,2,64,1024]{3,2,1,0:T(8,128)(2,1)} %copy.156), calls=%async_computation.1 | async-start | bytes 4194304 | tf_op jit(solution)/shard_map/all_to_all | solution.py:343
  64.3 24.7 %copy-start.21 = (bf16[256,512]{1,0:T(8,128)(2,1)S(1)}, bf16[256,512]{1,0:T(8,128)(2,1)}, u32[]{:S(2)}) copy-start(bf16[256,512]{1,0:T(8,128)(2,1)} %param.11) | copy-start | bytes 786436
  64.3 26.4 %copy-start.8 = (bf16[1024,512]{1,0:T(8,128)(2,1)S(1)}, bf16[1024,512]{1,0:T(8,128)(2,1)}, u32[]{:S(2)}) copy-start(bf16[1024,512]{1,0:T(8,128)(2,1)} %param.13) | copy-start | bytes 3145732
  64.4 116.9 %reduce-scatter.5.cloned.1.call-start = ((), (), s32[]{:S(2)}) async-start(), calls=%async_computation.8 | async-start | bytes 4718592 | tf_op jit(solution)/shard_map/reduce_scatter | solution.py:351
  67.1 14.3 %collective-permute-start.7 = (bf16[8,1,64,384]{3,2,1,0:T(8,128)(2,1)S(1)}, bf16[8,1,64,384]{3,2,1,0:T(8,128)(2,1)S(1)}, u32[]{:S(2)}, u32[]{:S(2)}) collective-permute-start(bf16[8,1,64,384]{3,2,1,0:T(8,128)(2,1)S(1)} %slice_bitcast_fusion.3), channel_id=1, source_target_pairs={{0,16},{8,24},{16,0},{24,8},{1,17},{9,25},{17,1},{25,9},{2,18},{10... | collective-permute-start | bytes 1179656 | tf_op jit(solution)/shard_map/ppermute | solution.py:205
  68.6 12.0 %collective-permute-start.6 = (bf16[8,1,64,384]{3,2,1,0:T(8,128)(2,1)S(1)}, bf16[8,1,64,384]{3,2,1,0:T(8,128)(2,1)S(1)}, u32[]{:S(2)}, u32[]{:S(2)}) collective-permute-start(bf16[8,1,64,384]{3,2,1,0:T(8,128)(2,1)S(1)} %slice_bitcast_fusion.3), channel_id=1, source_target_pairs={{0,8},{8,0},{16,24},{24,16},{1,9},{9,1},{17,25},{25,17},{2,10},{10... | collective-permute-start | bytes 1179656 | tf_op jit(solution)/shard_map/ppermute | solution.py:205
  68.7 19.5 %collective-permute-start.8 = (bf16[8,1,64,384]{3,2,1,0:T(8,128)(2,1)S(1)}, bf16[8,1,64,384]{3,2,1,0:T(8,128)(2,1)S(1)}, u32[]{:S(2)}, u32[]{:S(2)}) collective-permute-start(bf16[8,1,64,384]{3,2,1,0:T(8,128)(2,1)S(1)} %slice_bitcast_fusion.3), channel_id=1, source_target_pairs={{0,24},{8,16},{16,8},{24,0},{1,25},{9,17},{17,9},{25,1},{2,26},{10... | collective-permute-start | bytes 1179656 | tf_op jit(solution)/shard_map/ppermute | solution.py:205
  89.0 13.4 %collective-permute-start.10 = (bf16[256,512]{1,0:T(8,128)(2,1)S(1)}, bf16[256,512]{1,0:T(8,128)(2,1)S(1)}, u32[]{:S(2)}, u32[]{:S(2)}) collective-permute-start(bf16[256,512]{1,0:T(8,128)(2,1)S(1)} %copy-done.21), channel_id=1, source_target_pairs={{0,16},{8,24},{16,0},{24,8},{1,17},{9,25},{17,1},{25,9},{2,18},{10... | collective-permute-start | bytes 786440 | tf_op jit(solution)/shard_map/ppermute | solution.py:205
  90.4 14.2 %collective-permute-start.9 = (bf16[256,512]{1,0:T(8,128)(2,1)S(1)}, bf16[256,512]{1,0:T(8,128)(2,1)S(1)}, u32[]{:S(2)}, u32[]{:S(2)}) collective-permute-start(bf16[256,512]{1,0:T(8,128)(2,1)S(1)} %copy-done.21), channel_id=1, source_target_pairs={{0,8},{8,0},{16,24},{24,16},{1,9},{9,1},{17,25},{25,17},{2,10},{10... | collective-permute-start | bytes 786440 | tf_op jit(solution)/shard_map/ppermute | solution.py:205
  91.8 34.7 %collective-permute-start.15 = (bf16[512,512]{1,0:T(8,128)(2,1)}, bf16[512,512]{1,0:T(8,128)(2,1)S(1)}, u32[]{:S(2)}, u32[]{:S(2)}) collective-permute-start(bf16[512,512]{1,0:T(8,128)(2,1)} %get-tuple-element.202), channel_id=1, source_target_pairs={{0,16},{8,24},{16,0},{24,8},{1,17},{9,25},{17,1},{25,9},{2,18},{10... | collective-permute-start | bytes 1572872 | tf_op jit(solution)/shard_map/ppermute | solution.py:205
  93.5 33.1 %collective-permute-start.13 = (bf16[512,512]{1,0:T(8,128)(2,1)}, bf16[512,512]{1,0:T(8,128)(2,1)}, u32[]{:S(2)}, u32[]{:S(2)}) collective-permute-start(bf16[512,512]{1,0:T(8,128)(2,1)} %get-tuple-element.202), channel_id=1, source_target_pairs={{0,8},{8,0},{16,24},{24,16},{1,9},{9,1},{17,25},{25,17},{2,10},{10... | collective-permute-start | bytes 1572872 | tf_op jit(solution)/shard_map/ppermute | solution.py:205
  94.1 32.5 %collective-permute-start.14 = (bf16[512,512]{1,0:T(8,128)(2,1)}, bf16[512,512]{1,0:T(8,128)(2,1)}, u32[]{:S(2)}, u32[]{:S(2)}) collective-permute-start(bf16[512,512]{1,0:T(8,128)(2,1)} %get-tuple-element.203), channel_id=1, source_target_pairs={{0,16},{8,24},{16,0},{24,8},{1,17},{9,25},{17,1},{25,9},{2,18},{10... | collective-permute-start | bytes 1572872 | tf_op jit(solution)/shard_map/ppermute | solution.py:205
  102.4 24.2 %collective-permute-start.12 = (bf16[512,512]{1,0:T(8,128)(2,1)}, bf16[512,512]{1,0:T(8,128)(2,1)}, u32[]{:S(2)}, u32[]{:S(2)}) collective-permute-start(bf16[512,512]{1,0:T(8,128)(2,1)} %get-tuple-element.203), channel_id=1, source_target_pairs={{0,8},{8,0},{16,24},{24,16},{1,9},{9,1},{17,25},{25,17},{2,10},{10... | collective-permute-start | bytes 1572872 | tf_op jit(solution)/shard_map/ppermute | solution.py:205
  104.7 21.2 %collective-permute-start.11 = (bf16[256,512]{1,0:T(8,128)(2,1)S(1)}, bf16[256,512]{1,0:T(8,128)(2,1)S(1)}, u32[]{:S(2)}, u32[]{:S(2)}) collective-permute-start(bf16[256,512]{1,0:T(8,128)(2,1)S(1)} %copy-done.21), channel_id=1, source_target_pairs={{0,24},{8,16},{16,8},{24,0},{1,25},{9,17},{17,9},{25,1},{2,26},{10... | collective-permute-start | bytes 786440 | tf_op jit(solution)/shard_map/ppermute | solution.py:205
  131.3 51.2 %copy-start.3 = (bf16[1,128,2048]{2,1,0:T(8,128)(2,1)S(1)}, bf16[1,128,2048]{2,1,0:T(8,128)(2,1)}, u32[]{:S(2)}) copy-start(bf16[1,128,2048]{2,1,0:T(8,128)(2,1)} %param.8) | copy-start | bytes 1572868
  131.3 99.4 %all-gather.6.cloned.1.call-start = ((), (), s32[]{:S(2)}) async-start(), calls=%async_computation.9 | async-start | bytes 4718592 | tf_op jit(solution)/shard_map/all_gather | solution.py:347
  134.5 47.9 %collective-permute-start.19 = (bf16[8,64,1024]{2,1,0:T(8,128)(2,1)}, bf16[8,64,1024]{2,1,0:T(8,128)(2,1)}, u32[]{:S(2)}, u32[]{:S(2)}) collective-permute-start(bf16[8,64,1024]{2,1,0:T(8,128)(2,1)} %get-tuple-element.189.refs_4_), channel_id=1, source_target_pairs={{0,8},{8,0},{16,24},{24,16},{1,9},{9,1},{17,25},{25,17},{2,10},{10... | collective-permute-start | bytes 3145736 | tf_op jit(solution)/shard_map/ppermute | solution.py:205
  135.9 46.6 %collective-permute-start.18 = (bf16[8,64,1024]{2,1,0:T(8,128)(2,1)}, bf16[8,64,1024]{2,1,0:T(8,128)(2,1)}, u32[]{:S(2)}, u32[]{:S(2)}) collective-permute-start(bf16[8,64,1024]{2,1,0:T(8,128)(2,1)} %get-tuple-element.189.refs_4_), channel_id=1, source_target_pairs={{0,16},{8,24},{16,0},{24,8},{1,17},{9,25},{17,1},{25,9},{2,18},{10... | collective-permute-start | bytes 3145736 | tf_op jit(solution)/shard_map/ppermute | solution.py:205
  136.5 45.9 %collective-permute-start.17 = (bf16[8,64,1024]{2,1,0:T(8,128)(2,1)}, bf16[8,64,1024]{2,1,0:T(8,128)(2,1)}, u32[]{:S(2)}, u32[]{:S(2)}) collective-permute-start(bf16[8,64,1024]{2,1,0:T(8,128)(2,1)} %get-tuple-element.190.refs_0_), channel_id=1, source_target_pairs={{0,16},{8,24},{16,0},{24,8},{1,17},{9,25},{17,1},{25,9},{2,18},{10... | collective-permute-start | bytes 3145736 | tf_op jit(solution)/shard_map/ppermute | solution.py:205
  137.9 44.6 %collective-permute-start.16 = (bf16[8,64,1024]{2,1,0:T(8,128)(2,1)}, bf16[8,64,1024]{2,1,0:T(8,128)(2,1)}, u32[]{:S(2)}, u32[]{:S(2)}) collective-permute-start(bf16[8,64,1024]{2,1,0:T(8,128)(2,1)} %get-tuple-element.190.refs_0_), channel_id=1, source_target_pairs={{0,8},{8,0},{16,24},{24,16},{1,9},{9,1},{17,25},{25,17},{2,10},{10... | collective-permute-start | bytes 3145736 | tf_op jit(solution)/shard_map/ppermute | solution.py:205
  184.8 93.6 %all-gather.8.cloned.1.call-start = ((), (), s32[]{:S(2)}) async-start(), calls=%async_computation.10 | async-start | bytes 4718592 | tf_op jit(solution)/shard_map/all_gather | solution.py:347
  184.8 35.8 %collective-permute-start.20 = (bf16[8,64,1024]{2,1,0:T(8,128)(2,1)}, bf16[8,64,1024]{2,1,0:T(8,128)(2,1)}, u32[]{:S(2)}, u32[]{:S(2)}) collective-permute-start(bf16[8,64,1024]{2,1,0:T(8,128)(2,1)} %collective-permute-done.16.refs_1_), channel_id=1, source_target_pairs={{0,16},{8,24},{16,0},{24,8},{1,17},{9,25},{17,1},{25,9},{2,18},{10... | collective-permute-start | bytes 3145736 | tf_op jit(solution)/shard_map/ppermute | solution.py:205
  186.4 34.3 %collective-permute-start.21 = (bf16[8,64,1024]{2,1,0:T(8,128)(2,1)}, bf16[8,64,1024]{2,1,0:T(8,128)(2,1)}, u32[]{:S(2)}, u32[]{:S(2)}) collective-permute-start(bf16[8,64,1024]{2,1,0:T(8,128)(2,1)} %collective-permute-done.18.refs_6_), channel_id=1, source_target_pairs={{0,8},{8,0},{16,24},{24,16},{1,9},{9,1},{17,25},{25,17},{2,10},{10... | collective-permute-start | bytes 3145736 | tf_op jit(solution)/shard_map/ppermute | solution.py:205
  187.9 31.6 %collective-permute-start.22 = (bf16[512,512]{1,0:T(8,128)(2,1)}, bf16[512,512]{1,0:T(8,128)(2,1)}, u32[]{:S(2)}, u32[]{:S(2)}) collective-permute-start(bf16[512,512]{1,0:T(8,128)(2,1)} %collective-permute-done.12), channel_id=1, source_target_pairs={{0,16},{8,24},{16,0},{24,8},{1,17},{9,25},{17,1},{25,9},{2,18},{10... | collective-permute-start | bytes 1572872 | tf_op jit(solution)/shard_map/ppermute | solution.py:205
  188.4 32.3 %collective-permute-start.23 = (bf16[512,512]{1,0:T(8,128)(2,1)}, bf16[512,512]{1,0:T(8,128)(2,1)}, u32[]{:S(2)}, u32[]{:S(2)}) collective-permute-start(bf16[512,512]{1,0:T(8,128)(2,1)} %copy-done.19), channel_id=1, source_target_pairs={{0,8},{8,0},{16,24},{24,16},{1,9},{9,1},{17,25},{25,17},{2,10},{10... | collective-permute-start | bytes 1572872 | tf_op jit(solution)/shard_map/ppermute | solution.py:205
  230.7 102.0 %reduce-scatter.7.cloned.1.call-start = ((), (), s32[]{:S(2)}) async-start(), calls=%async_computation.11 | async-start | bytes 4718592 | tf_op jit(solution)/shard_map/reduce_scatter | solution.py:351
  236.1 25.0 %copy-start.12 = (bf16[1024,2048]{1,0:T(8,128)(2,1)}, bf16[1024,2048]{1,0:T(8,128)(2,1)S(1)}, u32[]{:S(2)}) copy-start(bf16[1024,2048]{1,0:T(8,128)(2,1)S(1)} %maximum_dynamic-update-slice_fusion.2) | copy-start | bytes 12582916
  278.4 105.4 %reduce-scatter.9.cloned.1.call-start = ((), (), s32[]{:S(2)}) async-start(), calls=%async_computation.12 | async-start | bytes 4718592 | tf_op jit(solution)/shard_map/reduce_scatter | solution.py:351
  287.4 47.4 %collective-permute-start.24 = (bf16[2,512,512]{2,1,0:T(8,128)(2,1)}, bf16[2,512,512]{2,1,0:T(8,128)(2,1)}, u32[]{:S(2)}, u32[]{:S(2)}) collective-permute-start(bf16[2,512,512]{2,1,0:T(8,128)(2,1)} %pad_maximum_fusion.2), channel_id=1, source_target_pairs={{0,8},{8,0},{16,24},{24,16},{1,9},{9,1},{17,25},{25,17},{2,10},{10... | collective-permute-start | bytes 3145736 | tf_op jit(solution)/shard_map/ppermute | solution.py:205
  289.9 44.9 %collective-permute-start.25 = (bf16[2,512,512]{2,1,0:T(8,128)(2,1)}, bf16[2,512,512]{2,1,0:T(8,128)(2,1)}, u32[]{:S(2)}, u32[]{:S(2)}) collective-permute-start(bf16[2,512,512]{2,1,0:T(8,128)(2,1)} %pad_maximum_fusion.3), channel_id=1, source_target_pairs={{0,16},{8,24},{16,0},{24,8},{1,17},{9,25},{17,1},{25,9},{2,18},{10... | collective-permute-start | bytes 3145736 | tf_op jit(solution)/shard_map/ppermute | solution.py:205
  334.8 104.8 %all-gather.10.cloned.1.call-start = ((), (), s32[]{:S(2)}) async-start(), calls=%async_computation.13 | async-start | bytes 4718592 | tf_op jit(solution)/shard_map/all_gather | solution.py:347
  338.1 47.0 %collective-permute-start.27 = (bf16[8,64,1024]{2,1,0:T(8,128)(2,1)}, bf16[8,64,1024]{2,1,0:T(8,128)(2,1)}, u32[]{:S(2)}, u32[]{:S(2)}) collective-permute-start(bf16[8,64,1024]{2,1,0:T(8,128)(2,1)} %get-tuple-element.177), channel_id=1, source_target_pairs={{0,8},{8,0},{16,24},{24,16},{1,9},{9,1},{17,25},{25,17},{2,10},{10... | collective-permute-start | bytes 3145736 | tf_op jit(solution)/shard_map/ppermute | solution.py:205
  339.6 46.7 %collective-permute-start.26 = (bf16[8,64,1024]{2,1,0:T(8,128)(2,1)}, bf16[8,64,1024]{2,1,0:T(8,128)(2,1)}, u32[]{:S(2)}, u32[]{:S(2)}) collective-permute-start(bf16[8,64,1024]{2,1,0:T(8,128)(2,1)} %get-tuple-element.178), channel_id=1, source_target_pairs={{0,8},{8,0},{16,24},{24,16},{1,9},{9,1},{17,25},{25,17},{2,10},{10... | collective-permute-start | bytes 3145736 | tf_op jit(solution)/shard_map/ppermute | solution.py:205
  341.7 44.6 %collective-permute-start.29 = (bf16[8,64,1024]{2,1,0:T(8,128)(2,1)}, bf16[8,64,1024]{2,1,0:T(8,128)(2,1)}, u32[]{:S(2)}, u32[]{:S(2)}) collective-permute-start(bf16[8,64,1024]{2,1,0:T(8,128)(2,1)} %get-tuple-element.175), channel_id=1, source_target_pairs={{0,16},{8,24},{16,0},{24,8},{1,17},{9,25},{17,1},{25,9},{2,18},{10... | collective-permute-start | bytes 3145736 | tf_op jit(solution)/shard_map/ppermute | solution.py:205
  343.2 46.1 %collective-permute-start.28 = (bf16[8,64,1024]{2,1,0:T(8,128)(2,1)}, bf16[8,64,1024]{2,1,0:T(8,128)(2,1)}, u32[]{:S(2)}, u32[]{:S(2)}) collective-permute-start(bf16[8,64,1024]{2,1,0:T(8,128)(2,1)} %get-tuple-element.176), channel_id=1, source_target_pairs={{0,16},{8,24},{16,0},{24,8},{1,17},{9,25},{17,1},{25,9},{2,18},{10... | collective-permute-start | bytes 3145736 | tf_op jit(solution)/shard_map/ppermute | solution.py:205
  397.0 26.3 %collective-permute-start.31 = (bf16[8,64,1024]{2,1,0:T(8,128)(2,1)}, bf16[8,64,1024]{2,1,0:T(8,128)(2,1)}, u32[]{:S(2)}, u32[]{:S(2)}) collective-permute-start(bf16[8,64,1024]{2,1,0:T(8,128)(2,1)} %fusion.5), channel_id=1, source_target_pairs={{0,8},{8,0},{16,24},{24,16},{1,9},{9,1},{17,25},{25,17},{2,10},{10... | collective-permute-start | bytes 3145736 | tf_op jit(solution)/shard_map/ppermute | solution.py:205
  401.5 26.3 %collective-permute-start.30 = (bf16[8,64,1024]{2,1,0:T(8,128)(2,1)}, bf16[8,64,1024]{2,1,0:T(8,128)(2,1)}, u32[]{:S(2)}, u32[]{:S(2)}) collective-permute-start(bf16[8,64,1024]{2,1,0:T(8,128)(2,1)} %fusion.8), channel_id=1, source_target_pairs={{0,16},{8,24},{16,0},{24,8},{1,17},{9,25},{17,1},{25,9},{2,18},{10... | collective-permute-start | bytes 3145736 | tf_op jit(solution)/shard_map/ppermute | solution.py:205
  407.0 25.5 %collective-permute-start.33 = (bf16[512,512]{1,0:T(8,128)(2,1)}, bf16[512,512]{1,0:T(8,128)(2,1)}, u32[]{:S(2)}, u32[]{:S(2)}) collective-permute-start(bf16[512,512]{1,0:T(8,128)(2,1)} %get-tuple-element.173), channel_id=1, source_target_pairs={{0,8},{8,0},{16,24},{24,16},{1,9},{9,1},{17,25},{25,17},{2,10},{10... | collective-permute-start | bytes 1572872 | tf_op jit(solution)/shard_map/ppermute | solution.py:205
  407.5 29.1 %collective-permute-start.32 = (bf16[512,512]{1,0:T(8,128)(2,1)}, bf16[512,512]{1,0:T(8,128)(2,1)}, u32[]{:S(2)}, u32[]{:S(2)}) collective-permute-start(bf16[512,512]{1,0:T(8,128)(2,1)} %get-tuple-element.174), channel_id=1, source_target_pairs={{0,16},{8,24},{16,0},{24,8},{1,17},{9,25},{17,1},{25,9},{2,18},{10... | collective-permute-start | bytes 1572872 | tf_op jit(solution)/shard_map/ppermute | solution.py:205
  439.6 62.7 %all-to-all-start.2 = ((bf16[8,2,64,1024]{3,2,1,0:T(8,128)(2,1)}), bf16[8,2,64,1024]{3,2,1,0:T(8,128)(2,1)}, u32[]{:S(2)}, u32[]{:S(2)}) async-start(bf16[8,2,64,1024]{3,2,1,0:T(8,128)(2,1)} %pad_maximum_fusion), calls=%async_computation.5 | async-start | bytes 4194304 | tf_op jit(solution)/shard_map/all_to_all | solution.py:343
  444.0 115.6 %reduce-scatter.11.cloned.1.call-start = ((), (), s32[]{:S(2)}) async-start(), calls=%async_computation.14 | async-start | bytes 4718592 | tf_op jit(solution)/shard_map/reduce_scatter | solution.py:351
  462.0 19.7 %collective-permute-start.37 = (bf16[256,512]{1,0:T(8,128)(2,1)S(1)}, bf16[256,512]{1,0:T(8,128)(2,1)}, u32[]{:S(2)}, u32[]{:S(2)}) collective-permute-start(bf16[256,512]{1,0:T(8,128)(2,1)S(1)} %get-tuple-element.199), channel_id=1, source_target_pairs={{0,8},{8,0},{16,24},{24,16},{1,9},{9,1},{17,25},{25,17},{2,10},{10... | collective-permute-start | bytes 786440 | tf_op jit(solution)/shard_map/ppermute | solution.py:205
  463.5 20.3 %collective-permute-start.39 = (bf16[256,512]{1,0:T(8,128)(2,1)S(1)}, bf16[256,512]{1,0:T(8,128)(2,1)}, u32[]{:S(2)}, u32[]{:S(2)}) collective-permute-start(bf16[256,512]{1,0:T(8,128)(2,1)S(1)} %get-tuple-element.200), channel_id=1, source_target_pairs={{0,24},{8,16},{16,8},{24,0},{1,25},{9,17},{17,9},{25,1},{2,26},{10... | collective-permute-start | bytes 786440 | tf_op jit(solution)/shard_map/ppermute | solution.py:205
  465.0 18.8 %collective-permute-start.38 = (bf16[256,512]{1,0:T(8,128)(2,1)S(1)}, bf16[256,512]{1,0:T(8,128)(2,1)}, u32[]{:S(2)}, u32[]{:S(2)}) collective-permute-start(bf16[256,512]{1,0:T(8,128)(2,1)S(1)} %get-tuple-element.201), channel_id=1, source_target_pairs={{0,16},{8,24},{16,0},{24,8},{1,17},{9,25},{17,1},{25,9},{2,18},{10... | collective-permute-start | bytes 786440 | tf_op jit(solution)/shard_map/ppermute | solution.py:205
  476.7 12.1 %collective-permute-start.34 = (bf16[8,64,384]{2,1,0:T(8,128)(2,1)S(1)}, bf16[8,64,384]{2,1,0:T(8,128)(2,1)S(1)}, u32[]{:S(2)}, u32[]{:S(2)}) collective-permute-start(bf16[8,64,384]{2,1,0:T(8,128)(2,1)S(1)} %get-tuple-element.195), channel_id=1, source_target_pairs={{0,8},{8,0},{16,24},{24,16},{1,9},{9,1},{17,25},{25,17},{2,10},{10... | collective-permute-start | bytes 1179656 | tf_op jit(solution)/shard_map/ppermute | solution.py:205
  478.3 18.5 %collective-permute-start.36 = (bf16[8,64,384]{2,1,0:T(8,128)(2,1)S(1)}, bf16[8,64,384]{2,1,0:T(8,128)(2,1)S(1)}, u32[]{:S(2)}, u32[]{:S(2)}) collective-permute-start(bf16[8,64,384]{2,1,0:T(8,128)(2,1)S(1)} %get-tuple-element.196), channel_id=1, source_target_pairs={{0,24},{8,16},{16,8},{24,0},{1,25},{9,17},{17,9},{25,1},{2,26},{10... | collective-permute-start | bytes 1179656 | tf_op jit(solution)/shard_map/ppermute | solution.py:205
  481.7 18.5 %collective-permute-start.35 = (bf16[8,64,384]{2,1,0:T(8,128)(2,1)S(1)}, bf16[8,64,384]{2,1,0:T(8,128)(2,1)S(1)}, u32[]{:S(2)}, u32[]{:S(2)}) collective-permute-start(bf16[8,64,384]{2,1,0:T(8,128)(2,1)S(1)} %get-tuple-element.197), channel_id=1, source_target_pairs={{0,16},{8,24},{16,0},{24,8},{1,17},{9,25},{17,1},{25,9},{2,18},{10... | collective-permute-start | bytes 1179656 | tf_op jit(solution)/shard_map/ppermute | solution.py:205
  505.5 13.1 %collective-permute-start.40 = (bf16[4,64,1024]{2,1,0:T(8,128)(2,1)}, bf16[4,64,1024]{2,1,0:T(8,128)(2,1)}, u32[]{:S(2)}, u32[]{:S(2)}) collective-permute-start(bf16[4,64,1024]{2,1,0:T(8,128)(2,1)} %get-tuple-element.185), channel_id=1, source_target_pairs={{0,8},{8,0},{16,24},{24,16},{1,9},{9,1},{17,25},{25,17},{2,10},{10... | collective-permute-start | bytes 1572872 | tf_op jit(solution)/shard_map/ppermute | solution.py:205
  507.0 23.2 %collective-permute-start.41 = (bf16[4,64,1024]{2,1,0:T(8,128)(2,1)}, bf16[4,64,1024]{2,1,0:T(8,128)(2,1)}, u32[]{:S(2)}, u32[]{:S(2)}) collective-permute-start(bf16[4,64,1024]{2,1,0:T(8,128)(2,1)} %get-tuple-element.184), channel_id=1, source_target_pairs={{0,16},{8,24},{16,0},{24,8},{1,17},{9,25},{17,1},{25,9},{2,18},{10... | collective-permute-start | bytes 1572872 | tf_op jit(solution)/shard_map/ppermute | solution.py:205
  507.5 26.0 %all-to-all-start.3 = ((bf16[8,72,384]{2,1,0:T(8,128)(2,1)}), bf16[8,72,384]{2,1,0:T(8,128)(2,1)S(1)}, u32[]{:S(2)}, u32[]{:S(2)}) async-start(bf16[8,72,384]{2,1,0:T(8,128)(2,1)} %fusion.36), calls=%async_computation.7 | async-start | bytes 884736 | tf_op jit(solution)/shard_map/all_to_all | solution.py:343
  512.5 18.7 %collective-permute-start.42 = (bf16[4,64,1024]{2,1,0:T(8,128)(2,1)}, bf16[4,64,1024]{2,1,0:T(8,128)(2,1)S(1)}, u32[]{:S(2)}, u32[]{:S(2)}) collective-permute-start(bf16[4,64,1024]{2,1,0:T(8,128)(2,1)} %get-tuple-element.183), channel_id=1, source_target_pairs={{0,24},{8,16},{16,8},{24,0},{1,25},{9,17},{17,9},{25,1},{2,26},{10... | collective-permute-start | bytes 1572872 | tf_op jit(solution)/shard_map/ppermute | solution.py:205
  533.5 6.6 %collective-permute-start.46 = (f32[2,256]{1,0:T(2,128)S(1)}, f32[2,256]{1,0:T(2,128)}, u32[]{:S(2)}, u32[]{:S(2)}) collective-permute-start(f32[2,256]{1,0:T(2,128)S(1)} %convert_reduce_fusion), channel_id=1, source_target_pairs={{0,8},{8,0},{16,24},{24,16},{1,9},{9,1},{17,25},{25,17},{2,10},{10... | collective-permute-start | bytes 6152 | tf_op jit(solution)/shard_map/ppermute | solution.py:205
  536.1 15.3 %collective-permute-start.43 = (bf16[64,768]{1,0:T(8,128)(2,1)S(1)}, bf16[64,768]{1,0:T(8,128)(2,1)S(1)}, u32[]{:S(2)}, u32[]{:S(2)}) collective-permute-start(bf16[64,768]{1,0:T(8,128)(2,1)S(1)} %bitcast.233), channel_id=1, source_target_pairs={{0,8},{8,0},{16,24},{24,16},{1,9},{9,1},{17,25},{25,17},{2,10},{10... | collective-permute-start | bytes 294920 | tf_op jit(solution)/shard_map/ppermute | solution.py:205
  537.6 13.8 %collective-permute-start.44 = (bf16[64,768]{1,0:T(8,128)(2,1)S(1)}, bf16[64,768]{1,0:T(8,128)(2,1)S(1)}, u32[]{:S(2)}, u32[]{:S(2)}) collective-permute-start(bf16[64,768]{1,0:T(8,128)(2,1)S(1)} %bitcast.232), channel_id=1, source_target_pairs={{0,16},{8,24},{16,0},{24,8},{1,17},{9,25},{17,1},{25,9},{2,18},{10... | collective-permute-start | bytes 294920 | tf_op jit(solution)/shard_map/ppermute | solution.py:205
  539.0 12.4 %collective-permute-start.45 = (bf16[64,768]{1,0:T(8,128)(2,1)S(1)}, bf16[64,768]{1,0:T(8,128)(2,1)S(1)}, u32[]{:S(2)}, u32[]{:S(2)}) collective-permute-start(bf16[64,768]{1,0:T(8,128)(2,1)S(1)} %bitcast.231), channel_id=1, source_target_pairs={{0,24},{8,16},{16,8},{24,0},{1,25},{9,17},{17,9},{25,1},{2,26},{10... | collective-permute-start | bytes 294920 | tf_op jit(solution)/shard_map/ppermute | solution.py:205
  540.8 10.0 %collective-permute-start.47 = (f32[2,256]{1,0:T(2,128)S(1)}, f32[2,256]{1,0:T(2,128)S(1)}, u32[]{:S(2)}, u32[]{:S(2)}) collective-permute-start(f32[2,256]{1,0:T(2,128)S(1)} %add.254), channel_id=1, source_target_pairs={{0,16},{8,24},{16,0},{24,8},{1,17},{9,25},{17,1},{25,9},{2,18},{10... | collective-permute-start | bytes 6152 | tf_op jit(solution)/shard_map/ppermute | solution.py:205
  (25 other events, 179.1 us)
Sparse Core Ops, SparseCore 0:
  9.6 59.0 all-gather.11
  131.4 49.8 reduce-scatter.4
  184.9 45.6 all-gather.5
  232.7 45.6 all-gather.7
  280.5 48.7 reduce-scatter.6
  334.9 48.8 reduce-scatter.8
  394.0 45.5 all-gather.9
  502.4 57.1 reduce-scatter.10

commit v5 on v3

--- a/solution.py
+++ b/solution.py
@@ -517,12 +517,13 @@
         axis=1,
     )
     gu_summed, down_partial = tie((gu_summed, down_partial))
-    grad_down = scatter_end(down_partial, down_got, 1)
     branch_grad, gu_summed = tie((branch_grad, gu_summed))
     gu_blocks = exchange(gu_summed, "seq")
 
     attended_grad = dot_nt(branch_grad, my_out).astype(BF16)
     qkv_grad = attend_back(saved, attended_grad, cosine, sine, lengths)
+    qkv_grad, down_partial = tie((qkv_grad, down_partial))
+    grad_down = scatter_end(down_partial, down_got, 1)
     normed_partial = dot_nt(qkv_grad, my_qkv)
     qkv_partial = dot_tn(normed, qkv_grad).astype(BF16).reshape(seqs, ranks, sub, -1)
     qkv_summed = scatter_direct(qkv_partial, 1).astype(BF16)

time: 571 us -> 583 us (1.021)
  waiting for transfers between devices: 255 us -> 264 us
    ppermute x47, waiting for transfers between devices: 126 us -> 136 us  [send(): return lax.ppermute(value, 'dp', flip(mask, lax.axis_size('dp')))]
  transfers between devices with their start and end apart: 59 -> 59, of which waited for: 26 -> 28; matrix products, arithmetic and copies ran while one was open for 29% -> 29% of each run, Pallas kernels for 7% -> 7%
where the time goes in v5:
time: 583 us; the launch traced here: 577 us
  waiting for transfers between devices  264 us (45%)
  matrix products  73 us (13%)
  starting transfers between devices  72.2 us (12%)
  local copies, waits for them, and re-layouts  56.8 us (10%)
  other arithmetic  54 us (9%)
  Pallas kernels  40.8 us (7%)
  between operations  16 us (3%)
    ppermute x47, waiting for transfers between devices, send(): return lax.ppermute(value, 'dp', flip(mask, lax.axis_size('dp')))  136 us
    reduce_scatter x4, waiting for transfers between devices, scatter_seq(): lax.psum_scatter(partial.astype(BF16), 'seq', scatter_dimension=0, tiled=...  89.3 us
    ppermute x47, starting transfers between devices, send(): return lax.ppermute(value, 'dp', flip(mask, lax.axis_size('dp')))  52.8 us
    dot_general x5, matrix products, dot_nt(): lax.dot_general(left, right, (((1,), (1,)), ((), ())), preferred_element_...  30.7 us
    all_gather x4, waiting for transfers between devices, gather_seq(): return lax.all_gather(shard, 'seq', axis=0, tiled=True)  29.9 us
    dot_general x5, matrix products, dot_tn(): lax.dot_general(left, right, (((0,), (0,)), ((), ())), preferred_element_...  27.7 us
    pallas_call x1, Pallas kernels, gate_up_of(): pl.pallas_call(gate_up_kernel, out_shape=(shape((slots, ff), F32),) * 2 +...  20 us
    all_to_all x4, starting transfers between devices, exchange(): lax.all_to_all(blocks, axis_name, split_axis=0, concat_axis=0, tiled=True)  18.7 us
  transfers between devices with their start and end apart: 59, of which 28 were waited for; matrix products, arithmetic and copies ran while one was open for 29% of the time, Pallas kernels for 7%

profile of v5, /device:TPU:0, one launch (start us, length us, event | category | flops | bytes accessed | tf_op | source)
XLA Modules:
  0.0 577.0 jit_solution(10064612265511709092)
XLA Ops:
  9.0 4.0 collective-permute-start.2
  15.0 3.2 collective-permute-done
  18.4 3.5 reshape.149
  26.9 5.0 all-to-all-start
  33.8 4.1 collective-permute-done.3
  39.2 11.0 %collective-permute-done.4 = bf16[4,64,1024]{2,0,1:T(4,128)(2,1)} collective-permute-done((bf16[4,64,1024]{2,0,1:T(4,128)(2,1)}, bf16[4,64,1024]{2,0,1:T(4,128)(2,1)}, u32[]{:S(2)}, u32[]{:S(2)}) %collective-permute-start.4) | collective-permute-done | bytes 524320 | tf_op jit(solution)/shard_map/ppermute | solution.py:205
  51.7 6.7 %all-to-all-done = bf16[8,72,384]{2,1,0:T(8,128)(2,1)S(1)} async-done(((bf16[8,72,384]{2,1,0:T(8,128)(2,1)}), bf16[8,72,384]{2,1,0:T(8,128)(2,1)S(1)}, u32[]{:S(2)}, u32[]{:S(2)}) %all-to-all-start) | async-done | bytes 442400 | tf_op jit(solution)/shard_map/all_to_all | solution.py:309
  60.0 4.4 all-to-all-start.1
  64.6 2.5 fusion.33
  68.7 2.0 collective-permute-start.8
  73.0 7.7 %collective-permute-done.6 = bf16[8,1,64,384]{3,2,1,0:T(8,128)(2,1)S(1)} collective-permute-done((bf16[8,1,64,384]{3,2,1,0:T(8,128)(2,1)S(1)}, bf16[8,1,64,384]{3,2,1,0:T(8,128)(2,1)S(1)}, u32[]{:S(2)}, u32[]{:S(2)}) %collective-permute-start.6) | collective-permute-done | bytes 393248 | tf_op jit(solution)/shard_map/ppermute | solution.py:205
  82.2 6.0 %collective-permute-done.8 = bf16[8,1,64,384]{3,2,1,0:T(8,128)(2,1)S(1)} collective-permute-done((bf16[8,1,64,384]{3,2,1,0:T(8,128)(2,1)S(1)}, bf16[8,1,64,384]{3,2,1,0:T(8,128)(2,1)S(1)}, u32[]{:S(2)}, u32[]{:S(2)}) %collective-permute-start.8) | collective-permute-done | bytes 393248 | tf_op jit(solution)/shard_map/ppermute | solution.py:205
  95.5 3.1 fusion.4
  98.6 3.8 fusion.14.qkv_ref
  106.4 10.0 %shard_map.135 = (bf16[1024,256]{1,0:T(8,128)(2,1)S(1)}, bf16[1024,256]{1,0:T(8,128)(2,1)S(1)}, bf16[1024,128]{1,0:T(8,128)(2,1)S(1)}, bf16[1024,128]{1,0:T(8,128)(2,1)S(1)}, f32[8,1024]{1,0:T(8,128)S(1)}) custom-call(s32[1]{0:T(128)} %copy.230.length_ref, f32[1024,384]{1,0:T(8,128)S(1)} %fusion.14.qkv_ref, f32[1024,128]{1,0:T(8,128)S(1)} %get-tuple-element.191.cos_ref, ...), custom_call_target="tpu_custom_call" | custom-call | flops 1073741824 | bytes 3145728 | tf_op jit(solution)/shard_map/pallas_call | solution.py:117
  117.8 8.0 %collective-permute-done.11 = bf16[256,512]{1,0:T(8,128)(2,1)S(1)} collective-permute-done((bf16[256,512]{1,0:T(8,128)(2,1)S(1)}, bf16[256,512]{1,0:T(8,128)(2,1)S(1)}, u32[]{:S(2)}, u32[]{:S(2)}) %collective-permute-start.11) | collective-permute-done | bytes 262176 | tf_op jit(solution)/shard_map/ppermute | solution.py:205
  126.6 4.7 convolution_convert_fusion
  131.3 3.3 slice_bitcast_fusion
  138.6 42.7 %reduce-scatter.5.cloned.1.call-done = bf16[128,2048]{1,0:T(8,128)(2,1)} async-done(((bf16[1024,2048]{1,0:T(8,128)(2,1)}), bf16[128,2048]{1,0:T(8,128)(2,1)}) %reduce-scatter.5.cloned.1.call-update) | async-done | bytes 524304 | tf_op jit(solution)/shard_map/reduce_scatter | solution.py:317
  189.5 2.0 fusion.26
  191.5 28.5 %collective-permute-done.22 = bf16[512,512]{1,0:T(8,128)(2,1)} collective-permute-done((bf16[512,512]{1,0:T(8,128)(2,1)}, bf16[512,512]{1,0:T(8,128)(2,1)}, u32[]{:S(2)}, u32[]{:S(2)}) %collective-permute-start.22) | collective-permute-done | bytes 524320 | tf_op jit(solution)/shard_map/ppermute | solution.py:205
  221.2 10.1 %all-gather.6.cloned.1.call-done.x_ref = bf16[1024,2048]{1,0:T(8,128)(2,1)} async-done(((bf16[128,2048]{1,0:T(8,128)(2,1)}), bf16[1024,2048]{1,0:T(8,128)(2,1)}) %all-gather.6.cloned.1.call-update) | async-done | bytes 4194320 | tf_op jit(solution)/shard_map/all_gather | solution.py:313
  236.7 20.0 %shard_map.136 = (f32[1024,1024]{1,0:T(8,128)}, f32[1024,1024]{1,0:T(8,128)}, bf16[8,4,64,1024]{3,2,1,0:T(8,128)(2,1)}, bf16[8,4,64,1024]{3,2,1,0:T(8,128)(2,1)}) custom-call(s32[1]{0:T(128)} %bitcast.33.me_ref, bf16[1024,2048]{1,0:T(8,128)(2,1)} %all-gather.6.cloned.1.call-done.x_ref, bf16[8,64,1024]{2,1,0:T(8,128)(2,1)} %get-tuple-element.175.refs_0_, ...), custom_call_target="tpu_custom_call" | custom-call | flops 8589934592 | bytes 25165824 | tf_op jit(solution)/shard_map/pallas_call | solution.py:367
  256.7 4.9 multiply_convert_fusion.2
  263.0 6.1 %convolution_convert_fusion.4 = bf16[1024,2048]{1,0:T(8,128)(2,1)} fusion(bf16[1024,1024]{1,0:T(8,128)(2,1)S(1)} %multiply_convert_fusion.2, bf16[1024,2048]{1,0:T(8,128)(2,1)S(1)} %maximum_dynamic-update-slice_fusion.2), kind=kOutput, calls=%fused_computation.17 | convolution fusion | flops 4297064448 | bytes 10485760 | tf_op jit(solution)/shard_map/dot_general | solution.py:29
  269.0 9.9 %all-gather.8.cloned.1.call-done = bf16[1024,2048]{1,0:T(8,128)(2,1)} async-done(((bf16[128,2048]{1,0:T(8,128)(2,1)}), bf16[1024,2048]{1,0:T(8,128)(2,1)}) %all-gather.8.cloned.1.call-update) | async-done | bytes 4194320 | tf_op jit(solution)/shard_map/all_gather | solution.py:313
  279.1 7.5 %convolution_convert_fusion.3 = bf16[1024,2048]{1,0:T(8,128)(2,1)S(1)} fusion(bf16[1024,1024]{1,0:T(8,128)(2,1)} %copy-done.15, bf16[1024,2048]{1,0:T(8,128)(2,1)} %all-gather.8.cloned.1.call-done), kind=kOutput, calls=%fused_computation.16 | convolution fusion | flops 4297064448 | bytes 10485760 | tf_op jit(solution)/shard_map/dot_general | solution.py:37
  286.6 2.0 copy-done.9
  288.7 1.9 constant_dynamic-slice_fusion.6
  290.5 2.4 collective-permute-start.26
  294.0 7.2 %multiply_convert_fusion = (bf16[1024,1024]{1,0:T(8,128)(2,1)}, bf16[1024,1024]{1,0:T(8,128)(2,1)S(1)}) fusion(f32[1024,1024]{1,0:T(8,128)S(1)} %copy-done.10, f32[1024,1024]{1,0:T(8,128)S(1)} %copy-done.11, bf16[1024,2048]{1,0:T(8,128)(2,1)S(1)} %copy-done.22, bf16[1024,2048]{1,0:T(8,128)(2,1)S(1)} %copy-done.13), kind=kOutput, calls=%fused_computation.9 | convolution fusion | flops 4308598784 | bytes 20971520 | tf_op jit(solution)/shard_map/dot_general | solution.py:33
  301.2 7.2 %fusion.40 = f32[1024,2048]{1,0:T(8,128)S(1)} fusion(bf16[1024,1024]{1,0:T(8,128)(2,1)S(1)} %get-tuple-element.162, bf16[2048,1024]{1,0:T(8,128)(2,1)} %bitcast.222), kind=kOutput, calls=%fused_computation.153 | convolution fusion | flops 4294967296 | bytes 14680064 | tf_op jit(solution)/shard_map/dot_general | solution.py:33
  308.4 6.1 %add_convert_fusion = bf16[1024,2048]{1,0:T(8,128)(2,1)} fusion(f32[1024,2048]{1,0:T(8,128)S(1)} %fusion.40, bf16[1024,1024]{1,0:T(8,128)(2,1)S(1)} %copy-done.27, bf16[2048,1024]{1,0:T(8,128)(2,1)S(1)} %bitcast.221), kind=kOutput, calls=%fused_computation.7 | convolution fusion | flops 4299161600 | bytes 18874368 | tf_op jit(solution)/shard_map/dot_general | solution.py:33
  314.6 9.6 %convolution_convert_fusion.1 = bf16[2048,1024]{1,0:T(8,128)(2,1)} fusion(bf16[1024,2048]{1,0:T(8,128)(2,1)} %all-gather.6.cloned.1.call-done.x_ref, bf16[1024,1024]{1,0:T(8,128)(2,1)} %get-tuple-element.161), kind=kOutput, calls=%fused_computation.14 | convolution fusion | flops 4297064448 | bytes 10485760 | tf_op jit(solution)/shard_map/dot_general | solution.py:37
  324.2 6.5 %convolution_convert_fusion.2 = bf16[2048,1024]{1,0:T(8,128)(2,1)} fusion(bf16[1024,2048]{1,0:T(8,128)(2,1)S(1)} %copy-done.21, bf16[1024,1024]{1,0:T(8,128)(2,1)S(1)} %copy-done.26), kind=kOutput, calls=%fused_computation.15 | convolution fusion | flops 4297064448 | bytes 10485760 | tf_op jit(solution)/shard_map/dot_general | solution.py:37
  330.7 2.1 convert_element_type.243
  332.8 6.7 %collective-permute-done.25 = bf16[1024,512]{1,0:T(8,128)(2,1)} collective-permute-done((bf16[1024,512]{1,0:T(8,128)(2,1)}, bf16[1024,512]{1,0:T(8,128)(2,1)}, u32[]{:S(2)}, u32[]{:S(2)}) %collective-permute-start.25) | collective-permute-done | bytes 1048608 | tf_op jit(solution)/shard_map/ppermute | solution.py:205
  339.6 3.2 dynamic-slice_bitcast_fusion.2
  348.5 39.4 %reduce-scatter.9.cloned.1.call-done = bf16[128,2048]{1,0:T(8,128)(2,1)} async-done(((bf16[1024,2048]{1,0:T(8,128)(2,1)}), bf16[128,2048]{1,0:T(8,128)(2,1)}) %reduce-scatter.9.cloned.1.call-update) | async-done | bytes 524304 | tf_op jit(solution)/shard_map/reduce_scatter | solution.py:317
  390.7 3.0 collective-permute-done.29
  395.3 2.9 multiply_convert_fusion.3
  398.2 3.0 fusion.5
  402.7 3.1 fusion.8
  405.9 19.2 %collective-permute-done.32 = bf16[8,64,1024]{2,1,0:T(8,128)(2,1)} collective-permute-done((bf16[8,64,1024]{2,1,0:T(8,128)(2,1)}, bf16[8,64,1024]{2,1,0:T(8,128)(2,1)}, u32[]{:S(2)}, u32[]{:S(2)}) %collective-permute-start.32) | collective-permute-done | bytes 1048608 | tf_op jit(solution)/shard_map/ppermute | solution.py:205
  425.1 2.5 fusion.23
  429.3 2.5 fusion.22
  433.3 9.9 %all-gather.10.cloned.1.call-done = bf16[1024,2048]{1,0:T(8,128)(2,1)} async-done(((bf16[128,2048]{1,0:T(8,128)(2,1)}), bf16[1024,2048]{1,0:T(8,128)(2,1)}) %all-gather.10.cloned.1.call-update) | async-done | bytes 4194320 | tf_op jit(solution)/shard_map/all_gather | solution.py:313
  443.2 4.3 all-to-all-start.2
  448.0 3.8 convolution_convert_fusion.7.grad_ref
  451.8 10.8 %shard_map.137 = bf16[1024,384]{1,0:T(8,128)(2,1)S(1)} custom-call(s32[1]{0:T(128)} %copy.230.length_ref, bf16[1024,256]{1,0:T(8,128)(2,1)S(1)} %get-tuple-element.124.q_ref, bf16[1024,128]{1,0:T(8,128)(2,1)S(1)} %get-tuple-element.125.k_ref, bf16[1024,128]{1,0:T(8,128)(2,1)S(1)} %get-tuple-element.126.v_ref, f32[8,1024]{1,0:T(8,128)S(1)} %get-tuple-element.127.lse_ref, ...), custom_call_target="tpu_custom_call" | custom-call | flops 2684354560 | bytes 3145728 | tf_op jit(solution)/shard_map/pallas_call | solution.py:186
  466.4 6.4 %fusion.3 = (bf16[2048]{0:T(1024)(128)(2,1)}, bf16[1024,2048]{1,0:T(8,128)(2,1)}) fusion(bf16[1024,2048]{1,0:T(8,128)(2,1)S(1)} %bitcast.197, f32[1024]{0:T(1024)S(1)} %add_rsqrt_fusion, bf16[1024,384]{1,0:T(8,128)(2,1)S(1)} %shard_map.137, bf16[2048,384]{1,0:T(8,128)(2,1)} %bitcast.25), kind=kOutput, calls=%fused_computation.5 | convolution fusion | flops 1621096448 | bytes 10756096 | tf_op jit(solution)/shard_map/dot_general | solution.py:33
  472.8 2.6 convolution_convert_fusion.5
  482.2 4.0 convert_add_fusion.4
  487.0 3.7 collective-permute-done.37
  490.7 2.0 convert_add_fusion.7
  494.4 7.6 %collective-permute-done.35 = bf16[8,64,384]{2,1,0:T(8,128)(2,1)} collective-permute-done((bf16[8,64,384]{2,1,0:T(8,128)(2,1)}, bf16[8,64,384]{2,1,0:T(8,128)(2,1)}, u32[]{:S(2)}, u32[]{:S(2)}) %collective-permute-start.35) | collective-permute-done | bytes 393248 | tf_op jit(solution)/shard_map/ppermute | solution.py:205
  502.0 5.5 collective-permute-done.34
  509.7 1.8 copy.165
  515.0 5.0 all-to-all-start.3
  521.5 6.6 %collective-permute-done.39 = bf16[4,64,1024]{2,1,0:T(8,128)(2,1)} collective-permute-done((bf16[4,64,1024]{2,1,0:T(8,128)(2,1)}, bf16[4,64,1024]{2,1,0:T(8,128)(2,1)}, u32[]{:S(2)}, u32[]{:S(2)}) %collective-permute-start.39) | collective-permute-done | bytes 524320 | tf_op jit(solution)/shard_map/ppermute | solution.py:205
  529.2 9.5 %collective-permute-done.40 = bf16[4,64,1024]{2,1,0:T(8,128)(2,1)} collective-permute-done((bf16[4,64,1024]{2,1,0:T(8,128)(2,1)}, bf16[4,64,1024]{2,1,0:T(8,128)(2,1)}, u32[]{:S(2)}, u32[]{:S(2)}) %collective-permute-start.40) | collective-permute-done | bytes 524320 | tf_op jit(solution)/shard_map/ppermute | solution.py:205
  549.8 2.7 copy.169
  552.5 5.8 %copy.179 = f32[32,8,4,1024]{3,1,2,0:T(8,128)} copy(f32[32,8,4,1024]{3,2,1,0:T(4,128)S(1)} %bitcast.186) | data formatting | bytes 8388608
  559.9 7.1 %reduce-scatter.11.cloned.1.call-done = bf16[128,2048]{1,0:T(8,128)(2,1)} async-done(((bf16[1024,2048]{1,0:T(8,128)(2,1)}), bf16[128,2048]{1,0:T(8,128)(2,1)}) %reduce-scatter.11.cloned.1.call-update) | async-done | bytes 524304 | tf_op jit(solution)/shard_map/reduce_scatter | solution.py:317
  (251 shorter events, 106.7 us)
Async XLA Ops:
  7.2 81.8 %all-gather.12.cloned.1.call-start = ((), (), s32[]{:S(2)}) async-start(), calls=%async_computation.15 | async-start | bytes 4718592 | tf_op jit(solution)/shard_map/all_gather | solution.py:313
  9.0 9.3 %collective-permute-start.2 = (bf16[64,768]{1,0:T(8,128)(2,1)S(1)}, bf16[64,768]{1,0:T(8,128)(2,1)S(1)}, u32[]{:S(2)}, u32[]{:S(2)}) collective-permute-start(bf16[64,768]{1,0:T(8,128)(2,1)S(1)} %get-tuple-element.200), channel_id=1, source_target_pairs={{0,24},{8,16},{16,8},{24,0},{1,25},{9,17},{17,9},{25,1},{2,26},{10... | collective-permute-start | bytes 294920 | tf_op jit(solution)/shard_map/ppermute | solution.py:205
  13.0 5.2 collective-permute-start.1
  13.5 4.7 collective-permute-start
  23.6 14.4 %collective-permute-start.3 = (bf16[4,64,1024]{2,0,1:T(4,128)(2,1)}, bf16[4,64,1024]{2,0,1:T(4,128)(2,1)}, u32[]{:S(2)}, u32[]{:S(2)}) collective-permute-start(bf16[4,64,1024]{2,0,1:T(4,128)(2,1)} %get-tuple-element.178), channel_id=1, source_target_pairs={{0,8},{8,0},{16,24},{24,16},{1,9},{9,1},{17,25},{25,17},{2,10},{10... | collective-permute-start | bytes 1572872 | tf_op jit(solution)/shard_map/ppermute | solution.py:205
  25.3 24.9 %collective-permute-start.4 = (bf16[4,64,1024]{2,0,1:T(4,128)(2,1)}, bf16[4,64,1024]{2,0,1:T(4,128)(2,1)}, u32[]{:S(2)}, u32[]{:S(2)}) collective-permute-start(bf16[4,64,1024]{2,0,1:T(4,128)(2,1)} %get-tuple-element.177), channel_id=1, source_target_pairs={{0,16},{8,24},{16,0},{24,8},{1,17},{9,25},{17,1},{25,9},{2,18},{10... | collective-permute-start | bytes 1572872 | tf_op jit(solution)/shard_map/ppermute | solution.py:205
  26.9 31.5 %all-to-all-start = ((bf16[8,72,384]{2,1,0:T(8,128)(2,1)}), bf16[8,72,384]{2,1,0:T(8,128)(2,1)S(1)}, u32[]{:S(2)}, u32[]{:S(2)}) async-start(bf16[8,72,384]{2,1,0:T(8,128)(2,1)} %copy.151), calls=%async_computation | async-start | bytes 884736 | tf_op jit(solution)/shard_map/all_to_all | solution.py:309
  31.9 19.5 %collective-permute-start.5 = (bf16[4,64,1024]{2,0,1:T(4,128)(2,1)}, bf16[4,64,1024]{2,0,1:T(4,128)(2,1)S(1)}, u32[]{:S(2)}, u32[]{:S(2)}) collective-permute-start(bf16[4,64,1024]{2,0,1:T(4,128)(2,1)} %get-tuple-element.176), channel_id=1, source_target_pairs={{0,24},{8,16},{16,8},{24,0},{1,25},{9,17},{17,9},{25,1},{2,26},{10... | collective-permute-start | bytes 1572872 | tf_op jit(solution)/shard_map/ppermute | solution.py:205
  60.0 66.6 %all-to-all-start.1 = ((bf16[8,2,64,1024]{3,2,1,0:T(8,128)(2,1)}), bf16[8,2,64,1024]{3,2,1,0:T(8,128)(2,1)}, u32[]{:S(2)}, u32[]{:S(2)}) async-start(bf16[8,2,64,1024]{3,2,1,0:T(8,128)(2,1)} %copy.156), calls=%async_computation.1 | async-start | bytes 4194304 | tf_op jit(solution)/shard_map/all_to_all | solution.py:309
  64.3 24.7 %copy-start.18 = (bf16[256,512]{1,0:T(8,128)(2,1)S(1)}, bf16[256,512]{1,0:T(8,128)(2,1)}, u32[]{:S(2)}) copy-start(bf16[256,512]{1,0:T(8,128)(2,1)} %param.11) | copy-start | bytes 786436
  64.4 26.5 %copy-start.7 = (bf16[1024,512]{1,0:T(8,128)(2,1)S(1)}, bf16[1024,512]{1,0:T(8,128)(2,1)}, u32[]{:S(2)}) copy-start(bf16[1024,512]{1,0:T(8,128)(2,1)} %param.13) | copy-start | bytes 3145732
  64.4 116.9 %reduce-scatter.5.cloned.1.call-start = ((), (), s32[]{:S(2)}) async-start(), calls=%async_computation.8 | async-start | bytes 4718592 | tf_op jit(solution)/shard_map/reduce_scatter | solution.py:317
  67.1 14.3 %collective-permute-start.7 = (bf16[8,1,64,384]{3,2,1,0:T(8,128)(2,1)S(1)}, bf16[8,1,64,384]{3,2,1,0:T(8,128)(2,1)S(1)}, u32[]{:S(2)}, u32[]{:S(2)}) collective-permute-start(bf16[8,1,64,384]{3,2,1,0:T(8,128)(2,1)S(1)} %slice_bitcast_fusion.3), channel_id=1, source_target_pairs={{0,16},{8,24},{16,0},{24,8},{1,17},{9,25},{17,1},{25,9},{2,18},{10... | collective-permute-start | bytes 1179656 | tf_op jit(solution)/shard_map/ppermute | solution.py:205
  68.6 12.0 %collective-permute-start.6 = (bf16[8,1,64,384]{3,2,1,0:T(8,128)(2,1)S(1)}, bf16[8,1,64,384]{3,2,1,0:T(8,128)(2,1)S(1)}, u32[]{:S(2)}, u32[]{:S(2)}) collective-permute-start(bf16[8,1,64,384]{3,2,1,0:T(8,128)(2,1)S(1)} %slice_bitcast_fusion.3), channel_id=1, source_target_pairs={{0,8},{8,0},{16,24},{24,16},{1,9},{9,1},{17,25},{25,17},{2,10},{10... | collective-permute-start | bytes 1179656 | tf_op jit(solution)/shard_map/ppermute | solution.py:205
  68.7 19.5 %collective-permute-start.8 = (bf16[8,1,64,384]{3,2,1,0:T(8,128)(2,1)S(1)}, bf16[8,1,64,384]{3,2,1,0:T(8,128)(2,1)S(1)}, u32[]{:S(2)}, u32[]{:S(2)}) collective-permute-start(bf16[8,1,64,384]{3,2,1,0:T(8,128)(2,1)S(1)} %slice_bitcast_fusion.3), channel_id=1, source_target_pairs={{0,24},{8,16},{16,8},{24,0},{1,25},{9,17},{17,9},{25,1},{2,26},{10... | collective-permute-start | bytes 1179656 | tf_op jit(solution)/shard_map/ppermute | solution.py:205
  89.0 13.4 %collective-permute-start.10 = (bf16[256,512]{1,0:T(8,128)(2,1)S(1)}, bf16[256,512]{1,0:T(8,128)(2,1)S(1)}, u32[]{:S(2)}, u32[]{:S(2)}) collective-permute-start(bf16[256,512]{1,0:T(8,128)(2,1)S(1)} %copy-done.18), channel_id=1, source_target_pairs={{0,16},{8,24},{16,0},{24,8},{1,17},{9,25},{17,1},{25,9},{2,18},{10... | collective-permute-start | bytes 786440 | tf_op jit(solution)/shard_map/ppermute | solution.py:205
  90.4 14.3 %collective-permute-start.9 = (bf16[256,512]{1,0:T(8,128)(2,1)S(1)}, bf16[256,512]{1,0:T(8,128)(2,1)S(1)}, u32[]{:S(2)}, u32[]{:S(2)}) collective-permute-start(bf16[256,512]{1,0:T(8,128)(2,1)S(1)} %copy-done.18), channel_id=1, source_target_pairs={{0,8},{8,0},{16,24},{24,16},{1,9},{9,1},{17,25},{25,17},{2,10},{10... | collective-permute-start | bytes 786440 | tf_op jit(solution)/shard_map/ppermute | solution.py:205
  91.9 34.7 %collective-permute-start.15 = (bf16[512,512]{1,0:T(8,128)(2,1)}, bf16[512,512]{1,0:T(8,128)(2,1)S(1)}, u32[]{:S(2)}, u32[]{:S(2)}) collective-permute-start(bf16[512,512]{1,0:T(8,128)(2,1)} %get-tuple-element.187), channel_id=1, source_target_pairs={{0,16},{8,24},{16,0},{24,8},{1,17},{9,25},{17,1},{25,9},{2,18},{10... | collective-permute-start | bytes 1572872 | tf_op jit(solution)/shard_map/ppermute | solution.py:205
  93.5 33.0 %collective-permute-start.13 = (bf16[512,512]{1,0:T(8,128)(2,1)}, bf16[512,512]{1,0:T(8,128)(2,1)}, u32[]{:S(2)}, u32[]{:S(2)}) collective-permute-start(bf16[512,512]{1,0:T(8,128)(2,1)} %get-tuple-element.187), channel_id=1, source_target_pairs={{0,8},{8,0},{16,24},{24,16},{1,9},{9,1},{17,25},{25,17},{2,10},{10... | collective-permute-start | bytes 1572872 | tf_op jit(solution)/shard_map/ppermute | solution.py:205
  94.1 32.5 %collective-permute-start.14 = (bf16[512,512]{1,0:T(8,128)(2,1)}, bf16[512,512]{1,0:T(8,128)(2,1)}, u32[]{:S(2)}, u32[]{:S(2)}) collective-permute-start(bf16[512,512]{1,0:T(8,128)(2,1)} %get-tuple-element.188), channel_id=1, source_target_pairs={{0,16},{8,24},{16,0},{24,8},{1,17},{9,25},{17,1},{25,9},{2,18},{10... | collective-permute-start | bytes 1572872 | tf_op jit(solution)/shard_map/ppermute | solution.py:205
  102.4 24.2 %collective-permute-start.12 = (bf16[512,512]{1,0:T(8,128)(2,1)}, bf16[512,512]{1,0:T(8,128)(2,1)}, u32[]{:S(2)}, u32[]{:S(2)}) collective-permute-start(bf16[512,512]{1,0:T(8,128)(2,1)} %get-tuple-element.188), channel_id=1, source_target_pairs={{0,8},{8,0},{16,24},{24,16},{1,9},{9,1},{17,25},{25,17},{2,10},{10... | collective-permute-start | bytes 1572872 | tf_op jit(solution)/shard_map/ppermute | solution.py:205
  104.7 21.1 %collective-permute-start.11 = (bf16[256,512]{1,0:T(8,128)(2,1)S(1)}, bf16[256,512]{1,0:T(8,128)(2,1)S(1)}, u32[]{:S(2)}, u32[]{:S(2)}) collective-permute-start(bf16[256,512]{1,0:T(8,128)(2,1)S(1)} %copy-done.18), channel_id=1, source_target_pairs={{0,24},{8,16},{16,8},{24,0},{1,25},{9,17},{17,9},{25,1},{2,26},{10... | collective-permute-start | bytes 786440 | tf_op jit(solution)/shard_map/ppermute | solution.py:205
  131.2 51.2 %copy-start.2 = (bf16[1,128,2048]{2,1,0:T(8,128)(2,1)S(1)}, bf16[1,128,2048]{2,1,0:T(8,128)(2,1)}, u32[]{:S(2)}) copy-start(bf16[1,128,2048]{2,1,0:T(8,128)(2,1)} %param.8) | copy-start | bytes 1572868
  131.3 100.0 %all-gather.6.cloned.1.call-start = ((), (), s32[]{:S(2)}) async-start(), calls=%async_computation.9 | async-start | bytes 4718592 | tf_op jit(solution)/shard_map/all_gather | solution.py:313
  134.6 47.9 %collective-permute-start.19 = (bf16[8,64,1024]{2,1,0:T(8,128)(2,1)}, bf16[8,64,1024]{2,1,0:T(8,128)(2,1)}, u32[]{:S(2)}, u32[]{:S(2)}) collective-permute-start(bf16[8,64,1024]{2,1,0:T(8,128)(2,1)} %get-tuple-element.174.refs_4_), channel_id=1, source_target_pairs={{0,8},{8,0},{16,24},{24,16},{1,9},{9,1},{17,25},{25,17},{2,10},{10... | collective-permute-start | bytes 3145736 | tf_op jit(solution)/shard_map/ppermute | solution.py:205
  136.0 46.5 %collective-permute-start.18 = (bf16[8,64,1024]{2,1,0:T(8,128)(2,1)}, bf16[8,64,1024]{2,1,0:T(8,128)(2,1)}, u32[]{:S(2)}, u32[]{:S(2)}) collective-permute-start(bf16[8,64,1024]{2,1,0:T(8,128)(2,1)} %get-tuple-element.174.refs_4_), channel_id=1, source_target_pairs={{0,16},{8,24},{16,0},{24,8},{1,17},{9,25},{17,1},{25,9},{2,18},{10... | collective-permute-start | bytes 3145736 | tf_op jit(solution)/shard_map/ppermute | solution.py:205
  136.7 45.8 %collective-permute-start.17 = (bf16[8,64,1024]{2,1,0:T(8,128)(2,1)}, bf16[8,64,1024]{2,1,0:T(8,128)(2,1)}, u32[]{:S(2)}, u32[]{:S(2)}) collective-permute-start(bf16[8,64,1024]{2,1,0:T(8,128)(2,1)} %get-tuple-element.175.refs_0_), channel_id=1, source_target_pairs={{0,16},{8,24},{16,0},{24,8},{1,17},{9,25},{17,1},{25,9},{2,18},{10... | collective-permute-start | bytes 3145736 | tf_op jit(solution)/shard_map/ppermute | solution.py:205
  138.0 44.5 %collective-permute-start.16 = (bf16[8,64,1024]{2,1,0:T(8,128)(2,1)}, bf16[8,64,1024]{2,1,0:T(8,128)(2,1)}, u32[]{:S(2)}, u32[]{:S(2)}) collective-permute-start(bf16[8,64,1024]{2,1,0:T(8,128)(2,1)} %get-tuple-element.175.refs_0_), channel_id=1, source_target_pairs={{0,8},{8,0},{16,24},{24,16},{1,9},{9,1},{17,25},{25,17},{2,10},{10... | collective-permute-start | bytes 3145736 | tf_op jit(solution)/shard_map/ppermute | solution.py:205
  185.3 93.7 %all-gather.8.cloned.1.call-start = ((), (), s32[]{:S(2)}) async-start(), calls=%async_computation.10 | async-start | bytes 4718592 | tf_op jit(solution)/shard_map/all_gather | solution.py:313
  185.3 35.8 %collective-permute-start.20 = (bf16[8,64,1024]{2,1,0:T(8,128)(2,1)}, bf16[8,64,1024]{2,1,0:T(8,128)(2,1)}, u32[]{:S(2)}, u32[]{:S(2)}) collective-permute-start(bf16[8,64,1024]{2,1,0:T(8,128)(2,1)} %collective-permute-done.16.refs_1_), channel_id=1, source_target_pairs={{0,16},{8,24},{16,0},{24,8},{1,17},{9,25},{17,1},{25,9},{2,18},{10... | collective-permute-start | bytes 3145736 | tf_op jit(solution)/shard_map/ppermute | solution.py:205
  186.9 34.3 %collective-permute-start.21 = (bf16[8,64,1024]{2,1,0:T(8,128)(2,1)}, bf16[8,64,1024]{2,1,0:T(8,128)(2,1)}, u32[]{:S(2)}, u32[]{:S(2)}) collective-permute-start(bf16[8,64,1024]{2,1,0:T(8,128)(2,1)} %collective-permute-done.18.refs_6_), channel_id=1, source_target_pairs={{0,8},{8,0},{16,24},{24,16},{1,9},{9,1},{17,25},{25,17},{2,10},{10... | collective-permute-start | bytes 3145736 | tf_op jit(solution)/shard_map/ppermute | solution.py:205
  188.4 31.6 %collective-permute-start.22 = (bf16[512,512]{1,0:T(8,128)(2,1)}, bf16[512,512]{1,0:T(8,128)(2,1)}, u32[]{:S(2)}, u32[]{:S(2)}) collective-permute-start(bf16[512,512]{1,0:T(8,128)(2,1)} %collective-permute-done.12), channel_id=1, source_target_pairs={{0,16},{8,24},{16,0},{24,8},{1,17},{9,25},{17,1},{25,9},{2,18},{10... | collective-permute-start | bytes 1572872 | tf_op jit(solution)/shard_map/ppermute | solution.py:205
  188.9 32.3 %collective-permute-start.23 = (bf16[512,512]{1,0:T(8,128)(2,1)}, bf16[512,512]{1,0:T(8,128)(2,1)}, u32[]{:S(2)}, u32[]{:S(2)}) collective-permute-start(bf16[512,512]{1,0:T(8,128)(2,1)} %copy-done.16), channel_id=1, source_target_pairs={{0,8},{8,0},{16,24},{24,16},{1,9},{9,1},{17,25},{25,17},{2,10},{10... | collective-permute-start | bytes 1572872 | tf_op jit(solution)/shard_map/ppermute | solution.py:205
  231.3 99.4 %reduce-scatter.7.cloned.1.call-start = ((), (), s32[]{:S(2)}) async-start(), calls=%async_computation.11 | async-start | bytes 4718592 | tf_op jit(solution)/shard_map/reduce_scatter | solution.py:317
  236.7 25.0 %copy-start.12 = (bf16[1024,2048]{1,0:T(8,128)(2,1)}, bf16[1024,2048]{1,0:T(8,128)(2,1)S(1)}, u32[]{:S(2)}) copy-start(bf16[1024,2048]{1,0:T(8,128)(2,1)S(1)} %maximum_dynamic-update-slice_fusion.2) | copy-start | bytes 12582916
  279.0 108.9 %reduce-scatter.9.cloned.1.call-start = ((), (), s32[]{:S(2)}) async-start(), calls=%async_computation.12 | async-start | bytes 4718592 | tf_op jit(solution)/shard_map/reduce_scatter | solution.py:317
  279.0 15.0 %copy-start.11 = (f32[1024,1024]{1,0:T(8,128)S(1)}, f32[1024,1024]{1,0:T(8,128)}, u32[]{:S(2)}) copy-start(f32[1024,1024]{1,0:T(8,128)} %get-tuple-element.108) | copy-start | bytes 12582916
  290.5 42.3 %collective-permute-start.26 = (bf16[1024,512]{1,0:T(8,128)(2,1)}, bf16[1024,512]{1,0:T(8,128)(2,1)}, u32[]{:S(2)}, u32[]{:S(2)}) collective-permute-start(bf16[1024,512]{1,0:T(8,128)(2,1)} %get-tuple-element.167), channel_id=1, source_target_pairs={{0,24},{8,16},{16,8},{24,0},{1,25},{9,17},{17,9},{25,1},{2,26},{10... | collective-permute-start | bytes 3145736 | tf_op jit(solution)/shard_map/ppermute | solution.py:205
  292.9 46.6 %collective-permute-start.25 = (bf16[1024,512]{1,0:T(8,128)(2,1)}, bf16[1024,512]{1,0:T(8,128)(2,1)}, u32[]{:S(2)}, u32[]{:S(2)}) collective-permute-start(bf16[1024,512]{1,0:T(8,128)(2,1)} %get-tuple-element.168), channel_id=1, source_target_pairs={{0,16},{8,24},{16,0},{24,8},{1,17},{9,25},{17,1},{25,9},{2,18},{10... | collective-permute-start | bytes 3145736 | tf_op jit(solution)/shard_map/ppermute | solution.py:205
  293.4 46.1 %collective-permute-start.24 = (bf16[1024,512]{1,0:T(8,128)(2,1)}, bf16[1024,512]{1,0:T(8,128)(2,1)}, u32[]{:S(2)}, u32[]{:S(2)}) collective-permute-start(bf16[1024,512]{1,0:T(8,128)(2,1)} %get-tuple-element.169), channel_id=1, source_target_pairs={{0,8},{8,0},{16,24},{24,16},{1,9},{9,1},{17,25},{25,17},{2,10},{10... | collective-permute-start | bytes 3145736 | tf_op jit(solution)/shard_map/ppermute | solution.py:205
  339.6 103.6 %all-gather.10.cloned.1.call-start = ((), (), s32[]{:S(2)}) async-start(), calls=%async_computation.13 | async-start | bytes 4718592 | tf_op jit(solution)/shard_map/all_gather | solution.py:313
  342.9 46.3 %collective-permute-start.28 = (bf16[8,64,1024]{2,1,0:T(8,128)(2,1)}, bf16[8,64,1024]{2,1,0:T(8,128)(2,1)}, u32[]{:S(2)}, u32[]{:S(2)}) collective-permute-start(bf16[8,64,1024]{2,1,0:T(8,128)(2,1)} %get-tuple-element.165), channel_id=1, source_target_pairs={{0,8},{8,0},{16,24},{24,16},{1,9},{9,1},{17,25},{25,17},{2,10},{10... | collective-permute-start | bytes 3145736 | tf_op jit(solution)/shard_map/ppermute | solution.py:205
  344.4 46.3 %collective-permute-start.27 = (bf16[8,64,1024]{2,1,0:T(8,128)(2,1)}, bf16[8,64,1024]{2,1,0:T(8,128)(2,1)}, u32[]{:S(2)}, u32[]{:S(2)}) collective-permute-start(bf16[8,64,1024]{2,1,0:T(8,128)(2,1)} %get-tuple-element.166), channel_id=1, source_target_pairs={{0,8},{8,0},{16,24},{24,16},{1,9},{9,1},{17,25},{25,17},{2,10},{10... | collective-permute-start | bytes 3145736 | tf_op jit(solution)/shard_map/ppermute | solution.py:205
  346.4 44.3 %collective-permute-start.30 = (bf16[8,64,1024]{2,1,0:T(8,128)(2,1)}, bf16[8,64,1024]{2,1,0:T(8,128)(2,1)}, u32[]{:S(2)}, u32[]{:S(2)}) collective-permute-start(bf16[8,64,1024]{2,1,0:T(8,128)(2,1)} %get-tuple-element.163), channel_id=1, source_target_pairs={{0,16},{8,24},{16,0},{24,8},{1,17},{9,25},{17,1},{25,9},{2,18},{10... | collective-permute-start | bytes 3145736 | tf_op jit(solution)/shard_map/ppermute | solution.py:205
  347.9 45.8 %collective-permute-start.29 = (bf16[8,64,1024]{2,1,0:T(8,128)(2,1)}, bf16[8,64,1024]{2,1,0:T(8,128)(2,1)}, u32[]{:S(2)}, u32[]{:S(2)}) collective-permute-start(bf16[8,64,1024]{2,1,0:T(8,128)(2,1)} %get-tuple-element.164), channel_id=1, source_target_pairs={{0,16},{8,24},{16,0},{24,8},{1,17},{9,25},{17,1},{25,9},{2,18},{10... | collective-permute-start | bytes 3145736 | tf_op jit(solution)/shard_map/ppermute | solution.py:205
  401.2 23.9 %collective-permute-start.32 = (bf16[8,64,1024]{2,1,0:T(8,128)(2,1)}, bf16[8,64,1024]{2,1,0:T(8,128)(2,1)}, u32[]{:S(2)}, u32[]{:S(2)}) collective-permute-start(bf16[8,64,1024]{2,1,0:T(8,128)(2,1)} %fusion.5), channel_id=1, source_target_pairs={{0,8},{8,0},{16,24},{24,16},{1,9},{9,1},{17,25},{25,17},{2,10},{10... | collective-permute-start | bytes 3145736 | tf_op jit(solution)/shard_map/ppermute | solution.py:205
  405.8 23.5 %collective-permute-start.31 = (bf16[8,64,1024]{2,1,0:T(8,128)(2,1)}, bf16[8,64,1024]{2,1,0:T(8,128)(2,1)}, u32[]{:S(2)}, u32[]{:S(2)}) collective-permute-start(bf16[8,64,1024]{2,1,0:T(8,128)(2,1)} %fusion.8), channel_id=1, source_target_pairs={{0,16},{8,24},{16,0},{24,8},{1,17},{9,25},{17,1},{25,9},{2,18},{10... | collective-permute-start | bytes 3145736 | tf_op jit(solution)/shard_map/ppermute | solution.py:205
  443.2 66.5 %all-to-all-start.2 = ((bf16[8,2,64,1024]{3,2,1,0:T(8,128)(2,1)}), bf16[8,2,64,1024]{3,2,1,0:T(8,128)(2,1)}, u32[]{:S(2)}, u32[]{:S(2)}) async-start(bf16[8,2,64,1024]{3,2,1,0:T(8,128)(2,1)} %pad_maximum_fusion), calls=%async_computation.5 | async-start | bytes 4194304 | tf_op jit(solution)/shard_map/all_to_all | solution.py:309
  447.5 119.5 %reduce-scatter.11.cloned.1.call-start = ((), (), s32[]{:S(2)}) async-start(), calls=%async_computation.14 | async-start | bytes 4718592 | tf_op jit(solution)/shard_map/reduce_scatter | solution.py:317
  464.9 16.6 %collective-permute-start.36 = (bf16[256,512]{1,0:T(8,128)(2,1)S(1)}, bf16[256,512]{1,0:T(8,128)(2,1)S(1)}, u32[]{:S(2)}, u32[]{:S(2)}) collective-permute-start(bf16[256,512]{1,0:T(8,128)(2,1)S(1)} %get-tuple-element.184), channel_id=1, source_target_pairs={{0,8},{8,0},{16,24},{24,16},{1,9},{9,1},{17,25},{25,17},{2,10},{10... | collective-permute-start | bytes 786440 | tf_op jit(solution)/shard_map/ppermute | solution.py:205
  475.5 11.5 %collective-permute-start.38 = (bf16[256,512]{1,0:T(8,128)(2,1)}, bf16[256,512]{1,0:T(8,128)(2,1)}, u32[]{:S(2)}, u32[]{:S(2)}) collective-permute-start(bf16[256,512]{1,0:T(8,128)(2,1)} %get-tuple-element.185), channel_id=1, source_target_pairs={{0,24},{8,16},{16,8},{24,0},{1,25},{9,17},{17,9},{25,1},{2,26},{10... | collective-permute-start | bytes 786440 | tf_op jit(solution)/shard_map/ppermute | solution.py:205
  477.0 13.7 %collective-permute-start.37 = (bf16[256,512]{1,0:T(8,128)(2,1)}, bf16[256,512]{1,0:T(8,128)(2,1)}, u32[]{:S(2)}, u32[]{:S(2)}) collective-permute-start(bf16[256,512]{1,0:T(8,128)(2,1)} %get-tuple-element.186), channel_id=1, source_target_pairs={{0,16},{8,24},{16,0},{24,8},{1,17},{9,25},{17,1},{25,9},{2,18},{10... | collective-permute-start | bytes 786440 | tf_op jit(solution)/shard_map/ppermute | solution.py:205
  478.6 15.8 %collective-permute-start.33 = (bf16[8,64,384]{2,1,0:T(8,128)(2,1)}, bf16[8,64,384]{2,1,0:T(8,128)(2,1)}, u32[]{:S(2)}, u32[]{:S(2)}) collective-permute-start(bf16[8,64,384]{2,1,0:T(8,128)(2,1)} %get-tuple-element.180), channel_id=1, source_target_pairs={{0,8},{8,0},{16,24},{24,16},{1,9},{9,1},{17,25},{25,17},{2,10},{10... | collective-permute-start | bytes 1179656 | tf_op jit(solution)/shard_map/ppermute | solution.py:205
  480.0 22.0 %collective-permute-start.35 = (bf16[8,64,384]{2,1,0:T(8,128)(2,1)}, bf16[8,64,384]{2,1,0:T(8,128)(2,1)}, u32[]{:S(2)}, u32[]{:S(2)}) collective-permute-start(bf16[8,64,384]{2,1,0:T(8,128)(2,1)} %get-tuple-element.181), channel_id=1, source_target_pairs={{0,24},{8,16},{16,8},{24,0},{1,25},{9,17},{17,9},{25,1},{2,26},{10... | collective-permute-start | bytes 1179656 | tf_op jit(solution)/shard_map/ppermute | solution.py:205
  481.5 26.0 %collective-permute-start.34 = (bf16[8,64,384]{2,1,0:T(8,128)(2,1)S(1)}, bf16[8,64,384]{2,1,0:T(8,128)(2,1)}, u32[]{:S(2)}, u32[]{:S(2)}) collective-permute-start(bf16[8,64,384]{2,1,0:T(8,128)(2,1)S(1)} %get-tuple-element.182), channel_id=1, source_target_pairs={{0,16},{8,24},{16,0},{24,8},{1,17},{9,25},{17,1},{25,9},{2,18},{10... | collective-permute-start | bytes 1179656 | tf_op jit(solution)/shard_map/ppermute | solution.py:205
  513.0 15.1 %collective-permute-start.39 = (bf16[4,64,1024]{2,1,0:T(8,128)(2,1)}, bf16[4,64,1024]{2,1,0:T(8,128)(2,1)}, u32[]{:S(2)}, u32[]{:S(2)}) collective-permute-start(bf16[4,64,1024]{2,1,0:T(8,128)(2,1)} %get-tuple-element.172), channel_id=1, source_target_pairs={{0,8},{8,0},{16,24},{24,16},{1,9},{9,1},{17,25},{25,17},{2,10},{10... | collective-permute-start | bytes 1572872 | tf_op jit(solution)/shard_map/ppermute | solution.py:205
  513.5 25.1 %collective-permute-start.40 = (bf16[4,64,1024]{2,1,0:T(8,128)(2,1)}, bf16[4,64,1024]{2,1,0:T(8,128)(2,1)}, u32[]{:S(2)}, u32[]{:S(2)}) collective-permute-start(bf16[4,64,1024]{2,1,0:T(8,128)(2,1)} %get-tuple-element.171), channel_id=1, source_target_pairs={{0,16},{8,24},{16,0},{24,8},{1,17},{9,25},{17,1},{25,9},{2,18},{10... | collective-permute-start | bytes 1572872 | tf_op jit(solution)/shard_map/ppermute | solution.py:205
  515.0 26.0 %all-to-all-start.3 = ((bf16[8,72,384]{2,1,0:T(8,128)(2,1)}), bf16[8,72,384]{2,1,0:T(8,128)(2,1)S(1)}, u32[]{:S(2)}, u32[]{:S(2)}) async-start(bf16[8,72,384]{2,1,0:T(8,128)(2,1)} %fusion.32), calls=%async_computation.7 | async-start | bytes 884736 | tf_op jit(solution)/shard_map/all_to_all | solution.py:309
  520.0 19.7 %collective-permute-start.41 = (bf16[4,64,1024]{2,1,0:T(8,128)(2,1)}, bf16[4,64,1024]{2,1,0:T(8,128)(2,1)S(1)}, u32[]{:S(2)}, u32[]{:S(2)}) collective-permute-start(bf16[4,64,1024]{2,1,0:T(8,128)(2,1)} %get-tuple-element.170), channel_id=1, source_target_pairs={{0,24},{8,16},{16,8},{24,0},{1,25},{9,17},{17,9},{25,1},{2,26},{10... | collective-permute-start | bytes 1572872 | tf_op jit(solution)/shard_map/ppermute | solution.py:205
  541.0 6.8 %collective-permute-start.45 = (f32[2,256]{1,0:T(2,128)S(1)}, f32[2,256]{1,0:T(2,128)}, u32[]{:S(2)}, u32[]{:S(2)}) collective-permute-start(f32[2,256]{1,0:T(2,128)S(1)} %convert_reduce_fusion), channel_id=1, source_target_pairs={{0,8},{8,0},{16,24},{24,16},{1,9},{9,1},{17,25},{25,17},{2,10},{10... | collective-permute-start | bytes 6152 | tf_op jit(solution)/shard_map/ppermute | solution.py:205
  543.8 15.1 %collective-permute-start.42 = (bf16[64,768]{1,0:T(8,128)(2,1)S(1)}, bf16[64,768]{1,0:T(8,128)(2,1)S(1)}, u32[]{:S(2)}, u32[]{:S(2)}) collective-permute-start(bf16[64,768]{1,0:T(8,128)(2,1)S(1)} %bitcast.215), channel_id=1, source_target_pairs={{0,8},{8,0},{16,24},{24,16},{1,9},{9,1},{17,25},{25,17},{2,10},{10... | collective-permute-start | bytes 294920 | tf_op jit(solution)/shard_map/ppermute | solution.py:205
  545.1 13.8 %collective-permute-start.43 = (bf16[64,768]{1,0:T(8,128)(2,1)S(1)}, bf16[64,768]{1,0:T(8,128)(2,1)S(1)}, u32[]{:S(2)}, u32[]{:S(2)}) collective-permute-start(bf16[64,768]{1,0:T(8,128)(2,1)S(1)} %bitcast.214), channel_id=1, source_target_pairs={{0,16},{8,24},{16,0},{24,8},{1,17},{9,25},{17,1},{25,9},{2,18},{10... | collective-permute-start | bytes 294920 | tf_op jit(solution)/shard_map/ppermute | solution.py:205
  545.6 13.3 %collective-permute-start.44 = (bf16[64,768]{1,0:T(8,128)(2,1)S(1)}, bf16[64,768]{1,0:T(8,128)(2,1)S(1)}, u32[]{:S(2)}, u32[]{:S(2)}) collective-permute-start(bf16[64,768]{1,0:T(8,128)(2,1)S(1)} %bitcast.213), channel_id=1, source_target_pairs={{0,24},{8,16},{16,8},{24,0},{1,25},{9,17},{17,9},{25,1},{2,26},{10... | collective-permute-start | bytes 294920 | tf_op jit(solution)/shard_map/ppermute | solution.py:205
  548.5 9.8 %collective-permute-start.46 = (f32[2,256]{1,0:T(2,128)S(1)}, f32[2,256]{1,0:T(2,128)S(1)}, u32[]{:S(2)}, u32[]{:S(2)}) collective-permute-start(f32[2,256]{1,0:T(2,128)S(1)} %add.240), channel_id=1, source_target_pairs={{0,16},{8,24},{16,0},{24,8},{1,17},{9,25},{17,1},{25,9},{2,18},{10... | collective-permute-start | bytes 6152 | tf_op jit(solution)/shard_map/ppermute | solution.py:205
  (23 other events, 154.4 us)
Sparse Core Ops, SparseCore 0:
  9.6 59.0 all-gather.11
  131.4 49.8 reduce-scatter.4
  185.4 45.7 all-gather.5
  233.3 45.6 all-gather.7
  281.1 48.7 reduce-scatter.6
  339.7 48.1 reduce-scatter.8
  398.4 44.7 all-gather.9
  509.9 57.1 reduce-scatter.10
